TPU v7x, 128 devices: a whole 4x4x4 slice. The times are simulated.
128 devices in a mesh: dom: 16 (over y_hi, z, core), blk: 8 (over x, y_lo).
Axes of the slice: x: 4, y: 4 (y_hi: 2, y_lo: 2; y = y_hi * 2 + y_lo), z: 4, core: 2. Of those that a mesh axis runs over, the one named last changes fastest.
Arguments:
- images: bfloat16 [1024, 128, 256], P('dom', 'blk'), may hold values from -4.5 to 6.5
- ref_store: bfloat16 [16, 16, 4, 128, 256], P('dom', None, None, 'blk'), may hold values from -0.03125 to 0.03125
- block_owner: int32 [16], replicated, may hold values from 0 to 15, as said below
- class_gain: float32 [64], replicated, may hold values from 0.5 to 2
- precision: float32 [1024], P('dom'), may hold values from 0.5 to 80
Outputs:
- class_sums: float32 [16, 1, 4, 128, 256], P('dom', None, None, 'blk')
Inputs may be any that keep to these rules, and one draw needn't show every extreme that they name: `block_owner`: each index d of dom owns exactly 1 block.
All inputs are finite; a program needn't handle non-finite values.
Results may differ from a plain program's by a relative error of at most 0.0049.
Values may be sent and summed in bfloat16 or wider, within the bound.
No kernel may reach another device: no remote copies, remote signals or barrier semaphores. Data moves between devices by JAX's collectives and lax.ppermute only.
A program may use at most 64 MiB of HBM per device.

v0:
```python
import jax
import jax.numpy as jnp
from jax import lax
from jax.sharding import PartitionSpec as P

S = 64
SG = 4


def from_root(array, axis, root):
    mine = lax.axis_index(axis) == root
    return lax.psum(jnp.where(mine, array, jnp.zeros_like(array)), axis)


def shards(images, ref_store, block_owner, class_gain, precision):
    particles = images.shape[0]
    cycle_count = images.shape[1]
    angles = images.shape[2]
    block_count = block_owner.shape[0]
    per_block = ref_store.shape[2]
    classes = block_count * per_block
    rot_step = angles // S
    stored_here = ref_store[0]

    def fetch_block(counter, running):
        block_piece = lax.dynamic_index_in_dim(stored_here, counter, 0, keepdims=False)
        root_index = lax.dynamic_index_in_dim(block_owner, counter, 0, keepdims=False)
        received = from_root(block_piece, "dom", root_index)
        return lax.dynamic_update_index_in_dim(running, received, counter, 0)

    stored = lax.fori_loop(0, block_count, fetch_block, jnp.zeros_like(stored_here))
    references = (
        stored.astype(jnp.float32) * class_gain.reshape(block_count, per_block, 1, 1)
    ).astype(jnp.bfloat16)
    ref_cube = references.reshape(classes, cycle_count, angles)
    ref_float = ref_cube.astype(jnp.float32)
    norm_part = jnp.sum(ref_float * ref_float, axis=(1, 2))
    flat_images = images.reshape(particles, cycle_count * angles)
    image_float = flat_images.astype(jnp.float32)
    doubled = jnp.concatenate([ref_cube, ref_cube], axis=2)
    groups = S // SG
    group_span = rot_step * SG

    def correlate(group_index, buffer):
        window = lax.dynamic_slice_in_dim(doubled, group_index * group_span, angles + group_span, 2)
        rolled = jnp.stack(
            [
                window[:, :, shift_index * rot_step : shift_index * rot_step + angles]
                for shift_index in range(SG)
            ],
            0,
        )
        rolled = rolled.reshape(SG * classes, cycle_count * angles)
        products = lax.dot_general(
            flat_images, rolled, (((1,), (1,)), ((), ())), preferred_element_type=jnp.float32
        )
        return lax.dynamic_update_index_in_dim(buffer, products, group_index, 0)

    scores = lax.fori_loop(
        0, groups, correlate, jnp.zeros((groups, particles, SG * classes), jnp.float32)
    )
    row_scale = precision[None, :, None]
    total_scores, total_norms = lax.psum((scores, norm_part), "blk")
    logits = row_scale * (total_scores - 0.5 * jnp.tile(total_norms, SG)[None, None, :])
    row_max = jnp.max(logits, axis=(0, 2), keepdims=True)
    exponent = jnp.exp(logits - row_max)
    weights = exponent / jnp.sum(exponent, axis=(0, 2), keepdims=True)

    def accumulate(counter, running):
        group_index = groups - 1 - counter
        group_weights = lax.dynamic_index_in_dim(weights, group_index, 0, keepdims=False)
        spread = lax.dot_general(
            group_weights,
            image_float,
            (((0,), (0,)), ((), ())),
            precision=lax.Precision.HIGHEST,
            preferred_element_type=jnp.float32,
        )
        spread = spread.reshape(SG, classes, cycle_count, angles)
        for shift_index in reversed(range(SG)):
            running = jnp.roll(running, rot_step, axis=2) + spread[shift_index]
        return running

    totals = lax.fori_loop(
        0, groups, accumulate, jnp.zeros((classes, cycle_count, angles), jnp.float32)
    )
    final_order = jnp.argsort(block_owner, stable=True)
    blocked = jnp.take(
        totals.reshape(block_count, per_block, cycle_count, angles), final_order, axis=0
    )
    owned_totals = lax.psum_scatter(blocked, "dom", scatter_dimension=0, tiled=True)
    return owned_totals[None]


def solution(mesh):
    return jax.shard_map(
        shards,
        mesh=mesh,
        in_specs=(P("dom", "blk", None), P("dom", None, None, "blk", None), P(), P(), P("dom")),
        out_specs=P("dom", None, None, "blk", None),
        check_vma=False,
    )
```

profile of v0, /device:TPU:0, one launch (start us, length us, event | category | flops | bytes accessed | tf_op | source)
XLA Modules:
  0.0 1514.2 jit_solution(2883615301706776567)
XLA Ops:
  6.5 1089.9 %while.42 = (s32[]{:T(128)}, bf16[16,4,16,256]{3,2,1,0:T(8,128)(2,1)S(1)}, s32[16]{0:T(128)}, bf16[16,4,16,256]{3,2,1,0:T(8,128)(2,1)}, s32[]{:T(128)}, /*index=5*/u32[]{:T(128)}, u32[]{:T(128)}) while((s32[]{:T(128)}, bf16[16,4,16,256]{3,2,1,0:T(8,128)(2,1)S(1)}, s32[16]{0:T(128)}, bf16[16,4,16,256]{3,2,1,0:T(8,128)(2,1)}, s32[]{:T(128)}, ...), condition=%wide.region_3.4_spmd, body=%wide.region_1.3_spmd.sunk | while | flops 32774 | bytes 196747 | solution.py:31
  6.5 1.4 dynamic_slice.44
  9.4 71.0 %psum.28 = bf16[1,4,16,256]{3,2,1,0:T(8,128)(2,1)S(1)} all-reduce(bf16[1,4,16,256]{3,2,1,0:T(8,128)(2,1)S(1)} %dynamic-slice_select_fusion.2), channel_id=1, replica_groups=mesh['dom'=16,'blk'=8] {'dom'}, use_global_device_ids=true, to_apply=%region_2.2 | all-reduce | flops 16384 | bytes 65536 | tf_op jit(solution)/shard_map/while/body/eval_jaxpr/psum | solution.py:12
  83.2 64.9 %psum.28 = bf16[1,4,16,256]{3,2,1,0:T(8,128)(2,1)S(1)} all-reduce(bf16[1,4,16,256]{3,2,1,0:T(8,128)(2,1)S(1)} %dynamic-slice_select_fusion.2), channel_id=1, replica_groups=mesh['dom'=16,'blk'=8] {'dom'}, use_global_device_ids=true, to_apply=%region_2.2 | all-reduce | flops 16384 | bytes 65536 | tf_op jit(solution)/shard_map/while/body/eval_jaxpr/psum | solution.py:12
  150.9 64.9 %psum.28 = bf16[1,4,16,256]{3,2,1,0:T(8,128)(2,1)S(1)} all-reduce(bf16[1,4,16,256]{3,2,1,0:T(8,128)(2,1)S(1)} %dynamic-slice_select_fusion.2), channel_id=1, replica_groups=mesh['dom'=16,'blk'=8] {'dom'}, use_global_device_ids=true, to_apply=%region_2.2 | all-reduce | flops 16384 | bytes 65536 | tf_op jit(solution)/shard_map/while/body/eval_jaxpr/psum | solution.py:12
  218.7 64.9 %psum.28 = bf16[1,4,16,256]{3,2,1,0:T(8,128)(2,1)S(1)} all-reduce(bf16[1,4,16,256]{3,2,1,0:T(8,128)(2,1)S(1)} %dynamic-slice_select_fusion.2), channel_id=1, replica_groups=mesh['dom'=16,'blk'=8] {'dom'}, use_global_device_ids=true, to_apply=%region_2.2 | all-reduce | flops 16384 | bytes 65536 | tf_op jit(solution)/shard_map/while/body/eval_jaxpr/psum | solution.py:12
  286.4 64.9 %psum.28 = bf16[1,4,16,256]{3,2,1,0:T(8,128)(2,1)S(1)} all-reduce(bf16[1,4,16,256]{3,2,1,0:T(8,128)(2,1)S(1)} %dynamic-slice_select_fusion.2), channel_id=1, replica_groups=mesh['dom'=16,'blk'=8] {'dom'}, use_global_device_ids=true, to_apply=%region_2.2 | all-reduce | flops 16384 | bytes 65536 | tf_op jit(solution)/shard_map/while/body/eval_jaxpr/psum | solution.py:12
  354.1 64.9 %psum.28 = bf16[1,4,16,256]{3,2,1,0:T(8,128)(2,1)S(1)} all-reduce(bf16[1,4,16,256]{3,2,1,0:T(8,128)(2,1)S(1)} %dynamic-slice_select_fusion.2), channel_id=1, replica_groups=mesh['dom'=16,'blk'=8] {'dom'}, use_global_device_ids=true, to_apply=%region_2.2 | all-reduce | flops 16384 | bytes 65536 | tf_op jit(solution)/shard_map/while/body/eval_jaxpr/psum | solution.py:12
  421.9 64.9 %psum.28 = bf16[1,4,16,256]{3,2,1,0:T(8,128)(2,1)S(1)} all-reduce(bf16[1,4,16,256]{3,2,1,0:T(8,128)(2,1)S(1)} %dynamic-slice_select_fusion.2), channel_id=1, replica_groups=mesh['dom'=16,'blk'=8] {'dom'}, use_global_device_ids=true, to_apply=%region_2.2 | all-reduce | flops 16384 | bytes 65536 | tf_op jit(solution)/shard_map/while/body/eval_jaxpr/psum | solution.py:12
  489.6 64.9 %psum.28 = bf16[1,4,16,256]{3,2,1,0:T(8,128)(2,1)S(1)} all-reduce(bf16[1,4,16,256]{3,2,1,0:T(8,128)(2,1)S(1)} %dynamic-slice_select_fusion.2), channel_id=1, replica_groups=mesh['dom'=16,'blk'=8] {'dom'}, use_global_device_ids=true, to_apply=%region_2.2 | all-reduce | flops 16384 | bytes 65536 | tf_op jit(solution)/shard_map/while/body/eval_jaxpr/psum | solution.py:12
  557.4 64.9 %psum.28 = bf16[1,4,16,256]{3,2,1,0:T(8,128)(2,1)S(1)} all-reduce(bf16[1,4,16,256]{3,2,1,0:T(8,128)(2,1)S(1)} %dynamic-slice_select_fusion.2), channel_id=1, replica_groups=mesh['dom'=16,'blk'=8] {'dom'}, use_global_device_ids=true, to_apply=%region_2.2 | all-reduce | flops 16384 | bytes 65536 | tf_op jit(solution)/shard_map/while/body/eval_jaxpr/psum | solution.py:12
  625.1 64.9 %psum.28 = bf16[1,4,16,256]{3,2,1,0:T(8,128)(2,1)S(1)} all-reduce(bf16[1,4,16,256]{3,2,1,0:T(8,128)(2,1)S(1)} %dynamic-slice_select_fusion.2), channel_id=1, replica_groups=mesh['dom'=16,'blk'=8] {'dom'}, use_global_device_ids=true, to_apply=%region_2.2 | all-reduce | flops 16384 | bytes 65536 | tf_op jit(solution)/shard_map/while/body/eval_jaxpr/psum | solution.py:12
  692.8 64.9 %psum.28 = bf16[1,4,16,256]{3,2,1,0:T(8,128)(2,1)S(1)} all-reduce(bf16[1,4,16,256]{3,2,1,0:T(8,128)(2,1)S(1)} %dynamic-slice_select_fusion.2), channel_id=1, replica_groups=mesh['dom'=16,'blk'=8] {'dom'}, use_global_device_ids=true, to_apply=%region_2.2 | all-reduce | flops 16384 | bytes 65536 | tf_op jit(solution)/shard_map/while/body/eval_jaxpr/psum | solution.py:12
  760.6 64.9 %psum.28 = bf16[1,4,16,256]{3,2,1,0:T(8,128)(2,1)S(1)} all-reduce(bf16[1,4,16,256]{3,2,1,0:T(8,128)(2,1)S(1)} %dynamic-slice_select_fusion.2), channel_id=1, replica_groups=mesh['dom'=16,'blk'=8] {'dom'}, use_global_device_ids=true, to_apply=%region_2.2 | all-reduce | flops 16384 | bytes 65536 | tf_op jit(solution)/shard_map/while/body/eval_jaxpr/psum | solution.py:12
  828.3 64.9 %psum.28 = bf16[1,4,16,256]{3,2,1,0:T(8,128)(2,1)S(1)} all-reduce(bf16[1,4,16,256]{3,2,1,0:T(8,128)(2,1)S(1)} %dynamic-slice_select_fusion.2), channel_id=1, replica_groups=mesh['dom'=16,'blk'=8] {'dom'}, use_global_device_ids=true, to_apply=%region_2.2 | all-reduce | flops 16384 | bytes 65536 | tf_op jit(solution)/shard_map/while/body/eval_jaxpr/psum | solution.py:12
  896.1 64.9 %psum.28 = bf16[1,4,16,256]{3,2,1,0:T(8,128)(2,1)S(1)} all-reduce(bf16[1,4,16,256]{3,2,1,0:T(8,128)(2,1)S(1)} %dynamic-slice_select_fusion.2), channel_id=1, replica_groups=mesh['dom'=16,'blk'=8] {'dom'}, use_global_device_ids=true, to_apply=%region_2.2 | all-reduce | flops 16384 | bytes 65536 | tf_op jit(solution)/shard_map/while/body/eval_jaxpr/psum | solution.py:12
  963.8 64.9 %psum.28 = bf16[1,4,16,256]{3,2,1,0:T(8,128)(2,1)S(1)} all-reduce(bf16[1,4,16,256]{3,2,1,0:T(8,128)(2,1)S(1)} %dynamic-slice_select_fusion.2), channel_id=1, replica_groups=mesh['dom'=16,'blk'=8] {'dom'}, use_global_device_ids=true, to_apply=%region_2.2 | all-reduce | flops 16384 | bytes 65536 | tf_op jit(solution)/shard_map/while/body/eval_jaxpr/psum | solution.py:12
  1031.5 64.9 %psum.28 = bf16[1,4,16,256]{3,2,1,0:T(8,128)(2,1)S(1)} all-reduce(bf16[1,4,16,256]{3,2,1,0:T(8,128)(2,1)S(1)} %dynamic-slice_select_fusion.2), channel_id=1, replica_groups=mesh['dom'=16,'blk'=8] {'dom'}, use_global_device_ids=true, to_apply=%region_2.2 | all-reduce | flops 16384 | bytes 65536 | tf_op jit(solution)/shard_map/while/body/eval_jaxpr/psum | solution.py:12
  1097.9 47.7 %while.43 = (s32[]{:T(128)}, f32[16,64,256]{2,1,0:T(8,128)S(1)}, bf16[64,16,512]{2,1,0:T(8,128)(2,1)S(1)}, bf16[64,4096]{1,0:T(8,128)(2,1)S(1)}, s32[]{:T(128)},...) while((s32[]{:T(128)}, f32[16,64,256]{2,1,0:T(8,128)S(1)}, ...), condition=%wide.region_5.6_spmd, body=%wide.region_4.5_spmd.sunk | while | flops 137363456 | bytes 15270099 | solution.py:59
  1146.9 19.0 %psum.26 = f32[64]{0:T(128)S(1)} all-reduce(f32[64]{0:T(128)S(1)} %reduce_sum.21), channel_id=1, replica_groups=mesh['dom'=16,'blk'=8] {'blk'}, use_global_device_ids=true, to_apply=%region_8.9 | all-reduce | flops 64 | bytes 512 | tf_op jit(solution)/shard_map/psum | solution.py:63
  1167.2 54.9 %all-reduce.2.cloned.1.call-done = f32[16,64,256]{2,1,0:T(8,128)} async-done(((f32[16,64,256]{2,1,0:T(8,128)}), f32[16,64,256]{2,1,0:T(8,128)}) %all-reduce.2.cloned.1.call-update) | async-done | bytes 1048592 | tf_op jit(solution)/shard_map/psum | solution.py:63
  1222.1 1.6 fusion.5
  1223.7 1.6 fusion.7
  1225.6 211.8 %while.44 = (s32[]{:T(128)}, f32[64,16,256]{2,1,0:T(8,128)}, f32[16,64,256]{2,1,0:T(8,128)S(1)}, f32[64,4096]{1,0:T(8,128)S(1)}, s32[]{:T(128)}, /*index=5*/s32[]{:T(128)}, s32[]{:T(128)}, s32[]{:T(128)}) while((s32[]{:T(128)}, f32[64,16,256]{2,1,0:T(8,128)}, f32[16,64,256]{2,1,0:T(8,128)S(1)}, f32[64,4096]{1,0:T(8,128)S(1)}, ...), condition=%wide.region_12.13_spmd.clone, body=%wide.region_11.12_spmd.clone.sunk | while | flops 807665664 | bytes 57868572 | solution.py:84
  1227.0 3.5 fusion.24
  1230.5 1.4 fusion.25
  1235.8 1.3 bitcast_add_fusion.11
  1239.1 3.5 fusion.24
  1242.6 1.4 fusion.25
  1252.4 3.5 fusion.24
  1255.9 1.4 fusion.25
  1262.5 1.3 bitcast_add_fusion.11
  1265.7 3.5 fusion.24
  1269.2 1.4 fusion.25
  1275.8 1.3 bitcast_add_fusion.11
  1279.0 3.5 fusion.24
  1282.5 1.4 fusion.25
  1292.4 3.5 fusion.24
  1295.8 1.4 fusion.25
  1305.7 3.5 fusion.24
  1309.2 1.4 fusion.25
  1315.7 1.3 bitcast_add_fusion.11
  1319.0 3.5 fusion.24
  1322.5 1.4 fusion.25
  1329.0 1.3 bitcast_add_fusion.11
  1332.3 3.5 fusion.24
  1335.8 1.4 fusion.25
  1342.3 1.3 bitcast_add_fusion.11
  1345.6 3.5 fusion.24
  1349.1 1.4 fusion.25
  1358.9 3.5 fusion.24
  1362.4 1.4 fusion.25
  1372.2 3.5 fusion.24
  1375.7 1.4 fusion.25
  1385.6 3.5 fusion.24
  1389.0 1.4 fusion.25
  1398.9 3.5 fusion.24
  1402.4 1.4 fusion.25
  1412.2 3.5 fusion.24
  1415.7 1.4 fusion.25
  1425.5 3.5 fusion.24
  1429.0 1.4 fusion.25
  1437.4 1.8 gather_fusion
  1440.4 67.0 %reduce-scatter.2.cloned.1.call-done = f32[1,4,16,256]{3,2,1,0:T(8,128)} async-done(((f32[16,4,16,256]{3,2,1,0:T(8,128)}), f32[1,4,16,256]{3,2,1,0:T(8,128)}) %reduce-scatter.2.cloned.1.call-update) | async-done | bytes 65552 | tf_op jit(solution)/shard_map/reduce_scatter | solution.py:91
  (506 shorter events, 209.2 us)
Async XLA Ops:
  6.5 1091.2 %copy-start.7 = (bf16[64,16,256]{2,1,0:T(8,128)(2,1)S(1)}, bf16[64,16,256]{2,1,0:T(8,128)(2,1)}, u32[]{:S(2)}) copy-start(bf16[64,16,256]{2,1,0:T(8,128)(2,1)} %param.11) | copy-start | bytes 1572868
  6.5 1215.6 %all-reduce.2.cloned.1.call-start = ((), (), s32[]{:S(2)}) async-start(), calls=%async_computation.1 | async-start | bytes 2097152 | tf_op jit(solution)/shard_map/psum | solution.py:63
  1145.6 20.4 %copy-start.9 = (s32[16]{0:T(128)S(1)}, s32[16]{0:T(128)}, u32[]{:S(2)}) copy-start(s32[16]{0:T(128)} %get-tuple-element.505) | copy-start | bytes 196
  1145.6 76.5 %copy-start.8 = (f32[64]{0:T(128)S(1)}, f32[64]{0:T(128)}, u32[]{:S(2)}) copy-start(f32[64]{0:T(128)} %param.15) | copy-start | bytes 772
  1146.6 360.7 %reduce-scatter.2.cloned.1.call-start = ((), (), s32[]{:S(2)}) async-start(), calls=%async_computation.2 | async-start | bytes 1114112 | tf_op jit(solution)/shard_map/reduce_scatter | solution.py:91
  1222.1 3.2 copy-start.3
  1225.6 1.4 copy-start.4
  1232.5 1.2 copy-start
  1235.8 1.3 copy-start.2
  1235.8 1.9 copy-start.5
  1237.7 1.4 copy-start.4
  1245.8 1.2 copy-start
  1249.1 1.3 copy-start.2
  1249.1 1.9 copy-start.5
  1251.0 1.4 copy-start.4
  1259.2 1.2 copy-start
  1262.4 1.3 copy-start.2
  1262.4 1.9 copy-start.5
  1264.4 1.4 copy-start.4
  1275.8 1.3 copy-start.2
  1275.8 1.9 copy-start.5
  1277.7 1.4 copy-start.4
  1289.1 1.3 copy-start.2
  1289.1 1.9 copy-start.5
  1291.0 1.4 copy-start.4
  1299.1 1.2 copy-start
  1302.4 1.3 copy-start.2
  1302.4 1.9 copy-start.5
  1304.3 1.4 copy-start.4
  1312.4 1.2 copy-start
  1315.7 1.3 copy-start.2
  1315.7 1.9 copy-start.5
  1317.6 1.4 copy-start.4
  1325.7 1.2 copy-start
  1329.0 1.3 copy-start.2
  1329.0 1.9 copy-start.5
  1330.9 1.4 copy-start.4
  1342.3 1.3 copy-start.2
  1342.3 1.9 copy-start.5
  1344.2 1.4 copy-start.4
  1355.6 1.3 copy-start.2
  1355.6 1.9 copy-start.5
  1357.6 1.4 copy-start.4
  1365.7 1.2 copy-start
  1368.9 1.3 copy-start.2
  1369.0 1.9 copy-start.5
  1370.9 1.4 copy-start.4
  1379.0 1.2 copy-start
  1382.3 1.3 copy-start.2
  1382.3 1.9 copy-start.5
  1384.2 1.4 copy-start.4
  1392.3 1.2 copy-start
  1395.6 1.3 copy-start.2
  1395.6 1.9 copy-start.5
  1397.5 1.4 copy-start.4
  1408.9 1.3 copy-start.2
  1408.9 1.9 copy-start.5
  1410.8 1.4 copy-start.4
  1418.9 1.2 copy-start
  1422.2 1.3 copy-start.2
  1422.2 1.9 copy-start.5
  1424.1 1.4 copy-start.4
  1435.5 1.3 copy-start.2
  1435.5 1.9 copy-start.5
  (23 other events, 25.0 us)
Sparse Core Ops, SparseCore 0:
  1146.8 75.3 all-reduce.1
  1440.6 66.7 reduce-scatter.1
where the time goes:
time: 1520 us; the launch traced here: 1510 us
  blocking collectives  1060 us (70%)
  local copies, waits for them, and re-layouts  153 us (10%)
  waiting for transfers between devices  122 us (8%)
  other arithmetic  80.8 us (5%)
  matrix products  67.9 us (4%)
    psum x16, blocking collectives, from_root(): return lax.psum(jnp.where(mine, array, jnp.zeros_like(array)), axis)  1050 us
    while x240, local copies, waits for them, and re-layouts  76.7 us
    reduce_scatter x1, waiting for transfers between devices, shards(): lax.psum_scatter(blocked, 'dom', scatter_dimension=0, tiled=True)  67 us
    dot_general x16, matrix products, accumulate(): lax.dot_general(group_weights, image_float, (((0,), (0,)), ((), ())), pre...  55.7 us
    psum x1, waiting for transfers between devices, shards(): total_scores, total_norms = lax.psum((scores, norm_part), 'blk')  54.9 us
    add x64, other arithmetic, accumulate(): running = jnp.roll(running, rot_step, axis=2) + spread[shift_index]  38 us
    slice x80, local copies, waits for them, and re-layouts, accumulate(): running = jnp.roll(running, rot_step, axis=2) + spread[shift_index]  35.2 us
  transfers between devices with their start and end apart: 2, of which 2 were waited for; matrix products, arithmetic and copies ran while one was open for 0% of the time, Pallas kernels for 0%

commit v1 on v0

v1 whole, which is shorter than its diff:
```python
import jax
import jax.numpy as jnp
from jax import lax
from jax.experimental import pallas as pl
from jax.experimental.pallas import tpu as pltpu
from jax.sharding import Mesh, PartitionSpec as P

BF = jnp.bfloat16
F32 = jnp.float32
VM = pltpu.VMEM
N1 = 8
N2 = 8


def spec(space=VM):
    return pl.BlockSpec(memory_space=space)


def scratch(rows, angles):
    return VM((angles // 128, rows, 128), F32)


def fill(scr, value):
    for h in range(scr.shape[0]):
        scr[h] = value[:, h * 128 : (h + 1) * 128]


def take_cycle(scr, r, rows, cycles):
    pieces = [scr.at[h][pl.ds(r, rows, stride=cycles), :] for h in range(scr.shape[0])]
    return jnp.concatenate(pieces, axis=1)


def params():
    return pltpu.CompilerParams(vmem_limit_bytes=56 * 1024 * 1024)


def pick_block(me, block_owner, class_gain, ref_store, copies):
    nblk, kb, cycles, angles = ref_store.shape

    def body(me_ref, owner_ref, gain_ref, store_ref, out_ref, buf, sem):
        block = jnp.int32(0)
        for b in range(nblk):
            block = jnp.where(owner_ref[b] == me_ref[0], jnp.int32(b), block)
        copy = pltpu.make_async_copy(store_ref.at[block], buf, sem)
        copy.start()
        copy.wait()
        for i in range(kb):
            piece = (buf[i].astype(F32) * gain_ref[block * kb + i]).astype(BF)
            for c in range(copies):
                out_ref[c, i * cycles : (i + 1) * cycles, :] = piece

    return pl.pallas_call(
        body,
        out_shape=jax.ShapeDtypeStruct((copies, kb * cycles, angles), BF),
        in_specs=[spec(pltpu.SMEM), spec(pltpu.SMEM), spec(pltpu.SMEM), spec(pl.ANY)],
        out_specs=spec(),
        scratch_shapes=[VM((kb, cycles, angles), BF), pltpu.SemaphoreType.DMA],
        compiler_params=params(),
        name="pick_block",
    )(me, block_owner, class_gain, ref_store)


def rotate_images(own, other, nb, step):
    particles, cycles, angles = own.shape
    per = particles // nb

    def body(own_ref, other_ref, out_ref, a_scr, b_scr):
        fill(a_scr, own_ref[...].astype(F32).reshape(particles * cycles, angles))
        fill(b_scr, other_ref[...].astype(F32).reshape(particles * cycles, angles))

        def cycle(r, carry):
            lanes = pl.ds(pl.multiple_of(r * angles, angles), angles)
            a = take_cycle(a_scr, r, particles, cycles).reshape(nb, per, angles)
            b = take_cycle(b_scr, r, particles, cycles).reshape(nb, per, angles)
            both = jnp.concatenate([a, b], axis=1).reshape(nb * 2 * per, angles)
            for s in range(N1):
                turned = pltpu.roll(both, step * s, 1) if s else both
                out_ref[:, s, :, lanes] = turned.astype(BF).reshape(nb, 2 * per, angles)
            return carry

        lax.fori_loop(0, cycles, cycle, 0)

    return pl.pallas_call(
        body,
        out_shape=jax.ShapeDtypeStruct((nb, N1, 2 * per, cycles * angles), BF),
        in_specs=[spec(), spec()],
        out_specs=spec(),
        scratch_shapes=[scratch(particles * cycles, angles)] * 2,
        compiler_params=params(),
        name="rotate_images",
    )(own, other)


def correlate(turned, refs, cycles, step):
    nb, n1, rows, depth = turned.shape
    angles = depth // cycles
    classes = refs.shape[0] * refs.shape[1] // cycles
    cols = N2 * classes

    def body(x_ref, r_ref, out_ref, scr, rr):
        fill(scr, r_ref[...].astype(F32).reshape(classes * cycles, angles))
        square = jnp.zeros((classes, angles), F32)
        for r in range(cycles):
            piece = take_cycle(scr, r, classes, cycles)
            square = square + piece * piece
            for s in range(N2):
                shift = (angles - step * s) % angles
                turned_ref = pltpu.roll(piece, shift, 1) if s else piece
                rr[s * classes : (s + 1) * classes, r * angles : (r + 1) * angles] = (
                    turned_ref.astype(BF)
                )
        half = 0.5 * jnp.sum(square, axis=1, keepdims=True)
        half = jnp.concatenate([half] * N2, axis=0)
        for j in range(0, nb, 2):
            x = x_ref[j : j + 2].reshape(2 * n1 * rows, depth)
            part = lax.dot_general(
                x, rr[...], (((1,), (1,)), ((), ())), preferred_element_type=F32
            )
            for i in range(2):
                piece = part[i * n1 * rows : (i + 1) * n1 * rows]
                out_ref[j + i] = (piece.T - half).astype(BF)

    return pl.pallas_call(
        body,
        out_shape=jax.ShapeDtypeStruct((nb, cols, n1 * rows), BF),
        in_specs=[spec(), spec()],
        out_specs=spec(),
        scratch_shapes=[scratch(classes * cycles, angles), VM((cols, depth), BF)],
        compiler_params=params(),
        name="correlate",
    )(turned, refs)


def local_softmax(me, scores, scale):
    nb, cols, lanes = scores.shape
    group = lanes // N1

    def across(op, row):
        width = group
        while width < lanes:
            row = op(row, pltpu.roll(row, width, 1))
            width *= 2
        return row

    def body(me_ref, x_ref, scale_ref, e_ref, stat_ref):
        total = x_ref[0].astype(F32)
        for i in range(1, nb):
            total = total + x_ref[i].astype(F32)
        logits = total * scale_ref[pl.ds(me_ref[0], 1), :]
        top = across(jnp.maximum, jnp.max(logits, axis=0, keepdims=True))
        e = jnp.exp(logits - top)
        e_ref[...] = e
        stat_ref[0:1, :] = top
        stat_ref[1:2, :] = across(jnp.add, jnp.sum(e, axis=0, keepdims=True))

    return pl.pallas_call(
        body,
        out_shape=(
            jax.ShapeDtypeStruct((cols, lanes), F32),
            jax.ShapeDtypeStruct((2, lanes), F32),
        ),
        in_specs=[spec(pltpu.SMEM), spec(), spec()],
        out_specs=(spec(), spec()),
        compiler_params=params(),
        name="local_softmax",
    )(me, scores, scale)


def normalize(e, mine, theirs, copies, half):
    cols, lanes = e.shape

    def body(e_ref, a_ref, b_ref, out_ref):
        b = pltpu.roll(b_ref[...], half, 1)
        top_a, sum_a = a_ref[0:1, :], a_ref[1:2, :]
        top_b, sum_b = b[0:1, :], b[1:2, :]
        top = jnp.maximum(top_a, top_b)
        part = jnp.exp(top_a - top)
        factor = part / (sum_a * part + sum_b * jnp.exp(top_b - top))
        w = (e_ref[...] * factor).astype(BF)
        for c in range(copies):
            out_ref[c] = w

    return pl.pallas_call(
        body,
        out_shape=jax.ShapeDtypeStruct((copies, cols, lanes), BF),
        in_specs=[spec(), spec(), spec()],
        out_specs=spec(),
        compiler_params=params(),
        name="normalize",
    )(e, mine, theirs)


def accumulate(weights, turned, cycles, owners, step):
    nb, cols, lanes = weights.shape
    depth = turned.shape[-1]
    angles = depth // cycles
    classes = cols // N2

    def body(w_ref, x_ref, out_ref, scr):
        w = jnp.concatenate([w_ref[j] for j in range(nb)], axis=1)

        def cycle(r, carry):
            x = x_ref[:, pl.ds(pl.multiple_of(r * angles, angles), angles)]
            spread = jnp.dot(w, x, preferred_element_type=F32)
            total = spread[0:classes]
            for s in range(1, N2):
                total = total + pltpu.roll(
                    spread[s * classes : (s + 1) * classes], step * s, 1
                )
            for h in range(angles // 128):
                piece = total[:, h * 128 : (h + 1) * 128]
                scr.at[h][pl.ds(r, classes, stride=cycles), :] = piece
            return carry

        lax.fori_loop(0, cycles, cycle, 0)
        whole = jnp.concatenate([scr[h] for h in range(angles // 128)], axis=1)
        out_ref[...] = whole.reshape(out_ref.shape).astype(BF)

    return pl.pallas_call(
        body,
        out_shape=jax.ShapeDtypeStruct((owners, classes // owners * cycles, angles), BF),
        in_specs=[spec(), spec()],
        out_specs=spec(),
        scratch_shapes=[scratch(classes * cycles, angles)],
        compiler_params=params(),
        name="accumulate",
    )(weights, turned.reshape(nb * lanes, depth))


def add_up(parts):
    def body(x_ref, out_ref):
        total = x_ref[0].astype(F32)
        for i in range(1, parts.shape[0]):
            total = total + x_ref[i].astype(F32)
        out_ref[...] = total

    return pl.pallas_call(
        body,
        out_shape=jax.ShapeDtypeStruct(parts.shape[1:], F32),
        in_specs=[spec()],
        out_specs=spec(),
        compiler_params=params(),
        name="add_up",
    )(parts)


def solution(mesh):
    dom, nb = mesh.devices.shape
    nd = dom // 2
    view = Mesh(mesh.devices.reshape(nd, 2, nb), ("dh", "core", "blk"))
    swap = [(0, 1), (1, 0)]

    def shards(images, ref_store, block_owner, class_gain, precision):
        particles, cycles, angles = images.shape
        kb = ref_store.shape[2]
        rot = angles // (N1 * N2)
        half = particles // nb
        other = lax.ppermute(images, "core", swap)
        other_precision = lax.ppermute(precision, "core", swap)
        me = (lax.axis_index("dh") * 2 + lax.axis_index("core"))[None].astype(jnp.int32)
        j = lax.axis_index("blk")[None].astype(jnp.int32)
        mine = pick_block(me, block_owner, class_gain, ref_store[0], nd)
        refs = lax.all_to_all(mine, "dh", 0, 0)
        turned = rotate_images(images, other, nb, rot)
        scores = correlate(turned, refs, cycles, rot * N1)
        scores = lax.all_to_all(scores, "blk", 0, 0)
        both = jnp.concatenate(
            [precision.reshape(nb, half), other_precision.reshape(nb, half)], axis=1
        )
        e, stats = local_softmax(j, scores, jnp.tile(both, (1, N1)))
        theirs = lax.ppermute(stats, "core", swap)
        weights = normalize(e, stats, theirs, nb, half)
        weights = lax.all_to_all(weights, "blk", 0, 0)
        totals = accumulate(weights, turned, cycles, nd, rot * N1)
        totals = lax.all_to_all(totals, "dh", 0, 0)
        return add_up(totals).reshape(1, 1, kb, cycles, angles)

    dom_axes = ("dh", "core")
    return jax.shard_map(
        shards,
        mesh=view,
        in_specs=(
            P(dom_axes, "blk", None),
            P(dom_axes, None, None, "blk", None),
            P(),
            P(),
            P(dom_axes),
        ),
        out_specs=P(dom_axes, None, None, "blk", None),
        check_vma=False,
    )
```

time: 1520 us -> 91.9 us (0.06)
  blocking collectives: 1060 us -> 30.8 us
  local copies, waits for them, and re-layouts: 153 us -> 3.74 us
  waiting for transfers between devices: 122 us -> 10.2 us
  other arithmetic: 80.8 us -> 0.08 us
  matrix products: 67.9 us -> 0 us
  Pallas kernels: 0 us -> 33.7 us
    psum x17 -> x0, blocking collectives: 1060 us -> none  [the longest x16 1050 us: from_root(): return lax.psum(jnp.where(mine, array, jnp.zeros_like(array)), axis)]
    while x240 -> x0, local copies, waits for them, and re-layouts: 76.7 us -> none
    dot_general x32 -> x0, matrix products: 67.9 us -> none  [the longest x16 55.7 us: accumulate(): lax.dot_general(group_weights, image_float, (((0,), (0,)), ((), ())), pre...]
    reduce_scatter x1 -> x0, waiting for transfers between devices: 67 us -> none  [shards(): lax.psum_scatter(blocked, 'dom', scatter_dimension=0, tiled=True)]
    psum x1 -> x0, waiting for transfers between devices: 54.9 us -> none  [shards(): total_scores, total_norms = lax.psum((scores, norm_part), 'blk')]
    add x64 -> x0, other arithmetic: 38 us -> none  [accumulate(): running = jnp.roll(running, rot_step, axis=2) + spread[shift_index]]
    slice x80 -> x0, local copies, waits for them, and re-layouts: 35.2 us -> none  [accumulate(): running = jnp.roll(running, rot_step, axis=2) + spread[shift_index]]
    pallas_call x0 -> x7, Pallas kernels: none -> 33.7 us  [the longest x1 10.7 us: accumulate(): pl.pallas_call(body, out_shape=jax.ShapeDtypeStruct((owners, classes // o...]
  transfers between devices with their start and end apart: 2 -> 5, of which waited for: 2 -> 3; matrix products, arithmetic and copies ran while one was open for 0% -> 1% of each run, Pallas kernels for 0% -> 12%
where the time goes in v1:
time: 91.9 us; the launch traced here: 91.2 us
  Pallas kernels  33.7 us (37%)
  blocking collectives  30.8 us (34%)
  starting transfers between devices  12.6 us (14%)
  waiting for transfers between devices  10.2 us (11%)
  local copies, waits for them, and re-layouts  3.74 us (4%)
    all_to_all x1, blocking collectives, shards(): totals = lax.all_to_all(totals, 'dh', 0, 0)  16.4 us
    all_to_all x1, blocking collectives, shards(): weights = lax.all_to_all(weights, 'blk', 0, 0)  14.5 us
    pallas_call x1, Pallas kernels, accumulate(): pl.pallas_call(body, out_shape=jax.ShapeDtypeStruct((owners, classes // o...  10.7 us
    pallas_call x1, Pallas kernels, rotate_images(): pl.pallas_call(body, out_shape=jax.ShapeDtypeStruct((nb, N1, 2 * per, cyc...  8.47 us
    all_to_all x1, starting transfers between devices, shards(): refs = lax.all_to_all(mine, 'dh', 0, 0)  8.07 us
    all_to_all x1, waiting for transfers between devices, shards(): scores = lax.all_to_all(scores, 'blk', 0, 0)  7.78 us
    pallas_call x1, Pallas kernels, correlate(): pl.pallas_call(body, out_shape=jax.ShapeDtypeStruct((nb, cols, n1 * rows)...  6.8 us
    all_to_all x1, starting transfers between devices, shards(): scores = lax.all_to_all(scores, 'blk', 0, 0)  4.41 us
  transfers between devices with their start and end apart: 5, of which 3 were waited for; matrix products, arithmetic and copies ran while one was open for 1% of the time, Pallas kernels for 12%

profile of v1, /device:TPU:0, one launch (start us, length us, event | category | flops | bytes accessed | tf_op | source)
XLA Modules:
  0.0 91.2 jit_solution(13091690978293671700)
XLA Ops:
  0.0 0.0 collective-permute-start
  0.0 2.2 %pick_block.1 = bf16[8,64,256]{2,1,0:T(8,128)(2,1)} custom-call(s32[1]{0:T(128)} %bitcast.1.me_ref, s32[16]{0:T(128)} %owner_ref.1, f32[64]{0:T(128)} %gain_ref.1, bf16[16,4,16,256]{3,2,1,0:T(8,128)(2,1)} %bitcast.6), custom_call_target="tpu_custom_call" | custom-call | tf_op jit(solution)/shard_map/pick_block/pallas_call | solution.py:52
  2.2 8.1 %all-to-all-start = ((bf16[8,64,256]{2,1,0:T(8,128)(2,1)}), bf16[8,64,256]{2,1,0:T(8,128)(2,1)S(1)}, u32[]{:S(2)}, u32[]{:S(2)}) async-start(bf16[8,64,256]{2,1,0:T(8,128)(2,1)} %pick_block.1), calls=%async_computation | async-start | bytes 524288 | tf_op jit(solution)/shard_map/all_to_all | solution.py:263
  10.3 0.0 copy-start.4
  10.3 0.0 collective-permute-done.other_ref
  10.3 0.0 copy-start.2
  10.3 0.8 copy-done.2
  11.1 8.5 %rotate_images.1.x_ref = bf16[8,8,16,4096]{3,2,1,0:T(8,128)(2,1)} custom-call(bf16[64,16,256]{2,1,0:T(8,128)(2,1)} %own_ref.1, bf16[64,16,256]{2,1,0:T(8,128)(2,1)} %copy-done.2), custom_call_target="tpu_custom_call" | custom-call | tf_op jit(solution)/shard_map/rotate_images/pallas_call | solution.py:83
  19.6 0.0 all-to-all-done.r_ref
  19.6 0.0 copy-start.1
  19.6 0.7 copy-done.1
  20.3 6.8 %correlate.1 = bf16[8,256,128]{2,1,0:T(8,128)(2,1)} custom-call(bf16[8,8,16,4096]{3,2,1,0:T(8,128)(2,1)} %rotate_images.1.x_ref, bf16[8,64,256]{2,1,0:T(8,128)(2,1)} %copy-done.1), custom_call_target="tpu_custom_call" | custom-call | tf_op jit(solution)/shard_map/correlate/pallas_call | solution.py:123
  27.1 4.4 %all-to-all-start.1 = ((bf16[8,256,128]{2,1,0:T(8,128)(2,1)}), bf16[8,256,128]{2,1,0:T(8,128)(2,1)S(1)}, u32[]{:S(2)}, u32[]{:S(2)}) async-start(bf16[8,256,128]{2,1,0:T(8,128)(2,1)} %correlate.1), calls=%async_computation.1 | async-start | bytes 1048576 | tf_op jit(solution)/shard_map/all_to_all | solution.py:266
  31.5 0.0 copy-done.4
  31.5 0.1 collective-permute-start.1
  31.6 0.1 reshape.16
  31.7 1.1 %collective-permute-done.1 = f32[64]{0:T(128)S(1)} collective-permute-done((f32[64]{0:T(128)S(1)}, f32[64]{0:T(128)S(1)}, u32[]{:S(2)}, u32[]{:S(2)}) %collective-permute-start.1) | collective-permute-done | bytes 288 | tf_op jit(solution)/shard_map/ppermute | solution.py:259
  32.7 0.1 reshape.17
  32.8 0.1 pad_maximum_fusion
  32.9 0.7 tile.10.scale_ref
  33.6 7.8 %all-to-all-done.1.x_ref = bf16[8,256,128]{2,1,0:T(8,128)(2,1)S(1)} async-done(((bf16[8,256,128]{2,1,0:T(8,128)(2,1)}), bf16[8,256,128]{2,1,0:T(8,128)(2,1)S(1)}, u32[]{:S(2)}, u32[]{:S(2)}) %all-to-all-start.1) | async-done | bytes 524320 | tf_op jit(solution)/shard_map/all_to_all | solution.py:266
  41.4 0.0 copy-start
  41.4 0.8 copy-done
  42.2 2.1 %local_softmax.1 = (f32[256,128]{1,0:T(8,128)}, f32[2,128]{1,0:T(2,128)}) custom-call(s32[1]{0:T(128)} %bitcast.me_ref, bf16[8,256,128]{2,1,0:T(8,128)(2,1)} %copy-done, f32[8,128]{1,0:T(8,128)} %tile.10.scale_ref), custom_call_target="tpu_custom_call" | custom-call | tf_op jit(solution)/shard_map/local_softmax/pallas_call | solution.py:156
  44.3 0.0 collective-permute-start.2
  44.3 1.4 %collective-permute-done.2.b_ref = f32[2,128]{1,0:T(2,128)S(1)} collective-permute-done((f32[2,128]{1,0:T(2,128)}, f32[2,128]{1,0:T(2,128)S(1)}, u32[]{:S(2)}, u32[]{:S(2)}) %collective-permute-start.2) | collective-permute-done | bytes 1056 | tf_op jit(solution)/shard_map/ppermute | solution.py:271
  45.7 0.0 copy-start.3
  45.7 0.6 copy-done.3
  46.2 1.9 %normalize.1 = bf16[8,256,128]{2,1,0:T(8,128)(2,1)} custom-call(f32[256,128]{1,0:T(8,128)} %get-tuple-element.7.e_ref, f32[2,128]{1,0:T(2,128)} %get-tuple-element.8.a_ref, f32[2,128]{1,0:T(2,128)} %copy-done.3), custom_call_target="tpu_custom_call" | custom-call | tf_op jit(solution)/shard_map/normalize/pallas_call | solution.py:183
  48.1 14.5 %all_to_all.20.w_ref = bf16[8,256,128]{2,1,0:T(8,128)(2,1)} all-to-all(bf16[8,256,128]{2,1,0:T(8,128)(2,1)} %normalize.1), channel_id=1, replica_groups=mesh['dh'=8,'core'=2,'blk'=8] {'blk'}, dimensions={0} | all-to-all | bytes 1048576 | tf_op jit(solution)/shard_map/all_to_all | solution.py:273
  62.6 10.7 %accumulate.1 = bf16[8,64,256]{2,1,0:T(8,128)(2,1)} custom-call(bf16[8,256,128]{2,1,0:T(8,128)(2,1)} %all_to_all.20.w_ref, bf16[1024,4096]{1,0:T(8,128)(2,1)} %bitcast.5), custom_call_target="tpu_custom_call" | custom-call | tf_op jit(solution)/shard_map/accumulate/pallas_call | solution.py:219
  73.2 16.4 %all_to_all.21.x_ref = bf16[8,64,256]{2,1,0:T(8,128)(2,1)} all-to-all(bf16[8,64,256]{2,1,0:T(8,128)(2,1)} %accumulate.1), channel_id=1, replica_groups=mesh['dh'=8,'core'=2,'blk'=8] {'dh'}, dimensions={0} | all-to-all | bytes 524288 | tf_op jit(solution)/shard_map/all_to_all | solution.py:275
  89.6 1.6 %add_up.1 = f32[64,256]{1,0:T(8,128)} custom-call(bf16[8,64,256]{2,1,0:T(8,128)(2,1)} %all_to_all.21.x_ref), custom_call_target="tpu_custom_call" | custom-call | tf_op jit(solution)/shard_map/add_up/pallas_call | solution.py:237
  (1 shorter events, 0.0 us)
Async XLA Ops:
  0.0 10.3 %collective-permute-start = (bf16[64,16,256]{2,1,0:T(8,128)(2,1)}, bf16[64,16,256]{2,1,0:T(8,128)(2,1)S(1)}, u32[]{:S(2)}, u32[]{:S(2)}) collective-permute-start(bf16[64,16,256]{2,1,0:T(8,128)(2,1)} %own_ref.1), channel_id=1, source_target_pairs={{0,8},{8,0},{1,9},{9,1},{2,10},{10,2},{3,11},{11,3},{4,12},{12,4},... | collective-permute-start | bytes 1572872 | tf_op jit(solution)/shard_map/ppermute | solution.py:258
  2.2 17.4 %all-to-all-start = ((bf16[8,64,256]{2,1,0:T(8,128)(2,1)}), bf16[8,64,256]{2,1,0:T(8,128)(2,1)S(1)}, u32[]{:S(2)}, u32[]{:S(2)}) async-start(bf16[8,64,256]{2,1,0:T(8,128)(2,1)} %pick_block.1), calls=%async_computation | async-start | bytes 524288 | tf_op jit(solution)/shard_map/all_to_all | solution.py:263
  10.3 21.2 %copy-start.4 = (f32[64]{0:T(128)S(1)}, f32[64]{0:T(128)}, u32[]{:S(2)}) copy-start(f32[64]{0:T(128)} %param.9) | copy-start | bytes 772
  10.3 0.8 copy-start.2
  19.6 0.7 copy-start.1
  27.1 14.3 %all-to-all-start.1 = ((bf16[8,256,128]{2,1,0:T(8,128)(2,1)}), bf16[8,256,128]{2,1,0:T(8,128)(2,1)S(1)}, u32[]{:S(2)}, u32[]{:S(2)}) async-start(bf16[8,256,128]{2,1,0:T(8,128)(2,1)} %correlate.1), calls=%async_computation.1 | async-start | bytes 1048576 | tf_op jit(solution)/shard_map/all_to_all | solution.py:266
  31.5 1.2 %collective-permute-start.1 = (f32[64]{0:T(128)S(1)}, f32[64]{0:T(128)S(1)}, u32[]{:S(2)}, u32[]{:S(2)}) collective-permute-start(f32[64]{0:T(128)S(1)} %copy-done.4), channel_id=1, source_target_pairs={{0,8},{8,0},{1,9},{9,1},{2,10},{10,2},{3,11},{11,3},{4,12},{12,4},... | collective-permute-start | bytes 776 | tf_op jit(solution)/shard_map/ppermute | solution.py:259
  41.4 0.8 copy-start
  44.3 1.4 %collective-permute-start.2 = (f32[2,128]{1,0:T(2,128)}, f32[2,128]{1,0:T(2,128)S(1)}, u32[]{:S(2)}, u32[]{:S(2)}) collective-permute-start(f32[2,128]{1,0:T(2,128)} %get-tuple-element.8.a_ref), channel_id=1, source_target_pairs={{0,8},{8,0},{1,9},{9,1},{2,10},{10,2},{3,11},{11,3},{4,12},{12,4},... | collective-permute-start | bytes 3080 | tf_op jit(solution)/shard_map/ppermute | solution.py:271
  45.7 0.6 copy-start.3

commit v2 on v1

v2 whole, which is shorter than its diff:
```python
import jax
import jax.numpy as jnp
from jax import lax
from jax.experimental import pallas as pl
from jax.experimental.pallas import tpu as pltpu
from jax.sharding import Mesh, PartitionSpec as P

BF = jnp.bfloat16
F32 = jnp.float32
VM = pltpu.VMEM
LANES = 128
N1 = 4
N2 = 8


def spec(space=VM):
    return pl.BlockSpec(memory_space=space)


def params(mib=24):
    return pltpu.CompilerParams(vmem_limit_bytes=mib * 1024 * 1024)


def here(x):
    return pltpu.with_memory_space_constraint(x, VM)


def away(x):
    return pltpu.with_memory_space_constraint(x, pltpu.HBM)


def fill(scr, value):
    for h in range(scr.shape[0]):
        scr[h] = value[:, h * LANES : (h + 1) * LANES]


def take_cycle(scr, r, rows, cycles):
    return [scr.at[h][pl.ds(r, rows, stride=cycles), :] for h in range(2)]


def narrow(x):
    wide = x * 65537.0
    return wide - (wide - x)


def narrow_sum(x):
    near = narrow(x)
    lane = lax.broadcasted_iota(jnp.int32, x.shape, 1)
    rest = jnp.sum(x - near, axis=1, keepdims=True)
    return jnp.where(lane == 0, near + rest, near)


def turn(plus, minus, t):
    t = t % (2 * LANES)
    if t == 0:
        return plus, minus
    if t >= LANES:
        return turn(plus, -minus, t - LANES)
    lane = lax.broadcasted_iota(jnp.int32, minus.shape, 1)
    minus = pltpu.roll(minus, t, 1)
    return pltpu.roll(plus, t, 1), jnp.where(lane < t, -minus, minus)


def pick_block(me, block_owner, class_gain, ref_store, copies):
    nblk, kb, cycles, angles = ref_store.shape

    def body(me_ref, owner_ref, gain_ref, store_ref, out_ref, buf, sem):
        block = jnp.int32(0)
        for b in range(nblk):
            block = jnp.where(owner_ref[b] == me_ref[0], jnp.int32(b), block)
        copy = pltpu.make_async_copy(store_ref.at[block], buf, sem)
        copy.start()
        copy.wait()
        for i in range(kb):
            piece = (buf[i].astype(F32) * gain_ref[block * kb + i]).astype(BF).astype(F32)
            a, b = piece[:, :LANES], piece[:, LANES:]
            piece = jnp.concatenate([narrow_sum(a + b), narrow(a - b)], axis=1).astype(BF)
            for c in range(copies):
                out_ref[c, i * cycles : (i + 1) * cycles, :] = piece

    return pl.pallas_call(
        body,
        out_shape=jax.ShapeDtypeStruct((copies, kb * cycles, angles), BF),
        in_specs=[spec(pltpu.SMEM), spec(pltpu.SMEM), spec(pltpu.SMEM), spec(pltpu.HBM)],
        out_specs=spec(),
        scratch_shapes=[VM((kb, cycles, angles), BF), pltpu.SemaphoreType.DMA],
        compiler_params=params(60),
        name="pick_block",
    )(me, block_owner, class_gain, away(ref_store))


def rotate_images(own, other, nb, step):
    particles, cycles, angles = own.shape
    per = particles // nb
    rows = N1 * 2 * per

    def body(own_ref, other_ref, out_ref, a_scr, b_scr):
        fill(a_scr, own_ref[...].astype(F32).reshape(per * cycles, angles))
        fill(b_scr, other_ref[...].astype(F32).reshape(per * cycles, angles))
        for r in range(cycles):
            a = take_cycle(a_scr, r, per, cycles)
            b = take_cycle(b_scr, r, per, cycles)
            plus = narrow(jnp.concatenate([a[0] + a[1], b[0] + b[1]], axis=0)).astype(BF)
            minus = narrow(jnp.concatenate([a[0] - a[1], b[0] - b[1]], axis=0)).astype(BF)
            for s in range(N1):
                p, m = turn(plus, minus, step * s)
                at = slice(s * 2 * per, (s + 1) * 2 * per)
                out_ref[0, r, at, :] = p
                out_ref[1, r, at, :] = m

    block = pl.BlockSpec((per, cycles, angles), lambda j: (j, 0, 0))
    return pl.pallas_call(
        body,
        grid=(nb,),
        out_shape=pltpu.HBM((2, cycles, nb * rows, LANES), BF),
        in_specs=[block, block],
        out_specs=pl.BlockSpec((2, cycles, rows, LANES), lambda j: (0, 0, j, 0)),
        scratch_shapes=[VM((2, per * cycles, LANES), F32)] * 2,
        compiler_params=params(),
        name="rotate_images",
    )(away(own), other)


def correlate(turned, refs, cycles, nb, step):
    total = turned.shape[2]
    rows = total // nb
    classes = refs.shape[0] * refs.shape[1] // cycles
    cols = N2 * classes
    angles = 2 * LANES

    def body(x_hbm, r_ref, out_ref, scr, rr, x, sems):
        copies = [pltpu.make_async_copy(x_hbm.at[i], x.at[i], sems.at[i]) for i in range(2)]
        for copy in copies:
            copy.start()
        fill(scr, r_ref[...].astype(F32).reshape(classes * cycles, angles))
        square = jnp.zeros((classes, LANES), F32)
        for r in range(cycles):
            plus, minus = take_cycle(scr, r, classes, cycles)
            square = square + 0.5 * (plus * plus + minus * minus)
            plus, minus = plus.astype(BF), minus.astype(BF)
            for s in range(N2):
                p, m = turn(plus, minus, angles - step * s)
                rr[0, r, s * classes : (s + 1) * classes, :] = p
                rr[1, r, s * classes : (s + 1) * classes, :] = m
        norm = jnp.broadcast_to(jnp.sum(square, axis=1, keepdims=True), (classes, cols))
        k = lax.broadcasted_iota(jnp.int32, (classes, cols), 0)
        lane = lax.broadcasted_iota(jnp.int32, (classes, cols), 1)
        norm = jnp.sum(jnp.where(lane % classes == k, norm, 0.0), axis=0, keepdims=True)
        for i in range(2):
            copies[i].wait()
            left = jnp.concatenate([x[i, r] for r in range(cycles)], axis=1)
            right = jnp.concatenate([rr[i, r] for r in range(cycles)], axis=1)
            part = lax.dot_general(
                left, right, (((1,), (1,)), ((), ())), preferred_element_type=F32
            )
            if i == 0:
                part = part - norm
            for t in range(cols // LANES):
                tile = part[:, t * LANES : (t + 1) * LANES].astype(BF)
                out_ref[:, t, i * rows : (i + 1) * rows, :] = tile.reshape(nb, rows, LANES)

    return pl.pallas_call(
        body,
        out_shape=jax.ShapeDtypeStruct((nb, cols // LANES, 2 * rows, LANES), BF),
        in_specs=[spec(pltpu.HBM), spec()],
        out_specs=spec(),
        scratch_shapes=[
            VM((2, classes * cycles, LANES), F32),
            VM((2, cycles, cols, LANES), BF),
            VM((2, cycles, total, LANES), BF),
            pltpu.SemaphoreType.DMA((2,)),
        ],
        compiler_params=params(),
        name="correlate",
    )(away(turned), here(refs))


def local_softmax(me, scores, precision, others):
    nb, tiles, rows, _ = scores.shape
    cols = tiles * LANES
    half = rows // 2
    group = half // N1
    own = group // 2

    def across(op, x):
        pieces = [x[i * group : (i + 1) * group] for i in range(N1)]
        return op(op(pieces[0], pieces[1]), op(pieces[2], pieces[3]))

    def body(me_ref, x_ref, a_ref, b_ref, e_ref, stat_ref):
        total = x_ref[0].astype(F32)
        for i in range(1, nb):
            total = total + x_ref[i].astype(F32)
        total = jnp.concatenate([total[t] for t in range(tiles)], axis=1)
        plus, minus = total[:half], total[half:]
        row = lax.broadcasted_iota(jnp.int32, (own, own), 0)
        col = lax.broadcasted_iota(jnp.int32, (own, own), 1)
        scale = [
            jnp.sum(jnp.where(row == col, ref[pl.ds(me_ref[0], 1), :], 0.0), axis=1, keepdims=True)
            for ref in (a_ref, b_ref)
        ]
        scale = jnp.concatenate(scale * N1, axis=0) * 0.5
        near, far = scale * (plus + minus), scale * (plus - minus)
        top = jnp.max(jnp.maximum(near, far), axis=1, keepdims=True)
        top = across(jnp.maximum, top)
        tops = jnp.concatenate([top] * N1, axis=0)
        near, far = jnp.exp(near - tops), jnp.exp(far - tops)
        e_ref[0] = near
        e_ref[1] = far
        amount = across(jnp.add, jnp.sum(near + far, axis=1, keepdims=True))
        stat_ref[0] = jnp.broadcast_to(top, (group, LANES))
        stat_ref[1] = jnp.broadcast_to(amount, (group, LANES))

    return pl.pallas_call(
        body,
        out_shape=(VM((2, half, cols), F32), VM((2, group, LANES), F32)),
        in_specs=[spec(pltpu.SMEM), spec(), spec(), spec()],
        out_specs=(spec(), spec()),
        compiler_params=params(),
        name="local_softmax",
    )(me, here(scores), here(precision), here(others))


def normalize(e, mine, theirs, copies):
    _, half, cols = e.shape
    group = mine.shape[1]

    def body(e_ref, a_ref, b_ref, out_ref):
        def flipped(x):
            return jnp.concatenate([x[group // 2 :], x[: group // 2]], axis=0)

        top_a, sum_a = a_ref[0], a_ref[1]
        top_b, sum_b = flipped(b_ref[0]), flipped(b_ref[1])
        top = jnp.maximum(top_a, top_b)
        part = jnp.exp(top_a - top)
        factor = part / (sum_a * part + sum_b * jnp.exp(top_b - top))
        factor = jnp.concatenate([jnp.concatenate([factor] * N1, axis=0)] * (cols // LANES), axis=1)
        near, far = e_ref[0] * factor, e_ref[1] * factor
        w = jnp.concatenate([near + far, near - far], axis=0).T.astype(BF)
        for c in range(copies):
            out_ref[c] = w

    return pl.pallas_call(
        body,
        out_shape=VM((copies, cols, 2 * half), BF),
        in_specs=[spec(), spec(), spec()],
        out_specs=spec(),
        compiler_params=params(),
        name="normalize",
    )(here(e), here(mine), here(theirs))


def accumulate(weights, turned, cycles, owners, step):
    nb, cols, lanes = weights.shape
    total = turned.shape[2]
    classes = cols // N2
    pair = 2 * LANES

    def body(w_ref, x_hbm, out_ref, scr, x, sems):
        copies = [pltpu.make_async_copy(x_hbm.at[i], x.at[i], sems.at[i]) for i in range(2)]
        for copy in copies:
            copy.start()
        left = lax.broadcasted_iota(jnp.int32, (cols, lanes), 1) < lanes // 2
        near, far = [], []
        for j in range(0, nb, 2):
            a, b = w_ref[j], w_ref[j + 1]
            near.append(jnp.where(left, a, pltpu.roll(b, lanes // 2, 1)))
            far.append(jnp.where(left, pltpu.roll(a, lanes // 2, 1), b))
        w = [jnp.concatenate(v, axis=1) for v in (near, far)]
        for copy in copies:
            copy.wait()
        for c in range(0, cycles, 2):
            spread = []
            for i in range(2):
                both = jnp.concatenate([x[i, c], x[i, c + 1]], axis=1)
                spread.append(jnp.dot(w[i], both, preferred_element_type=F32))
            for d in range(2):
                plus = minus = None
                for s in range(N2):
                    p, m = (
                        v[s * classes : (s + 1) * classes, d * LANES : (d + 1) * LANES]
                        for v in spread
                    )
                    p, m = turn(p, m, step * s)
                    plus = plus + p if s else p
                    minus = minus + m if s else m
                rows = pl.ds(c + d, classes, stride=cycles)
                scr.at[0][rows, :] = 0.5 * (plus + minus)
                scr.at[1][rows, :] = 0.5 * (plus - minus)
        whole = jnp.concatenate([scr[0], scr[1]], axis=1)
        out_ref[...] = whole.reshape(out_ref.shape).astype(BF)

    return pl.pallas_call(
        body,
        out_shape=VM((owners, classes // owners * cycles, pair), BF),
        in_specs=[spec(), spec(pltpu.HBM)],
        out_specs=spec(),
        scratch_shapes=[
            VM((2, classes * cycles, LANES), F32),
            VM((2, cycles, total, LANES), BF),
            pltpu.SemaphoreType.DMA((2,)),
        ],
        compiler_params=params(),
        name="accumulate",
    )(here(weights), away(turned))


def add_up(parts):
    def body(x_ref, out_ref):
        total = x_ref[0].astype(F32)
        for i in range(1, parts.shape[0]):
            total = total + x_ref[i].astype(F32)
        out_ref[...] = total

    return pl.pallas_call(
        body,
        out_shape=jax.ShapeDtypeStruct(parts.shape[1:], F32),
        in_specs=[spec()],
        out_specs=spec(),
        compiler_params=params(),
        name="add_up",
    )(here(parts))


def solution(mesh):
    dom, nb = mesh.devices.shape
    nd = dom // 2
    view = Mesh(mesh.devices.reshape(nd, 2, nb), ("dh", "core", "blk"))
    swap = [(0, 1), (1, 0)]

    def shards(images, ref_store, block_owner, class_gain, precision):
        particles, cycles, angles = images.shape
        kb = ref_store.shape[2]
        rot = angles // (2 * N1 * N2)
        half = particles // nb
        other = lax.ppermute(images, "core", swap)
        other_precision = lax.ppermute(precision, "core", swap)
        me = (lax.axis_index("dh") * 2 + lax.axis_index("core"))[None].astype(jnp.int32)
        j = lax.axis_index("blk")[None].astype(jnp.int32)
        mine = pick_block(me, block_owner, class_gain, ref_store[0], nd)
        refs = lax.all_to_all(mine, "dh", 0, 0)
        turned = rotate_images(images, other, nb, rot)
        scores = correlate(turned, refs, cycles, nb, rot * N1)
        scores = lax.all_to_all(scores, "blk", 0, 0)
        e, stats = local_softmax(
            j, scores, precision.reshape(nb, half), other_precision.reshape(nb, half)
        )
        theirs = lax.ppermute(stats, "core", swap)
        weights = normalize(e, stats, theirs, nb)
        weights = lax.all_to_all(weights, "blk", 0, 0)
        totals = accumulate(weights, turned, cycles, nd, rot * N1)
        totals = lax.all_to_all(totals, "dh", 0, 0)
        return add_up(totals).reshape(1, 1, kb, cycles, angles)

    dom_axes = ("dh", "core")
    return jax.shard_map(
        shards,
        mesh=view,
        in_specs=(
            P(dom_axes, "blk", None),
            P(dom_axes, None, None, "blk", None),
            P(),
            P(),
            P(dom_axes),
        ),
        out_specs=P(dom_axes, None, None, "blk", None),
        check_vma=False,
    )
```

time: 91.9 us -> 72.6 us (0.79)
  Pallas kernels: 33.7 us -> 18.9 us
  local copies, waits for them, and re-layouts: 3.74 us -> 0.16 us
  blocking collectives: 30.8 us -> 27.6 us
  waiting for transfers between devices: 10.2 us -> 12.4 us
    pallas_call x5, Pallas kernels: 29.9 us -> 16 us  [the longest x1 6.13 us: rotate_images(): pl.pallas_call(body, grid=(nb,), out_shape=pltpu.HBM((2, cycles, nb * row...]
    all_to_all x1, waiting for transfers between devices: 0.01 us -> 3.12 us  [shards(): refs = lax.all_to_all(mine, 'dh', 0, 0)]
    unnamed x10 -> x2, local copies, waits for them, and re-layouts: 2.91 us -> 0.01 us
    all_to_all x1, blocking collectives: 16.4 us -> 14.6 us  [shards(): totals = lax.all_to_all(totals, 'dh', 0, 0)]
    all_to_all x1, blocking collectives: 14.5 us -> 13.1 us  [shards(): weights = lax.all_to_all(weights, 'blk', 0, 0)]
    pallas_call x1, Pallas kernels: 1.62 us -> 0.67 us  [add_up(): pl.pallas_call(body, out_shape=jax.ShapeDtypeStruct(parts.shape[1:], F32)...]
  transfers between devices with their start and end apart: 5 -> 5, of which waited for: 3 -> 4; matrix products, arithmetic and copies ran while one was open for 1% -> 0% of each run, Pallas kernels for 12% -> 12%
where the time goes in v2:
time: 72.6 us; the launch traced here: 71.8 us
  blocking collectives  27.6 us (38%)
  Pallas kernels  18.9 us (26%)
  starting transfers between devices  12.6 us (17%)
  waiting for transfers between devices  12.4 us (17%)
    all_to_all x1, blocking collectives, shards(): totals = lax.all_to_all(totals, 'dh', 0, 0)  14.6 us
    all_to_all x1, blocking collectives, shards(): weights = lax.all_to_all(weights, 'blk', 0, 0)  13.1 us
    all_to_all x1, starting transfers between devices, shards(): refs = lax.all_to_all(mine, 'dh', 0, 0)  8.07 us
    all_to_all x1, waiting for transfers between devices, shards(): scores = lax.all_to_all(scores, 'blk', 0, 0)  7.07 us
    pallas_call x1, Pallas kernels, rotate_images(): pl.pallas_call(body, grid=(nb,), out_shape=pltpu.HBM((2, cycles, nb * row...  6.13 us
    pallas_call x1, Pallas kernels, correlate(): pl.pallas_call(body, out_shape=jax.ShapeDtypeStruct((nb, cols // LANES, 2...  5.49 us
    all_to_all x1, starting transfers between devices, shards(): scores = lax.all_to_all(scores, 'blk', 0, 0)  4.43 us
    pallas_call x1, Pallas kernels, accumulate(): pl.pallas_call(body, out_shape=VM((owners, classes // owners * cycles, pa...  3.85 us
  transfers between devices with their start and end apart: 5, of which 4 were waited for; matrix products, arithmetic and copies ran while one was open for 0% of the time, Pallas kernels for 12%

profile of v2, /device:TPU:0, one launch (start us, length us, event | category | flops | bytes accessed | tf_op | source)
XLA Modules:
  0.0 71.8 jit_solution(18117525480793554094)
XLA Ops:
  0.0 0.0 collective-permute-start
  0.0 2.3 %pick_block.1 = bf16[8,64,256]{2,1,0:T(8,128)(2,1)} custom-call(s32[1]{0:T(128)} %bitcast.1.me_ref, s32[16]{0:T(128)} %owner_ref.1, f32[64]{0:T(128)} %gain_ref.1, bf16[16,4,16,256]{3,2,1,0:T(8,128)(2,1)} %bitcast.4), custom_call_target="tpu_custom_call" | custom-call | tf_op jit(solution)/shard_map/pick_block/pallas_call | solution.py:81
  2.3 8.1 %all-to-all-start = ((bf16[8,64,256]{2,1,0:T(8,128)(2,1)}), bf16[8,64,256]{2,1,0:T(8,128)(2,1)S(1)}, u32[]{:S(2)}, u32[]{:S(2)}) async-start(bf16[8,64,256]{2,1,0:T(8,128)(2,1)} %pick_block.1), calls=%async_computation | async-start | bytes 524288 | tf_op jit(solution)/shard_map/all_to_all | solution.py:340
  10.3 0.0 collective-permute-done.other_ref
  10.3 6.1 %rotate_images.1.x_hbm = bf16[2,16,512,128]{3,2,1,0:T(8,128)(2,1)} custom-call(bf16[64,16,256]{2,1,0:T(8,128)(2,1)} %own_ref.1, bf16[64,16,256]{2,1,0:T(8,128)(2,1)S(1)} %collective-permute-done.other_ref), custom_call_target="tpu_custom_call" | custom-call | tf_op jit(solution)/shard_map/rotate_images/pallas_call | solution.py:112
  16.5 0.0 copy-start
  16.5 3.1 %all-to-all-done.r_ref = bf16[8,64,256]{2,1,0:T(8,128)(2,1)S(1)} async-done(((bf16[8,64,256]{2,1,0:T(8,128)(2,1)}), bf16[8,64,256]{2,1,0:T(8,128)(2,1)S(1)}, u32[]{:S(2)}, u32[]{:S(2)}) %all-to-all-start) | async-done | bytes 262176 | tf_op jit(solution)/shard_map/all_to_all | solution.py:340
  19.6 5.5 %correlate.1 = bf16[8,2,128,128]{3,2,1,0:T(8,128)(2,1)} custom-call(bf16[2,16,512,128]{3,2,1,0:T(8,128)(2,1)} %rotate_images.1.x_hbm, bf16[8,64,256]{2,1,0:T(8,128)(2,1)S(1)} %all-to-all-done.r_ref), custom_call_target="tpu_custom_call" | custom-call | tf_op jit(solution)/shard_map/correlate/pallas_call | solution.py:162
  25.1 4.4 %all-to-all-start.1 = ((bf16[8,2,128,128]{3,2,1,0:T(8,128)(2,1)}), bf16[8,2,128,128]{3,2,1,0:T(8,128)(2,1)S(1)}, u32[]{:S(2)}, u32[]{:S(2)}) async-start(bf16[8,2,128,128]{3,2,1,0:T(8,128)(2,1)} %correlate.1), calls=%async_computation.1 | async-start | bytes 1048576 | tf_op jit(solution)/shard_map/all_to_all | solution.py:343
  29.5 0.0 copy-done
  29.5 0.1 collective-permute-start.1
  29.6 0.1 reshape.9.a_ref
  29.7 1.1 %collective-permute-done.1 = f32[64]{0:T(128)S(1)} collective-permute-done((f32[64]{0:T(128)S(1)}, f32[64]{0:T(128)S(1)}, u32[]{:S(2)}, u32[]{:S(2)}) %collective-permute-start.1) | collective-permute-done | bytes 288 | tf_op jit(solution)/shard_map/ppermute | solution.py:336
  30.8 0.1 reshape.10.b_ref
  30.9 7.1 %all-to-all-done.1.x_ref = bf16[8,2,128,128]{3,2,1,0:T(8,128)(2,1)S(1)} async-done(((bf16[8,2,128,128]{3,2,1,0:T(8,128)(2,1)}), bf16[8,2,128,128]{3,2,1,0:T(8,128)(2,1)S(1)}, u32[]{:S(2)}, u32[]{:S(2)}) %all-to-all-start.1) | async-done | bytes 524320 | tf_op jit(solution)/shard_map/all_to_all | solution.py:343
  37.9 0.4 local_softmax.1
  38.3 0.1 collective-permute-start.2
  38.4 1.2 %collective-permute-done.2.b_ref = f32[2,16,128]{2,1,0:T(8,128)S(1)} collective-permute-done((f32[2,16,128]{2,1,0:T(8,128)S(1)}, f32[2,16,128]{2,1,0:T(8,128)S(1)}, u32[]{:S(2)}, u32[]{:S(2)}) %collective-permute-start.2) | collective-permute-done | bytes 16416 | tf_op jit(solution)/shard_map/ppermute | solution.py:347
  39.6 0.1 normalize.1
  39.7 13.1 %all_to_all.20.w_ref = bf16[8,256,128]{2,1,0:T(8,128)(2,1)S(1)} all-to-all(bf16[8,256,128]{2,1,0:T(8,128)(2,1)S(1)} %normalize.1), channel_id=1, replica_groups=mesh['dh'=8,'core'=2,'blk'=8] {'blk'}, dimensions={0} | all-to-all | bytes 1048576 | tf_op jit(solution)/shard_map/all_to_all | solution.py:349
  52.8 3.8 %accumulate.1 = bf16[8,64,256]{2,1,0:T(8,128)(2,1)S(1)} custom-call(bf16[8,256,128]{2,1,0:T(8,128)(2,1)S(1)} %all_to_all.20.w_ref, bf16[2,16,512,128]{3,2,1,0:T(8,128)(2,1)} %rotate_images.1.x_hbm), custom_call_target="tpu_custom_call" | custom-call | tf_op jit(solution)/shard_map/accumulate/pallas_call | solution.py:292
  56.6 14.6 %all_to_all.21.x_ref = bf16[8,64,256]{2,1,0:T(8,128)(2,1)S(1)} all-to-all(bf16[8,64,256]{2,1,0:T(8,128)(2,1)S(1)} %accumulate.1), channel_id=1, replica_groups=mesh['dh'=8,'core'=2,'blk'=8] {'dh'}, dimensions={0} | all-to-all | bytes 524288 | tf_op jit(solution)/shard_map/all_to_all | solution.py:351
  71.2 0.7 add_up.1
Async XLA Ops:
  0.0 10.3 %collective-permute-start = (bf16[64,16,256]{2,1,0:T(8,128)(2,1)}, bf16[64,16,256]{2,1,0:T(8,128)(2,1)S(1)}, u32[]{:S(2)}, u32[]{:S(2)}) collective-permute-start(bf16[64,16,256]{2,1,0:T(8,128)(2,1)} %own_ref.1), channel_id=1, source_target_pairs={{0,8},{8,0},{1,9},{9,1},{2,10},{10,2},{3,11},{11,3},{4,12},{12,4},... | collective-permute-start | bytes 1572872 | tf_op jit(solution)/shard_map/ppermute | solution.py:335
  2.3 17.3 %all-to-all-start = ((bf16[8,64,256]{2,1,0:T(8,128)(2,1)}), bf16[8,64,256]{2,1,0:T(8,128)(2,1)S(1)}, u32[]{:S(2)}, u32[]{:S(2)}) async-start(bf16[8,64,256]{2,1,0:T(8,128)(2,1)} %pick_block.1), calls=%async_computation | async-start | bytes 524288 | tf_op jit(solution)/shard_map/all_to_all | solution.py:340
  16.5 13.1 %copy-start = (f32[64]{0:T(128)S(1)}, f32[64]{0:T(128)}, u32[]{:S(2)}) copy-start(f32[64]{0:T(128)} %param.9) | copy-start | bytes 772
  25.1 12.8 %all-to-all-start.1 = ((bf16[8,2,128,128]{3,2,1,0:T(8,128)(2,1)}), bf16[8,2,128,128]{3,2,1,0:T(8,128)(2,1)S(1)}, u32[]{:S(2)}, u32[]{:S(2)}) async-start(bf16[8,2,128,128]{3,2,1,0:T(8,128)(2,1)} %correlate.1), calls=%async_computation.1 | async-start | bytes 1048576 | tf_op jit(solution)/shard_map/all_to_all | solution.py:343
  29.5 1.2 %collective-permute-start.1 = (f32[64]{0:T(128)S(1)}, f32[64]{0:T(128)S(1)}, u32[]{:S(2)}, u32[]{:S(2)}) collective-permute-start(f32[64]{0:T(128)S(1)} %copy-done), channel_id=1, source_target_pairs={{0,8},{8,0},{1,9},{9,1},{2,10},{10,2},{3,11},{11,3},{4,12},{12,4},... | collective-permute-start | bytes 776 | tf_op jit(solution)/shard_map/ppermute | solution.py:336
  38.3 1.2 %collective-permute-start.2 = (f32[2,16,128]{2,1,0:T(8,128)S(1)}, f32[2,16,128]{2,1,0:T(8,128)S(1)}, u32[]{:S(2)}, u32[]{:S(2)}) collective-permute-start(f32[2,16,128]{2,1,0:T(8,128)S(1)} %get-tuple-element.8.a_ref), channel_id=1, source_target_pairs={{0,8},{8,0},{1,9},{9,1},{2,10},{10,2},{3,11},{11,3},{4,12},{12,4},... | collective-permute-start | bytes 49160 | tf_op jit(solution)/shard_map/ppermute | solution.py:347

commit v3 on v2

--- a/solution.py
+++ b/solution.py
@@ -89,57 +89,63 @@
     )(me, block_owner, class_gain, away(ref_store))
 
 
-def rotate_images(own, other, nb, step):
+def halve_images(own, other, nb):
     particles, cycles, angles = own.shape
     per = particles // nb
-    rows = N1 * 2 * per
 
     def body(own_ref, other_ref, out_ref, a_scr, b_scr):
-        fill(a_scr, own_ref[...].astype(F32).reshape(per * cycles, angles))
-        fill(b_scr, other_ref[...].astype(F32).reshape(per * cycles, angles))
+        fill(a_scr, own_ref[...].astype(F32).reshape(particles * cycles, angles))
+        fill(b_scr, other_ref[...].astype(F32).reshape(particles * cycles, angles))
         for r in range(cycles):
-            a = take_cycle(a_scr, r, per, cycles)
-            b = take_cycle(b_scr, r, per, cycles)
-            plus = narrow(jnp.concatenate([a[0] + a[1], b[0] + b[1]], axis=0)).astype(BF)
-            minus = narrow(jnp.concatenate([a[0] - a[1], b[0] - b[1]], axis=0)).astype(BF)
-            for s in range(N1):
-                p, m = turn(plus, minus, step * s)
-                at = slice(s * 2 * per, (s + 1) * 2 * per)
-                out_ref[0, r, at, :] = p
-                out_ref[1, r, at, :] = m
-
-    block = pl.BlockSpec((per, cycles, angles), lambda j: (j, 0, 0))
-    return pl.pallas_call(
-        body,
-        grid=(nb,),
-        out_shape=pltpu.HBM((2, cycles, nb * rows, LANES), BF),
-        in_specs=[block, block],
-        out_specs=pl.BlockSpec((2, cycles, rows, LANES), lambda j: (0, 0, j, 0)),
-        scratch_shapes=[VM((2, per * cycles, LANES), F32)] * 2,
-        compiler_params=params(),
-        name="rotate_images",
-    )(away(own), other)
-
-
-def correlate(turned, refs, cycles, nb, step):
-    total = turned.shape[2]
+            a = take_cycle(a_scr, r, particles, cycles)
+            b = take_cycle(b_scr, r, particles, cycles)
+            for i, op in enumerate((jnp.add, jnp.subtract)):
+                x, y = op(a[0], a[1]), op(b[0], b[1])
+                both = [v.reshape(nb, per, LANES) for v in (x, y)]
+                both = jnp.concatenate(both, axis=1).reshape(2 * particles, LANES)
+                out_ref[i, r] = narrow(both).astype(BF)
+
+    return pl.pallas_call(
+        body,
+        out_shape=VM((2, cycles, 2 * particles, LANES), BF),
+        in_specs=[spec(), spec()],
+        out_specs=spec(),
+        scratch_shapes=[VM((2, particles * cycles, LANES), F32)] * 2,
+        compiler_params=params(),
+        name="halve_images",
+    )(own, here(other))
+
+
+def rotate_images(x_ref, r, nb, step):
+    plus, minus = x_ref[0, r], x_ref[1, r]
+    per = plus.shape[0] // nb
+    turned = [turn(plus, minus, step * s) for s in range(N1)]
+    return [
+        jnp.concatenate(
+            [t[i][j * per : (j + 1) * per] for j in range(nb) for t in turned], axis=0
+        )
+        for i in range(2)
+    ]
+
+
+def correlate(images, refs, nb, step):
+    _, cycles, particles, _ = images.shape
+    total = N1 * particles
     rows = total // nb
     classes = refs.shape[0] * refs.shape[1] // cycles
     cols = N2 * classes
     angles = 2 * LANES
 
-    def body(x_hbm, r_ref, out_ref, scr, rr, x, sems):
-        copies = [pltpu.make_async_copy(x_hbm.at[i], x.at[i], sems.at[i]) for i in range(2)]
-        for copy in copies:
-            copy.start()
+    def body(x_ref, r_ref, out_ref, scr, rr, x):
         fill(scr, r_ref[...].astype(F32).reshape(classes * cycles, angles))
         square = jnp.zeros((classes, LANES), F32)
         for r in range(cycles):
             plus, minus = take_cycle(scr, r, classes, cycles)
             square = square + 0.5 * (plus * plus + minus * minus)
             plus, minus = plus.astype(BF), minus.astype(BF)
+            x[0, r], x[1, r] = rotate_images(x_ref, r, nb, step)
             for s in range(N2):
-                p, m = turn(plus, minus, angles - step * s)
+                p, m = turn(plus, minus, angles - step * N1 * s)
                 rr[0, r, s * classes : (s + 1) * classes, :] = p
                 rr[1, r, s * classes : (s + 1) * classes, :] = m
         norm = jnp.broadcast_to(jnp.sum(square, axis=1, keepdims=True), (classes, cols))
@@ -147,7 +153,6 @@
         lane = lax.broadcasted_iota(jnp.int32, (classes, cols), 1)
         norm = jnp.sum(jnp.where(lane % classes == k, norm, 0.0), axis=0, keepdims=True)
         for i in range(2):
-            copies[i].wait()
             left = jnp.concatenate([x[i, r] for r in range(cycles)], axis=1)
             right = jnp.concatenate([rr[i, r] for r in range(cycles)], axis=1)
             part = lax.dot_general(
@@ -162,17 +167,16 @@
     return pl.pallas_call(
         body,
         out_shape=jax.ShapeDtypeStruct((nb, cols // LANES, 2 * rows, LANES), BF),
-        in_specs=[spec(pltpu.HBM), spec()],
+        in_specs=[spec(), spec()],
         out_specs=spec(),
         scratch_shapes=[
             VM((2, classes * cycles, LANES), F32),
             VM((2, cycles, cols, LANES), BF),
             VM((2, cycles, total, LANES), BF),
-            pltpu.SemaphoreType.DMA((2,)),
         ],
         compiler_params=params(),
         name="correlate",
-    )(away(turned), here(refs))
+    )(here(images), here(refs))
 
 
 def local_softmax(me, scores, precision, others):
@@ -249,16 +253,13 @@
     )(here(e), here(mine), here(theirs))
 
 
-def accumulate(weights, turned, cycles, owners, step):
+def accumulate(weights, images, owners, step):
     nb, cols, lanes = weights.shape
-    total = turned.shape[2]
+    cycles = images.shape[1]
     classes = cols // N2
     pair = 2 * LANES
 
-    def body(w_ref, x_hbm, out_ref, scr, x, sems):
-        copies = [pltpu.make_async_copy(x_hbm.at[i], x.at[i], sems.at[i]) for i in range(2)]
-        for copy in copies:
-            copy.start()
+    def body(w_ref, x_ref, out_ref, scr):
         left = lax.broadcasted_iota(jnp.int32, (cols, lanes), 1) < lanes // 2
         near, far = [], []
         for j in range(0, nb, 2):
@@ -266,12 +267,11 @@
             near.append(jnp.where(left, a, pltpu.roll(b, lanes // 2, 1)))
             far.append(jnp.where(left, pltpu.roll(a, lanes // 2, 1), b))
         w = [jnp.concatenate(v, axis=1) for v in (near, far)]
-        for copy in copies:
-            copy.wait()
         for c in range(0, cycles, 2):
+            turned = [rotate_images(x_ref, c + d, nb, step) for d in range(2)]
             spread = []
             for i in range(2):
-                both = jnp.concatenate([x[i, c], x[i, c + 1]], axis=1)
+                both = jnp.concatenate([turned[0][i], turned[1][i]], axis=1)
                 spread.append(jnp.dot(w[i], both, preferred_element_type=F32))
             for d in range(2):
                 plus = minus = None
@@ -280,7 +280,7 @@
                         v[s * classes : (s + 1) * classes, d * LANES : (d + 1) * LANES]
                         for v in spread
                     )
-                    p, m = turn(p, m, step * s)
+                    p, m = turn(p, m, step * N1 * s)
                     plus = plus + p if s else p
                     minus = minus + m if s else m
                 rows = pl.ds(c + d, classes, stride=cycles)
@@ -292,16 +292,12 @@
     return pl.pallas_call(
         body,
         out_shape=VM((owners, classes // owners * cycles, pair), BF),
-        in_specs=[spec(), spec(pltpu.HBM)],
-        out_specs=spec(),
-        scratch_shapes=[
-            VM((2, classes * cycles, LANES), F32),
-            VM((2, cycles, total, LANES), BF),
-            pltpu.SemaphoreType.DMA((2,)),
-        ],
+        in_specs=[spec(), spec()],
+        out_specs=spec(),
+        scratch_shapes=[VM((2, classes * cycles, LANES), F32)],
         compiler_params=params(),
         name="accumulate",
-    )(here(weights), away(turned))
+    )(here(weights), here(images))
 
 
 def add_up(parts):
@@ -338,8 +334,8 @@
         j = lax.axis_index("blk")[None].astype(jnp.int32)
         mine = pick_block(me, block_owner, class_gain, ref_store[0], nd)
         refs = lax.all_to_all(mine, "dh", 0, 0)
-        turned = rotate_images(images, other, nb, rot)
-        scores = correlate(turned, refs, cycles, nb, rot * N1)
+        halves = halve_images(images, other, nb)
+        scores = correlate(halves, refs, nb, rot)
         scores = lax.all_to_all(scores, "blk", 0, 0)
         e, stats = local_softmax(
             j, scores, precision.reshape(nb, half), other_precision.reshape(nb, half)
@@ -347,7 +343,7 @@
         theirs = lax.ppermute(stats, "core", swap)
         weights = normalize(e, stats, theirs, nb)
         weights = lax.all_to_all(weights, "blk", 0, 0)
-        totals = accumulate(weights, turned, cycles, nd, rot * N1)
+        totals = accumulate(weights, halves, nd, rot)
         totals = lax.all_to_all(totals, "dh", 0, 0)
         return add_up(totals).reshape(1, 1, kb, cycles, angles)
 

time: 72.6 us -> 68.8 us (0.948)
  Pallas kernels: 18.9 us -> 11.6 us
  waiting for transfers between devices: 12.4 us -> 17.2 us
  blocking collectives: 27.6 us -> 26.5 us
    pallas_call x1, Pallas kernels: 6.13 us -> 1.32 us  [halve_images(): pl.pallas_call(body, out_shape=VM((2, cycles, 2 * particles, LANES), BF),...]
    all_to_all x1, waiting for transfers between devices: 3.12 us -> 7.92 us  [shards(): refs = lax.all_to_all(mine, 'dh', 0, 0)]
    pallas_call x1, Pallas kernels: 5.49 us -> 2.77 us  [correlate(): pl.pallas_call(body, out_shape=jax.ShapeDtypeStruct((nb, cols // LANES, 2...]
    all_to_all x1, blocking collectives: 14.6 us -> 13.5 us  [shards(): totals = lax.all_to_all(totals, 'dh', 0, 0)]
  transfers between devices with their start and end apart: 5 -> 5, of which waited for: 4 -> 4; matrix products, arithmetic and copies ran while one was open for 0% -> 0% of each run, Pallas kernels for 12% -> 5%
where the time goes in v3:
time: 68.8 us; the launch traced here: 68.4 us
  blocking collectives  26.5 us (39%)
  waiting for transfers between devices  17.2 us (25%)
  starting transfers between devices  12.8 us (19%)
  Pallas kernels  11.6 us (17%)
    all_to_all x1, blocking collectives, shards(): totals = lax.all_to_all(totals, 'dh', 0, 0)  13.5 us
    all_to_all x1, blocking collectives, shards(): weights = lax.all_to_all(weights, 'blk', 0, 0)  13 us
    all_to_all x1, starting transfers between devices, shards(): refs = lax.all_to_all(mine, 'dh', 0, 0)  8.07 us
    all_to_all x1, waiting for transfers between devices, shards(): refs = lax.all_to_all(mine, 'dh', 0, 0)  7.92 us
    all_to_all x1, waiting for transfers between devices, shards(): scores = lax.all_to_all(scores, 'blk', 0, 0)  7.07 us
    all_to_all x1, starting transfers between devices, shards(): scores = lax.all_to_all(scores, 'blk', 0, 0)  4.54 us
    pallas_call x1, Pallas kernels, accumulate(): pl.pallas_call(body, out_shape=VM((owners, classes // owners * cycles, pa...  3.9 us
    pallas_call x1, Pallas kernels, correlate(): pl.pallas_call(body, out_shape=jax.ShapeDtypeStruct((nb, cols // LANES, 2...  2.77 us
  transfers between devices with their start and end apart: 5, of which 4 were waited for; matrix products, arithmetic and copies ran while one was open for 0% of the time, Pallas kernels for 5%

profile of v3, /device:TPU:0, one launch (start us, length us, event | category | flops | bytes accessed | tf_op | source)
XLA Modules:
  0.0 68.4 jit_solution(11894294348901890295)
XLA Ops:
  0.0 0.0 collective-permute-start
  0.0 0.0 copy-start
  0.0 2.4 %pick_block.1 = bf16[8,64,256]{2,1,0:T(8,128)(2,1)} custom-call(s32[1]{0:T(128)} %bitcast.1.me_ref, s32[16]{0:T(128)} %owner_ref.1, f32[64]{0:T(128)} %gain_ref.1, bf16[16,4,16,256]{3,2,1,0:T(8,128)(2,1)} %bitcast.4), custom_call_target="tpu_custom_call" | custom-call | tf_op jit(solution)/shard_map/pick_block/pallas_call | solution.py:81
  2.4 8.1 %all-to-all-start = ((bf16[8,64,256]{2,1,0:T(8,128)(2,1)}), bf16[8,64,256]{2,1,0:T(8,128)(2,1)S(1)}, u32[]{:S(2)}, u32[]{:S(2)}) async-start(bf16[8,64,256]{2,1,0:T(8,128)(2,1)} %pick_block.1), calls=%async_computation | async-start | bytes 524288 | tf_op jit(solution)/shard_map/all_to_all | solution.py:336
  10.5 0.0 collective-permute-done.other_ref
  10.5 0.0 copy-done
  10.5 1.3 %halve_images.1.x_ref = bf16[2,16,128,128]{3,2,1,0:T(8,128)(2,1)S(1)} custom-call(bf16[64,16,256]{2,1,0:T(8,128)(2,1)S(1)} %copy-done, bf16[64,16,256]{2,1,0:T(8,128)(2,1)S(1)} %collective-permute-done.other_ref), custom_call_target="tpu_custom_call" | custom-call | tf_op jit(solution)/shard_map/halve_images/pallas_call | solution.py:108
  11.8 7.9 %all-to-all-done.r_ref = bf16[8,64,256]{2,1,0:T(8,128)(2,1)S(1)} async-done(((bf16[8,64,256]{2,1,0:T(8,128)(2,1)}), bf16[8,64,256]{2,1,0:T(8,128)(2,1)S(1)}, u32[]{:S(2)}, u32[]{:S(2)}) %all-to-all-start) | async-done | bytes 262176 | tf_op jit(solution)/shard_map/all_to_all | solution.py:336
  19.7 2.8 %correlate.1 = bf16[8,2,128,128]{3,2,1,0:T(8,128)(2,1)} custom-call(bf16[2,16,128,128]{3,2,1,0:T(8,128)(2,1)S(1)} %halve_images.1.x_ref, bf16[8,64,256]{2,1,0:T(8,128)(2,1)S(1)} %all-to-all-done.r_ref), custom_call_target="tpu_custom_call" | custom-call | tf_op jit(solution)/shard_map/correlate/pallas_call | solution.py:167
  22.5 0.0 copy-start.1
  22.5 4.5 %all-to-all-start.1 = ((bf16[8,2,128,128]{3,2,1,0:T(8,128)(2,1)}), bf16[8,2,128,128]{3,2,1,0:T(8,128)(2,1)S(1)}, u32[]{:S(2)}, u32[]{:S(2)}) async-start(bf16[8,2,128,128]{3,2,1,0:T(8,128)(2,1)} %correlate.1), calls=%async_computation.1 | async-start | bytes 1048576 | tf_op jit(solution)/shard_map/all_to_all | solution.py:339
  27.1 0.0 copy-done.1
  27.1 0.1 collective-permute-start.1
  27.2 0.1 reshape.9.a_ref
  27.2 1.1 %collective-permute-done.1 = f32[64]{0:T(128)S(1)} collective-permute-done((f32[64]{0:T(128)S(1)}, f32[64]{0:T(128)S(1)}, u32[]{:S(2)}, u32[]{:S(2)}) %collective-permute-start.1) | collective-permute-done | bytes 288 | tf_op jit(solution)/shard_map/ppermute | solution.py:332
  28.3 0.1 reshape.10.b_ref
  28.4 7.1 %all-to-all-done.1.x_ref = bf16[8,2,128,128]{3,2,1,0:T(8,128)(2,1)S(1)} async-done(((bf16[8,2,128,128]{3,2,1,0:T(8,128)(2,1)}), bf16[8,2,128,128]{3,2,1,0:T(8,128)(2,1)S(1)}, u32[]{:S(2)}, u32[]{:S(2)}) %all-to-all-start.1) | async-done | bytes 524320 | tf_op jit(solution)/shard_map/all_to_all | solution.py:339
  35.4 0.4 local_softmax.1
  35.9 0.1 collective-permute-start.2
  35.9 1.2 %collective-permute-done.2.b_ref = f32[2,16,128]{2,1,0:T(8,128)S(1)} collective-permute-done((f32[2,16,128]{2,1,0:T(8,128)S(1)}, f32[2,16,128]{2,1,0:T(8,128)S(1)}, u32[]{:S(2)}, u32[]{:S(2)}) %collective-permute-start.2) | collective-permute-done | bytes 16416 | tf_op jit(solution)/shard_map/ppermute | solution.py:343
  37.1 0.1 normalize.1
  37.2 13.0 %all_to_all.20.w_ref = bf16[8,256,128]{2,1,0:T(8,128)(2,1)S(1)} all-to-all(bf16[8,256,128]{2,1,0:T(8,128)(2,1)S(1)} %normalize.1), channel_id=1, replica_groups=mesh['dh'=8,'core'=2,'blk'=8] {'blk'}, dimensions={0} | all-to-all | bytes 1048576 | tf_op jit(solution)/shard_map/all_to_all | solution.py:345
  50.3 3.9 %accumulate.1 = bf16[8,64,256]{2,1,0:T(8,128)(2,1)S(1)} custom-call(bf16[8,256,128]{2,1,0:T(8,128)(2,1)S(1)} %all_to_all.20.w_ref, bf16[2,16,128,128]{3,2,1,0:T(8,128)(2,1)S(1)} %halve_images.1.x_ref), custom_call_target="tpu_custom_call" | custom-call | tf_op jit(solution)/shard_map/accumulate/pallas_call | solution.py:292
  54.2 13.5 %all_to_all.21.x_ref = bf16[8,64,256]{2,1,0:T(8,128)(2,1)S(1)} all-to-all(bf16[8,64,256]{2,1,0:T(8,128)(2,1)S(1)} %accumulate.1), channel_id=1, replica_groups=mesh['dh'=8,'core'=2,'blk'=8] {'dh'}, dimensions={0} | all-to-all | bytes 524288 | tf_op jit(solution)/shard_map/all_to_all | solution.py:347
  67.7 0.7 add_up.1
Async XLA Ops:
  0.0 10.5 %collective-permute-start = (bf16[64,16,256]{2,1,0:T(8,128)(2,1)}, bf16[64,16,256]{2,1,0:T(8,128)(2,1)S(1)}, u32[]{:S(2)}, u32[]{:S(2)}) collective-permute-start(bf16[64,16,256]{2,1,0:T(8,128)(2,1)} %own_ref.1), channel_id=1, source_target_pairs={{0,8},{8,0},{1,9},{9,1},{2,10},{10,2},{3,11},{11,3},{4,12},{12,4},... | collective-permute-start | bytes 1572872 | tf_op jit(solution)/shard_map/ppermute | solution.py:331
  0.0 10.5 %copy-start = (bf16[64,16,256]{2,1,0:T(8,128)(2,1)S(1)}, bf16[64,16,256]{2,1,0:T(8,128)(2,1)}, u32[]{:S(2)}) copy-start(bf16[64,16,256]{2,1,0:T(8,128)(2,1)} %own_ref.1) | copy-start | bytes 1572868
  2.4 17.3 %all-to-all-start = ((bf16[8,64,256]{2,1,0:T(8,128)(2,1)}), bf16[8,64,256]{2,1,0:T(8,128)(2,1)S(1)}, u32[]{:S(2)}, u32[]{:S(2)}) async-start(bf16[8,64,256]{2,1,0:T(8,128)(2,1)} %pick_block.1), calls=%async_computation | async-start | bytes 524288 | tf_op jit(solution)/shard_map/all_to_all | solution.py:336
  22.5 4.5 %copy-start.1 = (f32[64]{0:T(128)S(1)}, f32[64]{0:T(128)}, u32[]{:S(2)}) copy-start(f32[64]{0:T(128)} %param.9) | copy-start | bytes 772
  22.5 12.9 %all-to-all-start.1 = ((bf16[8,2,128,128]{3,2,1,0:T(8,128)(2,1)}), bf16[8,2,128,128]{3,2,1,0:T(8,128)(2,1)S(1)}, u32[]{:S(2)}, u32[]{:S(2)}) async-start(bf16[8,2,128,128]{3,2,1,0:T(8,128)(2,1)} %correlate.1), calls=%async_computation.1 | async-start | bytes 1048576 | tf_op jit(solution)/shard_map/all_to_all | solution.py:339
  27.1 1.2 %collective-permute-start.1 = (f32[64]{0:T(128)S(1)}, f32[64]{0:T(128)S(1)}, u32[]{:S(2)}, u32[]{:S(2)}) collective-permute-start(f32[64]{0:T(128)S(1)} %copy-done.1), channel_id=1, source_target_pairs={{0,8},{8,0},{1,9},{9,1},{2,10},{10,2},{3,11},{11,3},{4,12},{12,4},... | collective-permute-start | bytes 776 | tf_op jit(solution)/shard_map/ppermute | solution.py:332
  35.9 1.2 %collective-permute-start.2 = (f32[2,16,128]{2,1,0:T(8,128)S(1)}, f32[2,16,128]{2,1,0:T(8,128)S(1)}, u32[]{:S(2)}, u32[]{:S(2)}) collective-permute-start(f32[2,16,128]{2,1,0:T(8,128)S(1)} %get-tuple-element.8.a_ref), channel_id=1, source_target_pairs={{0,8},{8,0},{1,9},{9,1},{2,10},{10,2},{3,11},{11,3},{4,12},{12,4},... | collective-permute-start | bytes 49160 | tf_op jit(solution)/shard_map/ppermute | solution.py:343

commit v4 on v3

--- a/solution.py
+++ b/solution.py
@@ -61,7 +61,7 @@
     return pltpu.roll(plus, t, 1), jnp.where(lane < t, -minus, minus)
 
 
-def pick_block(me, block_owner, class_gain, ref_store, copies):
+def pick_block(me, block_owner, class_gain, ref_store):
     nblk, kb, cycles, angles = ref_store.shape
 
     def body(me_ref, owner_ref, gain_ref, store_ref, out_ref, buf, sem):
@@ -75,12 +75,11 @@
             piece = (buf[i].astype(F32) * gain_ref[block * kb + i]).astype(BF).astype(F32)
             a, b = piece[:, :LANES], piece[:, LANES:]
             piece = jnp.concatenate([narrow_sum(a + b), narrow(a - b)], axis=1).astype(BF)
-            for c in range(copies):
-                out_ref[c, i * cycles : (i + 1) * cycles, :] = piece
-
-    return pl.pallas_call(
-        body,
-        out_shape=jax.ShapeDtypeStruct((copies, kb * cycles, angles), BF),
+            out_ref[i * cycles : (i + 1) * cycles, :] = piece
+
+    return pl.pallas_call(
+        body,
+        out_shape=VM((kb * cycles, angles), BF),
         in_specs=[spec(pltpu.SMEM), spec(pltpu.SMEM), spec(pltpu.SMEM), spec(pltpu.HBM)],
         out_specs=spec(),
         scratch_shapes=[VM((kb, cycles, angles), BF), pltpu.SemaphoreType.DMA],
@@ -132,12 +131,15 @@
     _, cycles, particles, _ = images.shape
     total = N1 * particles
     rows = total // nb
-    classes = refs.shape[0] * refs.shape[1] // cycles
+    near, far = refs[0].shape[:2]
+    classes = len(refs) * near * far // cycles
     cols = N2 * classes
     angles = 2 * LANES
 
-    def body(x_ref, r_ref, out_ref, scr, rr, x):
-        fill(scr, r_ref[...].astype(F32).reshape(classes * cycles, angles))
+    def body(x_ref, *args):
+        r_refs, (out_ref, scr, rr, x) = args[: len(refs)], args[len(refs) :]
+        blocks = [r_ref[d].astype(F32) for r_ref in r_refs for d in range(near)]
+        fill(scr, jnp.concatenate(blocks, axis=0))
         square = jnp.zeros((classes, LANES), F32)
         for r in range(cycles):
             plus, minus = take_cycle(scr, r, classes, cycles)
@@ -167,7 +169,7 @@
     return pl.pallas_call(
         body,
         out_shape=jax.ShapeDtypeStruct((nb, cols // LANES, 2 * rows, LANES), BF),
-        in_specs=[spec(), spec()],
+        in_specs=[spec()] * (1 + len(refs)),
         out_specs=spec(),
         scratch_shapes=[
             VM((2, classes * cycles, LANES), F32),
@@ -176,7 +178,7 @@
         ],
         compiler_params=params(),
         name="correlate",
-    )(here(images), here(refs))
+    )(here(images), *[here(r) for r in refs])
 
 
 def local_softmax(me, scores, precision, others):
@@ -253,13 +255,14 @@
     )(here(e), here(mine), here(theirs))
 
 
-def accumulate(weights, images, owners, step):
+def accumulate(me, weights, images, ny, nz, step):
+    owners = ny * nz
     nb, cols, lanes = weights.shape
     cycles = images.shape[1]
     classes = cols // N2
     pair = 2 * LANES
 
-    def body(w_ref, x_ref, out_ref, scr):
+    def body(me_ref, w_ref, x_ref, out_ref, scr):
         left = lax.broadcasted_iota(jnp.int32, (cols, lanes), 1) < lanes // 2
         near, far = [], []
         for j in range(0, nb, 2):
@@ -287,17 +290,22 @@
                 scr.at[0][rows, :] = 0.5 * (plus + minus)
                 scr.at[1][rows, :] = 0.5 * (plus - minus)
         whole = jnp.concatenate([scr[0], scr[1]], axis=1)
-        out_ref[...] = whole.reshape(out_ref.shape).astype(BF)
+        whole = whole.reshape(out_ref.shape).astype(BF)
+        place = me_ref[0] // 2
+        y, z = place // nz, place % nz
+        for slot in range(owners):
+            dz, dy = slot // ny, slot % ny
+            out_ref[(y + dy) % ny * nz + (z + nz - dz) % nz] = whole[slot]
 
     return pl.pallas_call(
         body,
         out_shape=VM((owners, classes // owners * cycles, pair), BF),
-        in_specs=[spec(), spec()],
+        in_specs=[spec(pltpu.SMEM), spec(), spec()],
         out_specs=spec(),
         scratch_shapes=[VM((2, classes * cycles, LANES), F32)],
         compiler_params=params(),
         name="accumulate",
-    )(here(weights), here(images))
+    )(me, here(weights), here(images))
 
 
 def add_up(parts):
@@ -319,8 +327,8 @@
 
 def solution(mesh):
     dom, nb = mesh.devices.shape
-    nd = dom // 2
-    view = Mesh(mesh.devices.reshape(nd, 2, nb), ("dh", "core", "blk"))
+    ny, nz = 2, dom // 4
+    view = Mesh(mesh.devices.reshape(ny, nz, 2, nb), ("yh", "z", "core", "blk"))
     swap = [(0, 1), (1, 0)]
 
     def shards(images, ref_store, block_owner, class_gain, precision):
@@ -330,10 +338,14 @@
         half = particles // nb
         other = lax.ppermute(images, "core", swap)
         other_precision = lax.ppermute(precision, "core", swap)
-        me = (lax.axis_index("dh") * 2 + lax.axis_index("core"))[None].astype(jnp.int32)
+        y, z = lax.axis_index("yh"), lax.axis_index("z")
+        me = ((y * nz + z) * 2 + lax.axis_index("core"))[None].astype(jnp.int32)
         j = lax.axis_index("blk")[None].astype(jnp.int32)
-        mine = pick_block(me, block_owner, class_gain, ref_store[0], nd)
-        refs = lax.all_to_all(mine, "dh", 0, 0)
+        mine = pick_block(me, block_owner, class_gain, ref_store[0])
+        refs = [jnp.stack([mine, lax.ppermute(mine, "yh", swap)])]
+        for d in range(1, nz):
+            ring = [(i, (i + d) % nz) for i in range(nz)]
+            refs.append(lax.ppermute(refs[0], "z", ring))
         halves = halve_images(images, other, nb)
         scores = correlate(halves, refs, nb, rot)
         scores = lax.all_to_all(scores, "blk", 0, 0)
@@ -343,11 +355,11 @@
         theirs = lax.ppermute(stats, "core", swap)
         weights = normalize(e, stats, theirs, nb)
         weights = lax.all_to_all(weights, "blk", 0, 0)
-        totals = accumulate(weights, halves, nd, rot)
-        totals = lax.all_to_all(totals, "dh", 0, 0)
+        totals = accumulate(me, weights, halves, ny, nz, rot)
+        totals = lax.all_to_all(totals, ("yh", "z"), 0, 0)
         return add_up(totals).reshape(1, 1, kb, cycles, angles)
 
-    dom_axes = ("dh", "core")
+    dom_axes = ("yh", "z", "core")
     return jax.shard_map(
         shards,
         mesh=view,

time: 68.8 us -> 67.8 us (0.985)
  waiting for transfers between devices: 17.2 us -> 13.1 us
  starting transfers between devices: 12.8 us -> 15.7 us
  blocking collectives: 26.5 us -> 27.6 us
  Pallas kernels: 11.6 us -> 10.9 us
    ppermute x0 -> x4, starting transfers between devices: none -> 10.1 us  [the longest x3 6.69 us: shards(): refs.append(lax.ppermute(refs[0], 'z', ring))]
    all_to_all x1 -> x0, starting transfers between devices: 8.07 us -> none  [shards(): refs = lax.all_to_all(mine, 'dh', 0, 0)]
    all_to_all x1 -> x0, waiting for transfers between devices: 7.92 us -> none  [shards(): refs = lax.all_to_all(mine, 'dh', 0, 0)]
    ppermute x0 -> x4, waiting for transfers between devices: none -> 4.03 us  [the longest x1 2.11 us: shards(): refs = [jnp.stack([mine, lax.ppermute(mine, 'yh', swap)])]]
    all_to_all x1, blocking collectives: 13.5 us -> 14.5 us  [shards(): totals = lax.all_to_all(totals, ('yh', 'z'), 0, 0)]
    all_to_all x1, starting transfers between devices: 4.54 us -> 5.44 us  [shards(): scores = lax.all_to_all(scores, 'blk', 0, 0)]
    pallas_call x1, Pallas kernels: 2.39 us -> 1.68 us  [pick_block(): pl.pallas_call(body, out_shape=VM((kb * cycles, angles), BF), in_specs=[s...]
  transfers between devices with their start and end apart: 5 -> 8, of which waited for: 4 -> 6; matrix products, arithmetic and copies ran while one was open for 0% -> 0% of each run, Pallas kernels for 5% -> 4%
where the time goes in v4:
time: 67.8 us; the launch traced here: 67.5 us
  blocking collectives  27.6 us (41%)
  starting transfers between devices  15.7 us (23%)
  waiting for transfers between devices  13.1 us (19%)
  Pallas kernels  10.9 us (16%)
    all_to_all x1, blocking collectives, shards(): totals = lax.all_to_all(totals, ('yh', 'z'), 0, 0)  14.5 us
    all_to_all x1, blocking collectives, shards(): weights = lax.all_to_all(weights, 'blk', 0, 0)  13.1 us
    all_to_all x1, waiting for transfers between devices, shards(): scores = lax.all_to_all(scores, 'blk', 0, 0)  6.85 us
    ppermute x3, starting transfers between devices, shards(): refs.append(lax.ppermute(refs[0], 'z', ring))  6.69 us
    all_to_all x1, starting transfers between devices, shards(): scores = lax.all_to_all(scores, 'blk', 0, 0)  5.44 us
    pallas_call x1, Pallas kernels, accumulate(): pl.pallas_call(body, out_shape=VM((owners, classes // owners * cycles, pa...  3.9 us
    ppermute x1, starting transfers between devices, shards(): refs = [jnp.stack([mine, lax.ppermute(mine, 'yh', swap)])]  3.39 us
    pallas_call x1, Pallas kernels, correlate(): pl.pallas_call(body, out_shape=jax.ShapeDtypeStruct((nb, cols // LANES, 2...  2.76 us
  transfers between devices with their start and end apart: 8, of which 6 were waited for; matrix products, arithmetic and copies ran while one was open for 0% of the time, Pallas kernels for 4%

profile of v4, /device:TPU:0, one launch (start us, length us, event | category | flops | bytes accessed | tf_op | source)
XLA Modules:
  0.0 67.5 jit_solution(15666102440484712263)
XLA Ops:
  0.0 0.0 copy-start
  0.0 0.0 collective-permute-start
  0.0 1.7 %pick_block.1 = bf16[64,256]{1,0:T(8,128)(2,1)S(1)} custom-call(s32[1]{0:T(128)} %bitcast.me_ref, s32[16]{0:T(128)} %owner_ref.1, f32[64]{0:T(128)} %gain_ref.1, bf16[16,4,16,256]{3,2,1,0:T(8,128)(2,1)} %bitcast.7), custom_call_target="tpu_custom_call" | custom-call | tf_op jit(solution)/shard_map/pick_block/pallas_call | solution.py:80
  1.7 3.4 %collective-permute-start.1 = (bf16[64,256]{1,0:T(8,128)(2,1)S(1)}, bf16[64,256]{1,0:T(8,128)(2,1)S(1)}, u32[]{:S(2)}, u32[]{:S(2)}) collective-permute-start(bf16[64,256]{1,0:T(8,128)(2,1)S(1)} %pick_block.1), channel_id=1, source_target_pairs={{0,64},{64,0},{1,65},{65,1},{2,66},{66,2},{3,67},{67,3},{4,68},{68... | collective-permute-start | bytes 98312 | tf_op jit(solution)/shard_map/ppermute | solution.py:345
  5.1 2.1 %collective-permute-done.1 = bf16[64,256]{1,0:T(8,128)(2,1)S(1)} collective-permute-done((bf16[64,256]{1,0:T(8,128)(2,1)S(1)}, bf16[64,256]{1,0:T(8,128)(2,1)S(1)}, u32[]{:S(2)}, u32[]{:S(2)}) %collective-permute-start.1) | collective-permute-done | bytes 32800 | tf_op jit(solution)/shard_map/ppermute | solution.py:345
  7.2 2.1 %collective-permute-start.2 = (bf16[2,64,256]{2,1,0:T(8,128)(2,1)S(1)}, bf16[2,64,256]{2,1,0:T(8,128)(2,1)S(1)}, u32[]{:S(2)}, u32[]{:S(2)}) collective-permute-start(bf16[2,64,256]{2,1,0:T(8,128)(2,1)S(1)} %pad_maximum_fusion.args_0_), channel_id=1, source_target_pairs={{0,16},{16,32},{32,48},{48,0},{1,17},{17,33},{33,49},{49,1},{2,18}... | collective-permute-start | bytes 196616 | tf_op jit(solution)/shard_map/ppermute | solution.py:348
  9.3 3.6 %collective-permute-start.3 = (bf16[2,64,256]{2,1,0:T(8,128)(2,1)S(1)}, bf16[2,64,256]{2,1,0:T(8,128)(2,1)S(1)}, u32[]{:S(2)}, u32[]{:S(2)}) collective-permute-start(bf16[2,64,256]{2,1,0:T(8,128)(2,1)S(1)} %pad_maximum_fusion.args_0_), channel_id=1, source_target_pairs={{0,32},{16,48},{32,0},{48,16},{1,33},{17,49},{33,1},{49,17},{2,34}... | collective-permute-start | bytes 196616 | tf_op jit(solution)/shard_map/ppermute | solution.py:348
  12.9 1.0 %collective-permute-start.4 = (bf16[2,64,256]{2,1,0:T(8,128)(2,1)S(1)}, bf16[2,64,256]{2,1,0:T(8,128)(2,1)S(1)}, u32[]{:S(2)}, u32[]{:S(2)}) collective-permute-start(bf16[2,64,256]{2,1,0:T(8,128)(2,1)S(1)} %pad_maximum_fusion.args_0_), channel_id=1, source_target_pairs={{0,48},{16,0},{32,16},{48,32},{1,49},{17,1},{33,17},{49,33},{2,50}... | collective-permute-start | bytes 196616 | tf_op jit(solution)/shard_map/ppermute | solution.py:348
  13.9 0.0 collective-permute-done.other_ref
  13.9 0.0 copy-done
  13.9 1.3 %halve_images.1.x_ref = bf16[2,16,128,128]{3,2,1,0:T(8,128)(2,1)S(1)} custom-call(bf16[64,16,256]{2,1,0:T(8,128)(2,1)S(1)} %copy-done, bf16[64,16,256]{2,1,0:T(8,128)(2,1)S(1)} %collective-permute-done.other_ref), custom_call_target="tpu_custom_call" | custom-call | tf_op jit(solution)/shard_map/halve_images/pallas_call | solution.py:107
  15.2 0.0 collective-permute-done.2.args_1_
  15.2 0.6 collective-permute-done.3.args_2_
  15.8 1.3 %collective-permute-done.4.args_3_ = bf16[2,64,256]{2,1,0:T(8,128)(2,1)S(1)} collective-permute-done((bf16[2,64,256]{2,1,0:T(8,128)(2,1)S(1)}, bf16[2,64,256]{2,1,0:T(8,128)(2,1)S(1)}, u32[]{:S(2)}, u32[]{:S(2)}) %collective-permute-start.4) | collective-permute-done | bytes 65568 | tf_op jit(solution)/shard_map/ppermute | solution.py:348
  17.2 2.8 %correlate.1 = bf16[8,2,128,128]{3,2,1,0:T(8,128)(2,1)} custom-call(bf16[2,16,128,128]{3,2,1,0:T(8,128)(2,1)S(1)} %halve_images.1.x_ref, bf16[2,64,256]{2,1,0:T(8,128)(2,1)S(1)} %pad_maximum_fusion.args_0_, bf16[2,64,256]{2,1,0:T(8,128)(2,1)S(1)} %collective-permute-done.2.args_1_, bf16[2,64,256]{2,1,0:T(8,128)(2,1)S(1)} %collective-permute-done.3.args_2_, ...), custom_call_target="tpu_custom_call" | custom-call | tf_op jit(solution)/shard_map/correlate/pallas_call | solution.py:169
  19.9 0.0 copy-start.1
  19.9 5.4 %all-to-all-start = ((bf16[8,2,128,128]{3,2,1,0:T(8,128)(2,1)}), bf16[8,2,128,128]{3,2,1,0:T(8,128)(2,1)S(1)}, u32[]{:S(2)}, u32[]{:S(2)}) async-start(bf16[8,2,128,128]{3,2,1,0:T(8,128)(2,1)} %correlate.1), calls=%async_computation | async-start | bytes 1048576 | tf_op jit(solution)/shard_map/all_to_all | solution.py:351
  25.4 0.0 copy-done.1
  25.4 0.1 collective-permute-start.5
  25.5 0.1 reshape.9.a_ref
  25.5 1.1 %collective-permute-done.5 = f32[64]{0:T(128)S(1)} collective-permute-done((f32[64]{0:T(128)S(1)}, f32[64]{0:T(128)S(1)}, u32[]{:S(2)}, u32[]{:S(2)}) %collective-permute-start.5) | collective-permute-done | bytes 288 | tf_op jit(solution)/shard_map/ppermute | solution.py:340
  26.6 0.1 reshape.10.b_ref
  26.7 6.9 %all-to-all-done.x_ref = bf16[8,2,128,128]{3,2,1,0:T(8,128)(2,1)S(1)} async-done(((bf16[8,2,128,128]{3,2,1,0:T(8,128)(2,1)}), bf16[8,2,128,128]{3,2,1,0:T(8,128)(2,1)S(1)}, u32[]{:S(2)}, u32[]{:S(2)}) %all-to-all-start) | async-done | bytes 524320 | tf_op jit(solution)/shard_map/all_to_all | solution.py:351
  33.5 0.4 local_softmax.1
  33.9 0.1 collective-permute-start.6
  34.0 1.2 %collective-permute-done.6.b_ref = f32[2,16,128]{2,1,0:T(8,128)S(1)} collective-permute-done((f32[2,16,128]{2,1,0:T(8,128)S(1)}, f32[2,16,128]{2,1,0:T(8,128)S(1)}, u32[]{:S(2)}, u32[]{:S(2)}) %collective-permute-start.6) | collective-permute-done | bytes 16416 | tf_op jit(solution)/shard_map/ppermute | solution.py:355
  35.2 0.1 normalize.1
  35.3 13.1 %all_to_all.15.w_ref = bf16[8,256,128]{2,1,0:T(8,128)(2,1)S(1)} all-to-all(bf16[8,256,128]{2,1,0:T(8,128)(2,1)S(1)} %normalize.1), channel_id=1, replica_groups=mesh['yh'=2,'z'=4,'core'=2,'blk'=8] {'blk'}, dimensions={0} | all-to-all | bytes 1048576 | tf_op jit(solution)/shard_map/all_to_all | solution.py:357
  48.4 3.9 %accumulate.1 = bf16[8,64,256]{2,1,0:T(8,128)(2,1)S(1)} custom-call(s32[1]{0:T(128)} %bitcast.me_ref, bf16[8,256,128]{2,1,0:T(8,128)(2,1)S(1)} %all_to_all.15.w_ref, bf16[2,16,128,128]{3,2,1,0:T(8,128)(2,1)S(1)} %halve_images.1.x_ref), custom_call_target="tpu_custom_call" | custom-call | tf_op jit(solution)/shard_map/accumulate/pallas_call | solution.py:300
  52.3 14.5 %all_to_all.16.x_ref = bf16[8,64,256]{2,1,0:T(8,128)(2,1)S(1)} all-to-all(bf16[8,64,256]{2,1,0:T(8,128)(2,1)S(1)} %accumulate.1), channel_id=1, replica_groups=mesh['yh'=2,'z'=4,'core'=2,'blk'=8] {'yh','z'}, dimensions={0} | all-to-all | bytes 524288 | tf_op jit(solution)/shard_map/all_to_all | solution.py:359
  66.8 0.7 add_up.1
  (1 shorter events, 0.0 us)
Async XLA Ops:
  0.0 13.9 %copy-start = (bf16[64,16,256]{2,1,0:T(8,128)(2,1)S(1)}, bf16[64,16,256]{2,1,0:T(8,128)(2,1)}, u32[]{:S(2)}) copy-start(bf16[64,16,256]{2,1,0:T(8,128)(2,1)} %own_ref.1) | copy-start | bytes 1572868
  0.0 13.9 %collective-permute-start = (bf16[64,16,256]{2,1,0:T(8,128)(2,1)}, bf16[64,16,256]{2,1,0:T(8,128)(2,1)S(1)}, u32[]{:S(2)}, u32[]{:S(2)}) collective-permute-start(bf16[64,16,256]{2,1,0:T(8,128)(2,1)} %own_ref.1), channel_id=1, source_target_pairs={{0,8},{8,0},{1,9},{9,1},{2,10},{10,2},{3,11},{11,3},{4,12},{12,4},... | collective-permute-start | bytes 1572872 | tf_op jit(solution)/shard_map/ppermute | solution.py:339
  1.7 5.5 %collective-permute-start.1 = (bf16[64,256]{1,0:T(8,128)(2,1)S(1)}, bf16[64,256]{1,0:T(8,128)(2,1)S(1)}, u32[]{:S(2)}, u32[]{:S(2)}) collective-permute-start(bf16[64,256]{1,0:T(8,128)(2,1)S(1)} %pick_block.1), channel_id=1, source_target_pairs={{0,64},{64,0},{1,65},{65,1},{2,66},{66,2},{3,67},{67,3},{4,68},{68... | collective-permute-start | bytes 98312 | tf_op jit(solution)/shard_map/ppermute | solution.py:345
  7.2 8.0 %collective-permute-start.2 = (bf16[2,64,256]{2,1,0:T(8,128)(2,1)S(1)}, bf16[2,64,256]{2,1,0:T(8,128)(2,1)S(1)}, u32[]{:S(2)}, u32[]{:S(2)}) collective-permute-start(bf16[2,64,256]{2,1,0:T(8,128)(2,1)S(1)} %pad_maximum_fusion.args_0_), channel_id=1, source_target_pairs={{0,16},{16,32},{32,48},{48,0},{1,17},{17,33},{33,49},{49,1},{2,18}... | collective-permute-start | bytes 196616 | tf_op jit(solution)/shard_map/ppermute | solution.py:348
  9.3 6.5 %collective-permute-start.3 = (bf16[2,64,256]{2,1,0:T(8,128)(2,1)S(1)}, bf16[2,64,256]{2,1,0:T(8,128)(2,1)S(1)}, u32[]{:S(2)}, u32[]{:S(2)}) collective-permute-start(bf16[2,64,256]{2,1,0:T(8,128)(2,1)S(1)} %pad_maximum_fusion.args_0_), channel_id=1, source_target_pairs={{0,32},{16,48},{32,0},{48,16},{1,33},{17,49},{33,1},{49,17},{2,34}... | collective-permute-start | bytes 196616 | tf_op jit(solution)/shard_map/ppermute | solution.py:348
  12.9 4.3 %collective-permute-start.4 = (bf16[2,64,256]{2,1,0:T(8,128)(2,1)S(1)}, bf16[2,64,256]{2,1,0:T(8,128)(2,1)S(1)}, u32[]{:S(2)}, u32[]{:S(2)}) collective-permute-start(bf16[2,64,256]{2,1,0:T(8,128)(2,1)S(1)} %pad_maximum_fusion.args_0_), channel_id=1, source_target_pairs={{0,48},{16,0},{32,16},{48,32},{1,49},{17,1},{33,17},{49,33},{2,50}... | collective-permute-start | bytes 196616 | tf_op jit(solution)/shard_map/ppermute | solution.py:348
  19.9 5.4 %copy-start.1 = (f32[64]{0:T(128)S(1)}, f32[64]{0:T(128)}, u32[]{:S(2)}) copy-start(f32[64]{0:T(128)} %param.9) | copy-start | bytes 772
  19.9 13.6 %all-to-all-start = ((bf16[8,2,128,128]{3,2,1,0:T(8,128)(2,1)}), bf16[8,2,128,128]{3,2,1,0:T(8,128)(2,1)S(1)}, u32[]{:S(2)}, u32[]{:S(2)}) async-start(bf16[8,2,128,128]{3,2,1,0:T(8,128)(2,1)} %correlate.1), calls=%async_computation | async-start | bytes 1048576 | tf_op jit(solution)/shard_map/all_to_all | solution.py:351
  25.4 1.2 %collective-permute-start.5 = (f32[64]{0:T(128)S(1)}, f32[64]{0:T(128)S(1)}, u32[]{:S(2)}, u32[]{:S(2)}) collective-permute-start(f32[64]{0:T(128)S(1)} %copy-done.1), channel_id=1, source_target_pairs={{0,8},{8,0},{1,9},{9,1},{2,10},{10,2},{3,11},{11,3},{4,12},{12,4},... | collective-permute-start | bytes 776 | tf_op jit(solution)/shard_map/ppermute | solution.py:340
  33.9 1.2 %collective-permute-start.6 = (f32[2,16,128]{2,1,0:T(8,128)S(1)}, f32[2,16,128]{2,1,0:T(8,128)S(1)}, u32[]{:S(2)}, u32[]{:S(2)}) collective-permute-start(f32[2,16,128]{2,1,0:T(8,128)S(1)} %get-tuple-element.8.a_ref), channel_id=1, source_target_pairs={{0,8},{8,0},{1,9},{9,1},{2,10},{10,2},{3,11},{11,3},{4,12},{12,4},... | collective-permute-start | bytes 49160 | tf_op jit(solution)/shard_map/ppermute | solution.py:355

commit v5 on v4

--- a/solution.py
+++ b/solution.py
@@ -113,6 +113,21 @@
         compiler_params=params(),
         name="halve_images",
     )(own, here(other))
+
+
+def pair_up(mine, theirs, halves):
+    def body(a_ref, b_ref, _, out_ref):
+        out_ref[0] = a_ref[...]
+        out_ref[1] = b_ref[...]
+
+    return pl.pallas_call(
+        body,
+        out_shape=VM((2,) + mine.shape, BF),
+        in_specs=[spec()] * 3,
+        out_specs=spec(),
+        compiler_params=params(),
+        name="pair_up",
+    )(here(mine), here(theirs), here(halves))
 
 
 def rotate_images(x_ref, r, nb, step):
@@ -262,7 +277,9 @@
     classes = cols // N2
     pair = 2 * LANES
 
-    def body(me_ref, w_ref, x_ref, out_ref, scr):
+    def body(me_ref, w_ref, x_ref, out_ref, scr, x):
+        for r in range(cycles):
+            x[0, r], x[1, r] = rotate_images(x_ref, r, nb, step)
         left = lax.broadcasted_iota(jnp.int32, (cols, lanes), 1) < lanes // 2
         near, far = [], []
         for j in range(0, nb, 2):
@@ -271,10 +288,9 @@
             far.append(jnp.where(left, pltpu.roll(a, lanes // 2, 1), b))
         w = [jnp.concatenate(v, axis=1) for v in (near, far)]
         for c in range(0, cycles, 2):
-            turned = [rotate_images(x_ref, c + d, nb, step) for d in range(2)]
             spread = []
             for i in range(2):
-                both = jnp.concatenate([turned[0][i], turned[1][i]], axis=1)
+                both = jnp.concatenate([x[i, c], x[i, c + 1]], axis=1)
                 spread.append(jnp.dot(w[i], both, preferred_element_type=F32))
             for d in range(2):
                 plus = minus = None
@@ -302,7 +318,10 @@
         out_shape=VM((owners, classes // owners * cycles, pair), BF),
         in_specs=[spec(pltpu.SMEM), spec(), spec()],
         out_specs=spec(),
-        scratch_shapes=[VM((2, classes * cycles, LANES), F32)],
+        scratch_shapes=[
+            VM((2, classes * cycles, LANES), F32),
+            VM((2, cycles, N1 * images.shape[2], LANES), BF),
+        ],
         compiler_params=params(),
         name="accumulate",
     )(me, here(weights), here(images))
@@ -342,11 +361,12 @@
         me = ((y * nz + z) * 2 + lax.axis_index("core"))[None].astype(jnp.int32)
         j = lax.axis_index("blk")[None].astype(jnp.int32)
         mine = pick_block(me, block_owner, class_gain, ref_store[0])
-        refs = [jnp.stack([mine, lax.ppermute(mine, "yh", swap)])]
+        theirs = lax.ppermute(mine, "yh", swap)
+        halves = halve_images(images, other, nb)
+        refs = [pair_up(mine, theirs, halves)]
         for d in range(1, nz):
             ring = [(i, (i + d) % nz) for i in range(nz)]
             refs.append(lax.ppermute(refs[0], "z", ring))
-        halves = halve_images(images, other, nb)
         scores = correlate(halves, refs, nb, rot)
         scores = lax.all_to_all(scores, "blk", 0, 0)
         e, stats = local_softmax(

time: 67.8 us -> 66.1 us (0.975)
  Pallas kernels: 10.9 us -> 9.32 us
    pallas_call x1, Pallas kernels: 3.9 us -> 2.34 us  [accumulate(): pl.pallas_call(body, out_shape=VM((owners, classes // owners * cycles, pa...]
    ppermute x3, waiting for transfers between devices: 1.91 us -> 3.26 us  [shards(): refs.append(lax.ppermute(refs[0], 'z', ring))]
    ppermute x1, waiting for transfers between devices: 2.11 us -> 0.78 us  [shards(): theirs = lax.ppermute(mine, 'yh', swap)]
  transfers between devices with their start and end apart: 8 -> 8, of which waited for: 6 -> 7; matrix products, arithmetic and copies ran while one was open for 0% -> 0% of each run, Pallas kernels for 4% -> 5%
where the time goes in v5:
time: 66.1 us; the launch traced here: 65.8 us
  blocking collectives  27.6 us (42%)
  starting transfers between devices  15.6 us (24%)
  waiting for transfers between devices  13.1 us (20%)
  Pallas kernels  9.32 us (14%)
    all_to_all x1, blocking collectives, shards(): totals = lax.all_to_all(totals, ('yh', 'z'), 0, 0)  14.4 us
    all_to_all x1, blocking collectives, shards(): weights = lax.all_to_all(weights, 'blk', 0, 0)  13.1 us
    all_to_all x1, waiting for transfers between devices, shards(): scores = lax.all_to_all(scores, 'blk', 0, 0)  6.85 us
    ppermute x3, starting transfers between devices, shards(): refs.append(lax.ppermute(refs[0], 'z', ring))  6.62 us
    all_to_all x1, starting transfers between devices, shards(): scores = lax.all_to_all(scores, 'blk', 0, 0)  5.44 us
    ppermute x1, starting transfers between devices, shards(): theirs = lax.ppermute(mine, 'yh', swap)  3.39 us
    ppermute x3, waiting for transfers between devices, shards(): refs.append(lax.ppermute(refs[0], 'z', ring))  3.26 us
    pallas_call x1, Pallas kernels, correlate(): pl.pallas_call(body, out_shape=jax.ShapeDtypeStruct((nb, cols // LANES, 2...  2.76 us
  transfers between devices with their start and end apart: 8, of which 7 were waited for; matrix products, arithmetic and copies ran while one was open for 0% of the time, Pallas kernels for 5%

profile of v5, /device:TPU:0, one launch (start us, length us, event | category | flops | bytes accessed | tf_op | source)
XLA Modules:
  0.0 65.8 jit_solution(17055841332171863145)
XLA Ops:
  0.0 0.0 copy-start
  0.0 0.0 collective-permute-start
  0.0 1.7 %pick_block.1.a_ref = bf16[64,256]{1,0:T(8,128)(2,1)S(1)} custom-call(s32[1]{0:T(128)} %bitcast.me_ref, s32[16]{0:T(128)} %owner_ref.1, f32[64]{0:T(128)} %gain_ref.1, bf16[16,4,16,256]{3,2,1,0:T(8,128)(2,1)} %bitcast.4), custom_call_target="tpu_custom_call" | custom-call | tf_op jit(solution)/shard_map/pick_block/pallas_call | solution.py:80
  1.7 3.4 %collective-permute-start.1 = (bf16[64,256]{1,0:T(8,128)(2,1)S(1)}, bf16[64,256]{1,0:T(8,128)(2,1)S(1)}, u32[]{:S(2)}, u32[]{:S(2)}) collective-permute-start(bf16[64,256]{1,0:T(8,128)(2,1)S(1)} %pick_block.1.a_ref), channel_id=1, source_target_pairs={{0,64},{64,0},{1,65},{65,1},{2,66},{66,2},{3,67},{67,3},{4,68},{68... | collective-permute-start | bytes 98312 | tf_op jit(solution)/shard_map/ppermute | solution.py:364
  5.1 0.0 collective-permute-done.other_ref
  5.1 0.0 copy-done
  5.1 1.3 %halve_images.1._.x_ref = bf16[2,16,128,128]{3,2,1,0:T(8,128)(2,1)S(1)} custom-call(bf16[64,16,256]{2,1,0:T(8,128)(2,1)S(1)} %copy-done, bf16[64,16,256]{2,1,0:T(8,128)(2,1)S(1)} %collective-permute-done.other_ref), custom_call_target="tpu_custom_call" | custom-call | tf_op jit(solution)/shard_map/halve_images/pallas_call | solution.py:107
  6.4 0.8 %collective-permute-done.1.b_ref = bf16[64,256]{1,0:T(8,128)(2,1)S(1)} collective-permute-done((bf16[64,256]{1,0:T(8,128)(2,1)S(1)}, bf16[64,256]{1,0:T(8,128)(2,1)S(1)}, u32[]{:S(2)}, u32[]{:S(2)}) %collective-permute-start.1) | collective-permute-done | bytes 32800 | tf_op jit(solution)/shard_map/ppermute | solution.py:364
  7.2 2.0 %collective-permute-start.2 = (bf16[2,64,256]{2,1,0:T(8,128)(2,1)S(1)}, bf16[2,64,256]{2,1,0:T(8,128)(2,1)S(1)}, u32[]{:S(2)}, u32[]{:S(2)}) collective-permute-start(bf16[2,64,256]{2,1,0:T(8,128)(2,1)S(1)} %pair_up.1.args_0_), channel_id=1, source_target_pairs={{0,16},{16,32},{32,48},{48,0},{1,17},{17,33},{33,49},{49,1},{2,18}... | collective-permute-start | bytes 196616 | tf_op jit(solution)/shard_map/ppermute | solution.py:369
  9.2 3.6 %collective-permute-start.3 = (bf16[2,64,256]{2,1,0:T(8,128)(2,1)S(1)}, bf16[2,64,256]{2,1,0:T(8,128)(2,1)S(1)}, u32[]{:S(2)}, u32[]{:S(2)}) collective-permute-start(bf16[2,64,256]{2,1,0:T(8,128)(2,1)S(1)} %pair_up.1.args_0_), channel_id=1, source_target_pairs={{0,32},{16,48},{32,0},{48,16},{1,33},{17,49},{33,1},{49,17},{2,34}... | collective-permute-start | bytes 196616 | tf_op jit(solution)/shard_map/ppermute | solution.py:369
  12.8 1.0 %collective-permute-start.4 = (bf16[2,64,256]{2,1,0:T(8,128)(2,1)S(1)}, bf16[2,64,256]{2,1,0:T(8,128)(2,1)S(1)}, u32[]{:S(2)}, u32[]{:S(2)}) collective-permute-start(bf16[2,64,256]{2,1,0:T(8,128)(2,1)S(1)} %pair_up.1.args_0_), channel_id=1, source_target_pairs={{0,48},{16,0},{32,16},{48,32},{1,49},{17,1},{33,17},{49,33},{2,50}... | collective-permute-start | bytes 196616 | tf_op jit(solution)/shard_map/ppermute | solution.py:369
  13.8 0.5 collective-permute-done.2.args_1_
  14.3 1.5 %collective-permute-done.3.args_2_ = bf16[2,64,256]{2,1,0:T(8,128)(2,1)S(1)} collective-permute-done((bf16[2,64,256]{2,1,0:T(8,128)(2,1)S(1)}, bf16[2,64,256]{2,1,0:T(8,128)(2,1)S(1)}, u32[]{:S(2)}, u32[]{:S(2)}) %collective-permute-start.3) | collective-permute-done | bytes 65568 | tf_op jit(solution)/shard_map/ppermute | solution.py:369
  15.8 1.3 %collective-permute-done.4.args_3_ = bf16[2,64,256]{2,1,0:T(8,128)(2,1)S(1)} collective-permute-done((bf16[2,64,256]{2,1,0:T(8,128)(2,1)S(1)}, bf16[2,64,256]{2,1,0:T(8,128)(2,1)S(1)}, u32[]{:S(2)}, u32[]{:S(2)}) %collective-permute-start.4) | collective-permute-done | bytes 65568 | tf_op jit(solution)/shard_map/ppermute | solution.py:369
  17.1 2.8 %correlate.1 = bf16[8,2,128,128]{3,2,1,0:T(8,128)(2,1)} custom-call(bf16[2,16,128,128]{3,2,1,0:T(8,128)(2,1)S(1)} %halve_images.1._.x_ref, bf16[2,64,256]{2,1,0:T(8,128)(2,1)S(1)} %pair_up.1.args_0_, bf16[2,64,256]{2,1,0:T(8,128)(2,1)S(1)} %collective-permute-done.2.args_1_, bf16[2,64,256]{2,1,0:T(8,128)(2,1)S(1)} %collective-permute-done.3.args_2_, ...), custom_call_target="tpu_custom_call" | custom-call | tf_op jit(solution)/shard_map/correlate/pallas_call | solution.py:184
  19.8 0.0 copy-start.1
  19.8 5.4 %all-to-all-start = ((bf16[8,2,128,128]{3,2,1,0:T(8,128)(2,1)}), bf16[8,2,128,128]{3,2,1,0:T(8,128)(2,1)S(1)}, u32[]{:S(2)}, u32[]{:S(2)}) async-start(bf16[8,2,128,128]{3,2,1,0:T(8,128)(2,1)} %correlate.1), calls=%async_computation | async-start | bytes 1048576 | tf_op jit(solution)/shard_map/all_to_all | solution.py:371
  25.3 0.0 copy-done.1
  25.3 0.1 collective-permute-start.5
  25.4 0.1 reshape.9.a_ref
  25.5 1.1 %collective-permute-done.5 = f32[64]{0:T(128)S(1)} collective-permute-done((f32[64]{0:T(128)S(1)}, f32[64]{0:T(128)S(1)}, u32[]{:S(2)}, u32[]{:S(2)}) %collective-permute-start.5) | collective-permute-done | bytes 288 | tf_op jit(solution)/shard_map/ppermute | solution.py:359
  26.5 0.1 reshape.10.b_ref
  26.6 6.9 %all-to-all-done.x_ref = bf16[8,2,128,128]{3,2,1,0:T(8,128)(2,1)S(1)} async-done(((bf16[8,2,128,128]{3,2,1,0:T(8,128)(2,1)}), bf16[8,2,128,128]{3,2,1,0:T(8,128)(2,1)S(1)}, u32[]{:S(2)}, u32[]{:S(2)}) %all-to-all-start) | async-done | bytes 524320 | tf_op jit(solution)/shard_map/all_to_all | solution.py:371
  33.5 0.4 local_softmax.1
  33.9 0.1 collective-permute-start.6
  33.9 1.2 %collective-permute-done.6.b_ref = f32[2,16,128]{2,1,0:T(8,128)S(1)} collective-permute-done((f32[2,16,128]{2,1,0:T(8,128)S(1)}, f32[2,16,128]{2,1,0:T(8,128)S(1)}, u32[]{:S(2)}, u32[]{:S(2)}) %collective-permute-start.6) | collective-permute-done | bytes 16416 | tf_op jit(solution)/shard_map/ppermute | solution.py:375
  35.1 0.1 normalize.1
  35.3 13.1 %all_to_all.15.w_ref = bf16[8,256,128]{2,1,0:T(8,128)(2,1)S(1)} all-to-all(bf16[8,256,128]{2,1,0:T(8,128)(2,1)S(1)} %normalize.1), channel_id=1, replica_groups=mesh['yh'=2,'z'=4,'core'=2,'blk'=8] {'blk'}, dimensions={0} | all-to-all | bytes 1048576 | tf_op jit(solution)/shard_map/all_to_all | solution.py:377
  48.4 2.3 %accumulate.1 = bf16[8,64,256]{2,1,0:T(8,128)(2,1)S(1)} custom-call(s32[1]{0:T(128)} %bitcast.me_ref, bf16[8,256,128]{2,1,0:T(8,128)(2,1)S(1)} %all_to_all.15.w_ref, bf16[2,16,128,128]{3,2,1,0:T(8,128)(2,1)S(1)} %halve_images.1._.x_ref), custom_call_target="tpu_custom_call" | custom-call | tf_op jit(solution)/shard_map/accumulate/pallas_call | solution.py:316
  50.7 14.4 %all_to_all.16.x_ref = bf16[8,64,256]{2,1,0:T(8,128)(2,1)S(1)} all-to-all(bf16[8,64,256]{2,1,0:T(8,128)(2,1)S(1)} %accumulate.1), channel_id=1, replica_groups=mesh['yh'=2,'z'=4,'core'=2,'blk'=8] {'yh','z'}, dimensions={0} | all-to-all | bytes 524288 | tf_op jit(solution)/shard_map/all_to_all | solution.py:379
  65.2 0.7 %add_up.1 = f32[64,256]{1,0:T(8,128)} custom-call(bf16[8,64,256]{2,1,0:T(8,128)(2,1)S(1)} %all_to_all.16.x_ref), custom_call_target="tpu_custom_call" | custom-call | tf_op jit(solution)/shard_map/add_up/pallas_call | solution.py:337
  (1 shorter events, 0.0 us)
Async XLA Ops:
  0.0 5.1 %copy-start = (bf16[64,16,256]{2,1,0:T(8,128)(2,1)S(1)}, bf16[64,16,256]{2,1,0:T(8,128)(2,1)}, u32[]{:S(2)}) copy-start(bf16[64,16,256]{2,1,0:T(8,128)(2,1)} %own_ref.1) | copy-start | bytes 1572868
  0.0 5.1 %collective-permute-start = (bf16[64,16,256]{2,1,0:T(8,128)(2,1)}, bf16[64,16,256]{2,1,0:T(8,128)(2,1)S(1)}, u32[]{:S(2)}, u32[]{:S(2)}) collective-permute-start(bf16[64,16,256]{2,1,0:T(8,128)(2,1)} %own_ref.1), channel_id=1, source_target_pairs={{0,8},{8,0},{1,9},{9,1},{2,10},{10,2},{3,11},{11,3},{4,12},{12,4},... | collective-permute-start | bytes 1572872 | tf_op jit(solution)/shard_map/ppermute | solution.py:358
  1.7 5.5 %collective-permute-start.1 = (bf16[64,256]{1,0:T(8,128)(2,1)S(1)}, bf16[64,256]{1,0:T(8,128)(2,1)S(1)}, u32[]{:S(2)}, u32[]{:S(2)}) collective-permute-start(bf16[64,256]{1,0:T(8,128)(2,1)S(1)} %pick_block.1.a_ref), channel_id=1, source_target_pairs={{0,64},{64,0},{1,65},{65,1},{2,66},{66,2},{3,67},{67,3},{4,68},{68... | collective-permute-start | bytes 98312 | tf_op jit(solution)/shard_map/ppermute | solution.py:364
  7.2 7.1 %collective-permute-start.2 = (bf16[2,64,256]{2,1,0:T(8,128)(2,1)S(1)}, bf16[2,64,256]{2,1,0:T(8,128)(2,1)S(1)}, u32[]{:S(2)}, u32[]{:S(2)}) collective-permute-start(bf16[2,64,256]{2,1,0:T(8,128)(2,1)S(1)} %pair_up.1.args_0_), channel_id=1, source_target_pairs={{0,16},{16,32},{32,48},{48,0},{1,17},{17,33},{33,49},{49,1},{2,18}... | collective-permute-start | bytes 196616 | tf_op jit(solution)/shard_map/ppermute | solution.py:369
  9.2 6.5 %collective-permute-start.3 = (bf16[2,64,256]{2,1,0:T(8,128)(2,1)S(1)}, bf16[2,64,256]{2,1,0:T(8,128)(2,1)S(1)}, u32[]{:S(2)}, u32[]{:S(2)}) collective-permute-start(bf16[2,64,256]{2,1,0:T(8,128)(2,1)S(1)} %pair_up.1.args_0_), channel_id=1, source_target_pairs={{0,32},{16,48},{32,0},{48,16},{1,33},{17,49},{33,1},{49,17},{2,34}... | collective-permute-start | bytes 196616 | tf_op jit(solution)/shard_map/ppermute | solution.py:369
  12.8 4.3 %collective-permute-start.4 = (bf16[2,64,256]{2,1,0:T(8,128)(2,1)S(1)}, bf16[2,64,256]{2,1,0:T(8,128)(2,1)S(1)}, u32[]{:S(2)}, u32[]{:S(2)}) collective-permute-start(bf16[2,64,256]{2,1,0:T(8,128)(2,1)S(1)} %pair_up.1.args_0_), channel_id=1, source_target_pairs={{0,48},{16,0},{32,16},{48,32},{1,49},{17,1},{33,17},{49,33},{2,50}... | collective-permute-start | bytes 196616 | tf_op jit(solution)/shard_map/ppermute | solution.py:369
  19.8 5.4 %copy-start.1 = (f32[64]{0:T(128)S(1)}, f32[64]{0:T(128)}, u32[]{:S(2)}) copy-start(f32[64]{0:T(128)} %param.9) | copy-start | bytes 772
  19.8 13.6 %all-to-all-start = ((bf16[8,2,128,128]{3,2,1,0:T(8,128)(2,1)}), bf16[8,2,128,128]{3,2,1,0:T(8,128)(2,1)S(1)}, u32[]{:S(2)}, u32[]{:S(2)}) async-start(bf16[8,2,128,128]{3,2,1,0:T(8,128)(2,1)} %correlate.1), calls=%async_computation | async-start | bytes 1048576 | tf_op jit(solution)/shard_map/all_to_all | solution.py:371
  25.3 1.2 %collective-permute-start.5 = (f32[64]{0:T(128)S(1)}, f32[64]{0:T(128)S(1)}, u32[]{:S(2)}, u32[]{:S(2)}) collective-permute-start(f32[64]{0:T(128)S(1)} %copy-done.1), channel_id=1, source_target_pairs={{0,8},{8,0},{1,9},{9,1},{2,10},{10,2},{3,11},{11,3},{4,12},{12,4},... | collective-permute-start | bytes 776 | tf_op jit(solution)/shard_map/ppermute | solution.py:359
  33.9 1.2 %collective-permute-start.6 = (f32[2,16,128]{2,1,0:T(8,128)S(1)}, f32[2,16,128]{2,1,0:T(8,128)S(1)}, u32[]{:S(2)}, u32[]{:S(2)}) collective-permute-start(f32[2,16,128]{2,1,0:T(8,128)S(1)} %get-tuple-element.8.a_ref), channel_id=1, source_target_pairs={{0,8},{8,0},{1,9},{9,1},{2,10},{10,2},{3,11},{11,3},{4,12},{12,4},... | collective-permute-start | bytes 49160 | tf_op jit(solution)/shard_map/ppermute | solution.py:375

commit v6 on v5

--- a/solution.py
+++ b/solution.py
@@ -270,14 +270,14 @@
     )(here(e), here(mine), here(theirs))
 
 
-def accumulate(me, weights, images, ny, nz, step):
-    owners = ny * nz
+def accumulate(order, weights, images, step):
+    owners = order.shape[0]
     nb, cols, lanes = weights.shape
     cycles = images.shape[1]
     classes = cols // N2
     pair = 2 * LANES
 
-    def body(me_ref, w_ref, x_ref, out_ref, scr, x):
+    def body(order_ref, w_ref, x_ref, out_ref, scr, x):
         for r in range(cycles):
             x[0, r], x[1, r] = rotate_images(x_ref, r, nb, step)
         left = lax.broadcasted_iota(jnp.int32, (cols, lanes), 1) < lanes // 2
@@ -307,11 +307,8 @@
                 scr.at[1][rows, :] = 0.5 * (plus - minus)
         whole = jnp.concatenate([scr[0], scr[1]], axis=1)
         whole = whole.reshape(out_ref.shape).astype(BF)
-        place = me_ref[0] // 2
-        y, z = place // nz, place % nz
         for slot in range(owners):
-            dz, dy = slot // ny, slot % ny
-            out_ref[(y + dy) % ny * nz + (z + nz - dz) % nz] = whole[slot]
+            out_ref[order_ref[slot]] = whole[slot]
 
     return pl.pallas_call(
         body,
@@ -324,7 +321,7 @@
         ],
         compiler_params=params(),
         name="accumulate",
-    )(me, here(weights), here(images))
+    )(order, here(weights), here(images))
 
 
 def add_up(parts):
@@ -375,7 +372,9 @@
         theirs = lax.ppermute(stats, "core", swap)
         weights = normalize(e, stats, theirs, nb)
         weights = lax.all_to_all(weights, "blk", 0, 0)
-        totals = accumulate(me, weights, halves, ny, nz, rot)
+        slot = jnp.arange(ny * nz, dtype=jnp.int32)
+        order = (y + slot % ny) % ny * nz + (z + nz - slot // ny) % nz
+        totals = accumulate(order.astype(jnp.int32), weights, halves, rot)
         totals = lax.all_to_all(totals, ("yh", "z"), 0, 0)
         return add_up(totals).reshape(1, 1, kb, cycles, angles)
 

time: 66.1 us -> 68 us (1.029)
  blocking collectives: 27.6 us -> 14.5 us
  waiting for transfers between devices: 13.1 us -> 23.1 us
  starting transfers between devices: 15.6 us -> 19.1 us
  Pallas kernels: 9.32 us -> 10.7 us
    all_to_all x1 -> x0, blocking collectives: 13.1 us -> none  [shards(): weights = lax.all_to_all(weights, 'blk', 0, 0)]
    all_to_all x0 -> x1, waiting for transfers between devices: none -> 9.98 us  [shards(): weights = lax.all_to_all(weights, 'blk', 0, 0)]
    all_to_all x0 -> x1, starting transfers between devices: none -> 3.49 us  [shards(): weights = lax.all_to_all(weights, 'blk', 0, 0)]
    pallas_call x1, Pallas kernels: 0.14 us -> 0.94 us  [normalize(): pl.pallas_call(body, out_shape=VM((copies, cols, 2 * half), BF), in_specs...]
  transfers between devices with their start and end apart: 8 -> 9, of which waited for: 7 -> 8; matrix products, arithmetic and copies ran while one was open for 0% -> 0% of each run, Pallas kernels for 5% -> 4%
where the time goes in v6:
time: 68 us; the launch traced here: 67.6 us
  waiting for transfers between devices  23.1 us (34%)
  starting transfers between devices  19.1 us (28%)
  blocking collectives  14.5 us (21%)
  Pallas kernels  10.7 us (16%)
    all_to_all x1, blocking collectives, shards(): totals = lax.all_to_all(totals, ('yh', 'z'), 0, 0)  14.5 us
    all_to_all x1, waiting for transfers between devices, shards(): weights = lax.all_to_all(weights, 'blk', 0, 0)  9.98 us
    all_to_all x1, waiting for transfers between devices, shards(): scores = lax.all_to_all(scores, 'blk', 0, 0)  6.85 us
    ppermute x3, starting transfers between devices, shards(): refs.append(lax.ppermute(refs[0], 'z', ring))  6.62 us
    all_to_all x1, starting transfers between devices, shards(): scores = lax.all_to_all(scores, 'blk', 0, 0)  5.44 us
    all_to_all x1, starting transfers between devices, shards(): weights = lax.all_to_all(weights, 'blk', 0, 0)  3.49 us
    ppermute x1, starting transfers between devices, shards(): theirs = lax.ppermute(mine, 'yh', swap)  3.39 us
    ppermute x3, waiting for transfers between devices, shards(): refs.append(lax.ppermute(refs[0], 'z', ring))  3.26 us
  transfers between devices with their start and end apart: 9, of which 8 were waited for; matrix products, arithmetic and copies ran while one was open for 0% of the time, Pallas kernels for 4%

profile of v6, /device:TPU:0, one launch (start us, length us, event | category | flops | bytes accessed | tf_op | source)
XLA Modules:
  0.0 67.6 jit_solution(14270943162747366192)
XLA Ops:
  0.0 0.0 copy-start
  0.0 0.0 collective-permute-start
  0.0 1.7 %pick_block.1.a_ref = bf16[64,256]{1,0:T(8,128)(2,1)S(1)} custom-call(s32[1]{0:T(128)} %bitcast.1.me_ref, s32[16]{0:T(128)} %owner_ref.1, f32[64]{0:T(128)} %gain_ref.1, bf16[16,4,16,256]{3,2,1,0:T(8,128)(2,1)} %bitcast.4), custom_call_target="tpu_custom_call" | custom-call | tf_op jit(solution)/shard_map/pick_block/pallas_call | solution.py:80
  1.7 3.4 %collective-permute-start.1 = (bf16[64,256]{1,0:T(8,128)(2,1)S(1)}, bf16[64,256]{1,0:T(8,128)(2,1)S(1)}, u32[]{:S(2)}, u32[]{:S(2)}) collective-permute-start(bf16[64,256]{1,0:T(8,128)(2,1)S(1)} %pick_block.1.a_ref), channel_id=1, source_target_pairs={{0,64},{64,0},{1,65},{65,1},{2,66},{66,2},{3,67},{67,3},{4,68},{68... | collective-permute-start | bytes 98312 | tf_op jit(solution)/shard_map/ppermute | solution.py:361
  5.1 0.0 collective-permute-done.other_ref
  5.1 0.0 copy-done
  5.1 1.3 %halve_images.1._.x_ref = bf16[2,16,128,128]{3,2,1,0:T(8,128)(2,1)S(1)} custom-call(bf16[64,16,256]{2,1,0:T(8,128)(2,1)S(1)} %copy-done, bf16[64,16,256]{2,1,0:T(8,128)(2,1)S(1)} %collective-permute-done.other_ref), custom_call_target="tpu_custom_call" | custom-call | tf_op jit(solution)/shard_map/halve_images/pallas_call | solution.py:107
  6.4 0.8 %collective-permute-done.1.b_ref = bf16[64,256]{1,0:T(8,128)(2,1)S(1)} collective-permute-done((bf16[64,256]{1,0:T(8,128)(2,1)S(1)}, bf16[64,256]{1,0:T(8,128)(2,1)S(1)}, u32[]{:S(2)}, u32[]{:S(2)}) %collective-permute-start.1) | collective-permute-done | bytes 32800 | tf_op jit(solution)/shard_map/ppermute | solution.py:361
  7.2 2.0 %collective-permute-start.2 = (bf16[2,64,256]{2,1,0:T(8,128)(2,1)S(1)}, bf16[2,64,256]{2,1,0:T(8,128)(2,1)S(1)}, u32[]{:S(2)}, u32[]{:S(2)}) collective-permute-start(bf16[2,64,256]{2,1,0:T(8,128)(2,1)S(1)} %pair_up.1.args_0_), channel_id=1, source_target_pairs={{0,16},{16,32},{32,48},{48,0},{1,17},{17,33},{33,49},{49,1},{2,18}... | collective-permute-start | bytes 196616 | tf_op jit(solution)/shard_map/ppermute | solution.py:366
  9.2 3.6 %collective-permute-start.3 = (bf16[2,64,256]{2,1,0:T(8,128)(2,1)S(1)}, bf16[2,64,256]{2,1,0:T(8,128)(2,1)S(1)}, u32[]{:S(2)}, u32[]{:S(2)}) collective-permute-start(bf16[2,64,256]{2,1,0:T(8,128)(2,1)S(1)} %pair_up.1.args_0_), channel_id=1, source_target_pairs={{0,32},{16,48},{32,0},{48,16},{1,33},{17,49},{33,1},{49,17},{2,34}... | collective-permute-start | bytes 196616 | tf_op jit(solution)/shard_map/ppermute | solution.py:366
  12.8 1.0 %collective-permute-start.4 = (bf16[2,64,256]{2,1,0:T(8,128)(2,1)S(1)}, bf16[2,64,256]{2,1,0:T(8,128)(2,1)S(1)}, u32[]{:S(2)}, u32[]{:S(2)}) collective-permute-start(bf16[2,64,256]{2,1,0:T(8,128)(2,1)S(1)} %pair_up.1.args_0_), channel_id=1, source_target_pairs={{0,48},{16,0},{32,16},{48,32},{1,49},{17,1},{33,17},{49,33},{2,50}... | collective-permute-start | bytes 196616 | tf_op jit(solution)/shard_map/ppermute | solution.py:366
  13.8 0.5 collective-permute-done.2.args_1_
  14.3 1.5 %collective-permute-done.3.args_2_ = bf16[2,64,256]{2,1,0:T(8,128)(2,1)S(1)} collective-permute-done((bf16[2,64,256]{2,1,0:T(8,128)(2,1)S(1)}, bf16[2,64,256]{2,1,0:T(8,128)(2,1)S(1)}, u32[]{:S(2)}, u32[]{:S(2)}) %collective-permute-start.3) | collective-permute-done | bytes 65568 | tf_op jit(solution)/shard_map/ppermute | solution.py:366
  15.8 1.3 %collective-permute-done.4.args_3_ = bf16[2,64,256]{2,1,0:T(8,128)(2,1)S(1)} collective-permute-done((bf16[2,64,256]{2,1,0:T(8,128)(2,1)S(1)}, bf16[2,64,256]{2,1,0:T(8,128)(2,1)S(1)}, u32[]{:S(2)}, u32[]{:S(2)}) %collective-permute-start.4) | collective-permute-done | bytes 65568 | tf_op jit(solution)/shard_map/ppermute | solution.py:366
  17.1 2.8 %correlate.1 = bf16[8,2,128,128]{3,2,1,0:T(8,128)(2,1)} custom-call(bf16[2,16,128,128]{3,2,1,0:T(8,128)(2,1)S(1)} %halve_images.1._.x_ref, bf16[2,64,256]{2,1,0:T(8,128)(2,1)S(1)} %pair_up.1.args_0_, bf16[2,64,256]{2,1,0:T(8,128)(2,1)S(1)} %collective-permute-done.2.args_1_, bf16[2,64,256]{2,1,0:T(8,128)(2,1)S(1)} %collective-permute-done.3.args_2_, ...), custom_call_target="tpu_custom_call" | custom-call | tf_op jit(solution)/shard_map/correlate/pallas_call | solution.py:184
  19.8 0.0 copy-start.1
  19.8 5.4 %all-to-all-start = ((bf16[8,2,128,128]{3,2,1,0:T(8,128)(2,1)}), bf16[8,2,128,128]{3,2,1,0:T(8,128)(2,1)S(1)}, u32[]{:S(2)}, u32[]{:S(2)}) async-start(bf16[8,2,128,128]{3,2,1,0:T(8,128)(2,1)} %correlate.1), calls=%async_computation | async-start | bytes 1048576 | tf_op jit(solution)/shard_map/all_to_all | solution.py:368
  25.3 0.0 copy-done.1
  25.3 0.1 collective-permute-start.5
  25.4 0.1 reshape.9.a_ref
  25.5 1.1 %collective-permute-done.5 = f32[64]{0:T(128)S(1)} collective-permute-done((f32[64]{0:T(128)S(1)}, f32[64]{0:T(128)S(1)}, u32[]{:S(2)}, u32[]{:S(2)}) %collective-permute-start.5) | collective-permute-done | bytes 288 | tf_op jit(solution)/shard_map/ppermute | solution.py:356
  26.5 0.1 reshape.10.b_ref
  26.6 6.9 %all-to-all-done.x_ref = bf16[8,2,128,128]{3,2,1,0:T(8,128)(2,1)S(1)} async-done(((bf16[8,2,128,128]{3,2,1,0:T(8,128)(2,1)}), bf16[8,2,128,128]{3,2,1,0:T(8,128)(2,1)S(1)}, u32[]{:S(2)}, u32[]{:S(2)}) %all-to-all-start) | async-done | bytes 524320 | tf_op jit(solution)/shard_map/all_to_all | solution.py:368
  33.5 0.4 local_softmax.1
  33.9 0.1 collective-permute-start.6
  33.9 1.2 %collective-permute-done.6.b_ref = f32[2,16,128]{2,1,0:T(8,128)S(1)} collective-permute-done((f32[2,16,128]{2,1,0:T(8,128)S(1)}, f32[2,16,128]{2,1,0:T(8,128)S(1)}, u32[]{:S(2)}, u32[]{:S(2)}) %collective-permute-start.6) | collective-permute-done | bytes 16416 | tf_op jit(solution)/shard_map/ppermute | solution.py:372
  35.1 0.9 %normalize.1 = bf16[8,256,128]{2,1,0:T(8,128)(2,1)} custom-call(f32[2,64,256]{2,1,0:T(8,128)S(1)} %get-tuple-element.7.e_ref, f32[2,16,128]{2,1,0:T(8,128)S(1)} %get-tuple-element.8.a_ref, f32[2,16,128]{2,1,0:T(8,128)S(1)} %collective-permute-done.6.b_ref), custom_call_target="tpu_custom_call" | custom-call | tf_op jit(solution)/shard_map/normalize/pallas_call | solution.py:263
  36.1 3.5 %all-to-all-start.1 = ((bf16[8,256,128]{2,1,0:T(8,128)(2,1)}), bf16[8,256,128]{2,1,0:T(8,128)(2,1)S(1)}, u32[]{:S(2)}, u32[]{:S(2)}) async-start(bf16[8,256,128]{2,1,0:T(8,128)(2,1)} %normalize.1), calls=%async_computation.1 | async-start | bytes 1048576 | tf_op jit(solution)/shard_map/all_to_all | solution.py:374
  39.6 10.0 %all-to-all-done.1.w_ref = bf16[8,256,128]{2,1,0:T(8,128)(2,1)S(1)} async-done(((bf16[8,256,128]{2,1,0:T(8,128)(2,1)}), bf16[8,256,128]{2,1,0:T(8,128)(2,1)S(1)}, u32[]{:S(2)}, u32[]{:S(2)}) %all-to-all-start.1) | async-done | bytes 524320 | tf_op jit(solution)/shard_map/all_to_all | solution.py:374
  49.6 2.9 %accumulate.1 = bf16[8,64,256]{2,1,0:T(8,128)(2,1)S(1)} custom-call(s32[8]{0:T(128)S(1)} %fusion.order_ref, bf16[8,256,128]{2,1,0:T(8,128)(2,1)S(1)} %all-to-all-done.1.w_ref, bf16[2,16,128,128]{3,2,1,0:T(8,128)(2,1)S(1)} %halve_images.1._.x_ref), custom_call_target="tpu_custom_call" | custom-call | tf_op jit(solution)/shard_map/accumulate/pallas_call | solution.py:313
  52.4 14.5 %all_to_all.15.x_ref = bf16[8,64,256]{2,1,0:T(8,128)(2,1)S(1)} all-to-all(bf16[8,64,256]{2,1,0:T(8,128)(2,1)S(1)} %accumulate.1), channel_id=1, replica_groups=mesh['yh'=2,'z'=4,'core'=2,'blk'=8] {'yh','z'}, dimensions={0} | all-to-all | bytes 524288 | tf_op jit(solution)/shard_map/all_to_all | solution.py:378
  66.9 0.7 add_up.1
  (2 shorter events, 0.0 us)
Async XLA Ops:
  0.0 5.1 %copy-start = (bf16[64,16,256]{2,1,0:T(8,128)(2,1)S(1)}, bf16[64,16,256]{2,1,0:T(8,128)(2,1)}, u32[]{:S(2)}) copy-start(bf16[64,16,256]{2,1,0:T(8,128)(2,1)} %own_ref.1) | copy-start | bytes 1572868
  0.0 5.1 %collective-permute-start = (bf16[64,16,256]{2,1,0:T(8,128)(2,1)}, bf16[64,16,256]{2,1,0:T(8,128)(2,1)S(1)}, u32[]{:S(2)}, u32[]{:S(2)}) collective-permute-start(bf16[64,16,256]{2,1,0:T(8,128)(2,1)} %own_ref.1), channel_id=1, source_target_pairs={{0,8},{8,0},{1,9},{9,1},{2,10},{10,2},{3,11},{11,3},{4,12},{12,4},... | collective-permute-start | bytes 1572872 | tf_op jit(solution)/shard_map/ppermute | solution.py:355
  1.7 5.5 %collective-permute-start.1 = (bf16[64,256]{1,0:T(8,128)(2,1)S(1)}, bf16[64,256]{1,0:T(8,128)(2,1)S(1)}, u32[]{:S(2)}, u32[]{:S(2)}) collective-permute-start(bf16[64,256]{1,0:T(8,128)(2,1)S(1)} %pick_block.1.a_ref), channel_id=1, source_target_pairs={{0,64},{64,0},{1,65},{65,1},{2,66},{66,2},{3,67},{67,3},{4,68},{68... | collective-permute-start | bytes 98312 | tf_op jit(solution)/shard_map/ppermute | solution.py:361
  7.2 7.1 %collective-permute-start.2 = (bf16[2,64,256]{2,1,0:T(8,128)(2,1)S(1)}, bf16[2,64,256]{2,1,0:T(8,128)(2,1)S(1)}, u32[]{:S(2)}, u32[]{:S(2)}) collective-permute-start(bf16[2,64,256]{2,1,0:T(8,128)(2,1)S(1)} %pair_up.1.args_0_), channel_id=1, source_target_pairs={{0,16},{16,32},{32,48},{48,0},{1,17},{17,33},{33,49},{49,1},{2,18}... | collective-permute-start | bytes 196616 | tf_op jit(solution)/shard_map/ppermute | solution.py:366
  9.2 6.5 %collective-permute-start.3 = (bf16[2,64,256]{2,1,0:T(8,128)(2,1)S(1)}, bf16[2,64,256]{2,1,0:T(8,128)(2,1)S(1)}, u32[]{:S(2)}, u32[]{:S(2)}) collective-permute-start(bf16[2,64,256]{2,1,0:T(8,128)(2,1)S(1)} %pair_up.1.args_0_), channel_id=1, source_target_pairs={{0,32},{16,48},{32,0},{48,16},{1,33},{17,49},{33,1},{49,17},{2,34}... | collective-permute-start | bytes 196616 | tf_op jit(solution)/shard_map/ppermute | solution.py:366
  12.8 4.3 %collective-permute-start.4 = (bf16[2,64,256]{2,1,0:T(8,128)(2,1)S(1)}, bf16[2,64,256]{2,1,0:T(8,128)(2,1)S(1)}, u32[]{:S(2)}, u32[]{:S(2)}) collective-permute-start(bf16[2,64,256]{2,1,0:T(8,128)(2,1)S(1)} %pair_up.1.args_0_), channel_id=1, source_target_pairs={{0,48},{16,0},{32,16},{48,32},{1,49},{17,1},{33,17},{49,33},{2,50}... | collective-permute-start | bytes 196616 | tf_op jit(solution)/shard_map/ppermute | solution.py:366
  19.8 5.4 %copy-start.1 = (f32[64]{0:T(128)S(1)}, f32[64]{0:T(128)}, u32[]{:S(2)}) copy-start(f32[64]{0:T(128)} %param.9) | copy-start | bytes 772
  19.8 13.6 %all-to-all-start = ((bf16[8,2,128,128]{3,2,1,0:T(8,128)(2,1)}), bf16[8,2,128,128]{3,2,1,0:T(8,128)(2,1)S(1)}, u32[]{:S(2)}, u32[]{:S(2)}) async-start(bf16[8,2,128,128]{3,2,1,0:T(8,128)(2,1)} %correlate.1), calls=%async_computation | async-start | bytes 1048576 | tf_op jit(solution)/shard_map/all_to_all | solution.py:368
  25.3 1.2 %collective-permute-start.5 = (f32[64]{0:T(128)S(1)}, f32[64]{0:T(128)S(1)}, u32[]{:S(2)}, u32[]{:S(2)}) collective-permute-start(f32[64]{0:T(128)S(1)} %copy-done.1), channel_id=1, source_target_pairs={{0,8},{8,0},{1,9},{9,1},{2,10},{10,2},{3,11},{11,3},{4,12},{12,4},... | collective-permute-start | bytes 776 | tf_op jit(solution)/shard_map/ppermute | solution.py:356
  33.9 1.2 %collective-permute-start.6 = (f32[2,16,128]{2,1,0:T(8,128)S(1)}, f32[2,16,128]{2,1,0:T(8,128)S(1)}, u32[]{:S(2)}, u32[]{:S(2)}) collective-permute-start(f32[2,16,128]{2,1,0:T(8,128)S(1)} %get-tuple-element.8.a_ref), channel_id=1, source_target_pairs={{0,8},{8,0},{1,9},{9,1},{2,10},{10,2},{3,11},{11,3},{4,12},{12,4},... | collective-permute-start | bytes 49160 | tf_op jit(solution)/shard_map/ppermute | solution.py:372
  36.1 13.5 %all-to-all-start.1 = ((bf16[8,256,128]{2,1,0:T(8,128)(2,1)}), bf16[8,256,128]{2,1,0:T(8,128)(2,1)S(1)}, u32[]{:S(2)}, u32[]{:S(2)}) async-start(bf16[8,256,128]{2,1,0:T(8,128)(2,1)} %normalize.1), calls=%async_computation.1 | async-start | bytes 1048576 | tf_op jit(solution)/shard_map/all_to_all | solution.py:374

commit v7 on v5

--- a/solution.py
+++ b/solution.py
@@ -142,7 +142,7 @@
     ]
 
 
-def correlate(images, refs, nb, step):
+def correlate(images, refs, nb, step, before=()):
     _, cycles, particles, _ = images.shape
     total = N1 * particles
     rows = total // nb
@@ -150,9 +150,16 @@
     classes = len(refs) * near * far // cycles
     cols = N2 * classes
     angles = 2 * LANES
+    first = sum(b.shape[1] for b in before)
+    tiles = first + cols // LANES
 
     def body(x_ref, *args):
-        r_refs, (out_ref, scr, rr, x) = args[: len(refs)], args[len(refs) :]
+        r_refs, args = args[: len(refs)], args[len(refs) :]
+        b_refs, (out_ref, scr, rr, x) = args[: len(before)], args[len(before) :]
+        at = 0
+        for b_ref in b_refs:
+            out_ref[:, at : at + b_ref.shape[1]] = b_ref[...]
+            at += b_ref.shape[1]
         blocks = [r_ref[d].astype(F32) for r_ref in r_refs for d in range(near)]
         fill(scr, jnp.concatenate(blocks, axis=0))
         square = jnp.zeros((classes, LANES), F32)
@@ -179,12 +186,14 @@
                 part = part - norm
             for t in range(cols // LANES):
                 tile = part[:, t * LANES : (t + 1) * LANES].astype(BF)
-                out_ref[:, t, i * rows : (i + 1) * rows, :] = tile.reshape(nb, rows, LANES)
-
-    return pl.pallas_call(
-        body,
-        out_shape=jax.ShapeDtypeStruct((nb, cols // LANES, 2 * rows, LANES), BF),
-        in_specs=[spec()] * (1 + len(refs)),
+                at = slice(i * rows, (i + 1) * rows)
+                out_ref[:, first + t, at, :] = tile.reshape(nb, rows, LANES)
+
+    out_shape = jax.ShapeDtypeStruct if before else VM
+    return pl.pallas_call(
+        body,
+        out_shape=out_shape((nb, tiles, 2 * rows, LANES), BF),
+        in_specs=[spec()] * (1 + len(refs) + len(before)),
         out_specs=spec(),
         scratch_shapes=[
             VM((2, classes * cycles, LANES), F32),
@@ -193,7 +202,7 @@
         ],
         compiler_params=params(),
         name="correlate",
-    )(here(images), *[here(r) for r in refs])
+    )(here(images), *[here(r) for r in (*refs, *before)])
 
 
 def local_softmax(me, scores, precision, others):
@@ -275,6 +284,7 @@
     nb, cols, lanes = weights.shape
     cycles = images.shape[1]
     classes = cols // N2
+    per = LANES // N2
     pair = 2 * LANES
 
     def body(me_ref, w_ref, x_ref, out_ref, scr, x):
@@ -296,7 +306,13 @@
                 plus = minus = None
                 for s in range(N2):
                     p, m = (
-                        v[s * classes : (s + 1) * classes, d * LANES : (d + 1) * LANES]
+                        jnp.concatenate(
+                            [
+                                v[t + s * per : t + (s + 1) * per, d * LANES : (d + 1) * LANES]
+                                for t in range(0, cols, LANES)
+                            ],
+                            axis=0,
+                        )
                         for v in spread
                     )
                     p, m = turn(p, m, step * N1 * s)
@@ -310,8 +326,8 @@
         place = me_ref[0] // 2
         y, z = place // nz, place % nz
         for slot in range(owners):
-            dz, dy = slot // ny, slot % ny
-            out_ref[(y + dy) % ny * nz + (z + nz - dz) % nz] = whole[slot]
+            dz, dy = (0, 1, 3, 2)[slot // ny], slot % ny
+            out_ref[(y ^ dy) * nz + (z ^ dz)] = whole[slot]
 
     return pl.pallas_call(
         body,
@@ -364,10 +380,11 @@
         theirs = lax.ppermute(mine, "yh", swap)
         halves = halve_images(images, other, nb)
         refs = [pair_up(mine, theirs, halves)]
-        for d in range(1, nz):
-            ring = [(i, (i + d) % nz) for i in range(nz)]
+        for d in (1, 3, 2):
+            ring = [(i, i ^ d) for i in range(nz)]
             refs.append(lax.ppermute(refs[0], "z", ring))
-        scores = correlate(halves, refs, nb, rot)
+        early = correlate(halves, refs[:2], nb, rot)
+        scores = correlate(halves, refs[2:], nb, rot, (early,))
         scores = lax.all_to_all(scores, "blk", 0, 0)
         e, stats = local_softmax(
             j, scores, precision.reshape(nb, half), other_precision.reshape(nb, half)

time: 66.1 us -> 64.9 us (0.982)
  blocking collectives: 27.6 us -> 26.3 us
  Pallas kernels: 9.32 us -> 10.4 us
  starting transfers between devices: 15.6 us -> 14.6 us
    all_to_all x1, blocking collectives: 14.4 us -> 13.2 us  [shards(): totals = lax.all_to_all(totals, ('yh', 'z'), 0, 0)]
    pallas_call x1 -> x2, Pallas kernels: 2.76 us -> 3.8 us  [correlate(): pl.pallas_call(body, out_shape=out_shape((nb, tiles, 2 * rows, LANES), BF...]
    ppermute x3, starting transfers between devices: 6.62 us -> 5.61 us  [shards(): refs.append(lax.ppermute(refs[0], 'z', ring))]
  transfers between devices with their start and end apart: 8 -> 8, of which waited for: 7 -> 6; matrix products, arithmetic and copies ran while one was open for 0% -> 0% of each run, Pallas kernels for 5% -> 7%
where the time goes in v7:
time: 64.9 us; the launch traced here: 64.6 us
  blocking collectives  26.3 us (41%)
  starting transfers between devices  14.6 us (22%)
  waiting for transfers between devices  13.1 us (20%)
  Pallas kernels  10.4 us (16%)
    all_to_all x1, blocking collectives, shards(): totals = lax.all_to_all(totals, ('yh', 'z'), 0, 0)  13.2 us
    all_to_all x1, blocking collectives, shards(): weights = lax.all_to_all(weights, 'blk', 0, 0)  13.1 us
    all_to_all x1, waiting for transfers between devices, shards(): scores = lax.all_to_all(scores, 'blk', 0, 0)  6.85 us
    ppermute x3, starting transfers between devices, shards(): refs.append(lax.ppermute(refs[0], 'z', ring))  5.61 us
    all_to_all x1, starting transfers between devices, shards(): scores = lax.all_to_all(scores, 'blk', 0, 0)  5.45 us
    pallas_call x2, Pallas kernels, correlate(): pl.pallas_call(body, out_shape=out_shape((nb, tiles, 2 * rows, LANES), BF...  3.8 us
    ppermute x1, starting transfers between devices, shards(): theirs = lax.ppermute(mine, 'yh', swap)  3.39 us
    ppermute x3, waiting for transfers between devices, shards(): refs.append(lax.ppermute(refs[0], 'z', ring))  3.19 us
  transfers between devices with their start and end apart: 8, of which 6 were waited for; matrix products, arithmetic and copies ran while one was open for 0% of the time, Pallas kernels for 7%

profile of v7, /device:TPU:0, one launch (start us, length us, event | category | flops | bytes accessed | tf_op | source)
XLA Modules:
  0.0 64.6 jit_solution(5304824988059519067)
XLA Ops:
  0.0 0.0 copy-start
  0.0 0.0 collective-permute-start
  0.0 1.7 %pick_block.1.a_ref = bf16[64,256]{1,0:T(8,128)(2,1)S(1)} custom-call(s32[1]{0:T(128)} %bitcast.me_ref, s32[16]{0:T(128)} %owner_ref.1, f32[64]{0:T(128)} %gain_ref.1, bf16[16,4,16,256]{3,2,1,0:T(8,128)(2,1)} %bitcast.4), custom_call_target="tpu_custom_call" | custom-call | tf_op jit(solution)/shard_map/pick_block/pallas_call | solution.py:80
  1.7 3.4 %collective-permute-start.1 = (bf16[64,256]{1,0:T(8,128)(2,1)S(1)}, bf16[64,256]{1,0:T(8,128)(2,1)S(1)}, u32[]{:S(2)}, u32[]{:S(2)}) collective-permute-start(bf16[64,256]{1,0:T(8,128)(2,1)S(1)} %pick_block.1.a_ref), channel_id=1, source_target_pairs={{0,64},{64,0},{1,65},{65,1},{2,66},{66,2},{3,67},{67,3},{4,68},{68... | collective-permute-start | bytes 98312 | tf_op jit(solution)/shard_map/ppermute | solution.py:380
  5.1 0.0 collective-permute-done.other_ref
  5.1 0.0 copy-done
  5.1 1.3 %halve_images.1._.x_ref = bf16[2,16,128,128]{3,2,1,0:T(8,128)(2,1)S(1)} custom-call(bf16[64,16,256]{2,1,0:T(8,128)(2,1)S(1)} %copy-done, bf16[64,16,256]{2,1,0:T(8,128)(2,1)S(1)} %collective-permute-done.other_ref), custom_call_target="tpu_custom_call" | custom-call | tf_op jit(solution)/shard_map/halve_images/pallas_call | solution.py:107
  6.4 0.8 %collective-permute-done.1.b_ref = bf16[64,256]{1,0:T(8,128)(2,1)S(1)} collective-permute-done((bf16[64,256]{1,0:T(8,128)(2,1)S(1)}, bf16[64,256]{1,0:T(8,128)(2,1)S(1)}, u32[]{:S(2)}, u32[]{:S(2)}) %collective-permute-start.1) | collective-permute-done | bytes 32800 | tf_op jit(solution)/shard_map/ppermute | solution.py:380
  7.2 2.0 %collective-permute-start.4 = (bf16[2,64,256]{2,1,0:T(8,128)(2,1)S(1)}, bf16[2,64,256]{2,1,0:T(8,128)(2,1)S(1)}, u32[]{:S(2)}, u32[]{:S(2)}) collective-permute-start(bf16[2,64,256]{2,1,0:T(8,128)(2,1)S(1)} %pair_up.1.args_0_), channel_id=1, source_target_pairs={{0,16},{16,0},{32,48},{48,32},{1,17},{17,1},{33,49},{49,33},{2,18}... | collective-permute-start | bytes 196616 | tf_op jit(solution)/shard_map/ppermute | solution.py:385
  9.2 2.5 %collective-permute-start.2 = (bf16[2,64,256]{2,1,0:T(8,128)(2,1)S(1)}, bf16[2,64,256]{2,1,0:T(8,128)(2,1)S(1)}, u32[]{:S(2)}, u32[]{:S(2)}) collective-permute-start(bf16[2,64,256]{2,1,0:T(8,128)(2,1)S(1)} %pair_up.1.args_0_), channel_id=1, source_target_pairs={{0,48},{16,32},{32,16},{48,0},{1,49},{17,33},{33,17},{49,1},{2,50}... | collective-permute-start | bytes 196616 | tf_op jit(solution)/shard_map/ppermute | solution.py:385
  11.8 1.1 %collective-permute-start.3 = (bf16[2,64,256]{2,1,0:T(8,128)(2,1)S(1)}, bf16[2,64,256]{2,1,0:T(8,128)(2,1)S(1)}, u32[]{:S(2)}, u32[]{:S(2)}) collective-permute-start(bf16[2,64,256]{2,1,0:T(8,128)(2,1)S(1)} %pair_up.1.args_0_), channel_id=1, source_target_pairs={{0,32},{16,48},{32,0},{48,16},{1,33},{17,49},{33,1},{49,17},{2,34}... | collective-permute-start | bytes 196616 | tf_op jit(solution)/shard_map/ppermute | solution.py:385
  12.8 0.0 collective-permute-done.4.args_1_
  12.8 1.5 %correlate.2.args_2_ = bf16[8,1,128,128]{3,2,1,0:T(8,128)(2,1)S(1)} custom-call(bf16[2,16,128,128]{3,2,1,0:T(8,128)(2,1)S(1)} %halve_images.1._.x_ref, bf16[2,64,256]{2,1,0:T(8,128)(2,1)S(1)} %pair_up.1.args_0_, bf16[2,64,256]{2,1,0:T(8,128)(2,1)S(1)} %collective-permute-done.4.args_1_), custom_call_target="tpu_custom_call" | custom-call | tf_op jit(solution)/shard_map/correlate/pallas_call | solution.py:193
  14.3 0.5 collective-permute-done.2.args_0_
  14.8 2.7 %collective-permute-done.3.args_1_ = bf16[2,64,256]{2,1,0:T(8,128)(2,1)S(1)} collective-permute-done((bf16[2,64,256]{2,1,0:T(8,128)(2,1)S(1)}, bf16[2,64,256]{2,1,0:T(8,128)(2,1)S(1)}, u32[]{:S(2)}, u32[]{:S(2)}) %collective-permute-start.3) | collective-permute-done | bytes 65568 | tf_op jit(solution)/shard_map/ppermute | solution.py:385
  17.5 2.3 %correlate.3 = bf16[8,2,128,128]{3,2,1,0:T(8,128)(2,1)} custom-call(bf16[2,16,128,128]{3,2,1,0:T(8,128)(2,1)S(1)} %halve_images.1._.x_ref, bf16[2,64,256]{2,1,0:T(8,128)(2,1)S(1)} %collective-permute-done.2.args_0_, bf16[2,64,256]{2,1,0:T(8,128)(2,1)S(1)} %collective-permute-done.3.args_1_, bf16[8,1,128,128]{3,2,1,0:T(8,128)(2,1)S(1)} %correlate.2.args_2_), custom_call_target="tpu_custom_call" | custom-call | tf_op jit(solution)/shard_map/correlate/pallas_call | solution.py:193
  19.8 0.0 copy-start.1
  19.8 5.4 %all-to-all-start = ((bf16[8,2,128,128]{3,2,1,0:T(8,128)(2,1)}), bf16[8,2,128,128]{3,2,1,0:T(8,128)(2,1)S(1)}, u32[]{:S(2)}, u32[]{:S(2)}) async-start(bf16[8,2,128,128]{3,2,1,0:T(8,128)(2,1)} %correlate.3), calls=%async_computation | async-start | bytes 1048576 | tf_op jit(solution)/shard_map/all_to_all | solution.py:388
  25.3 0.0 copy-done.1
  25.3 0.1 collective-permute-start.5
  25.4 0.1 reshape.9.a_ref
  25.4 1.1 %collective-permute-done.5 = f32[64]{0:T(128)S(1)} collective-permute-done((f32[64]{0:T(128)S(1)}, f32[64]{0:T(128)S(1)}, u32[]{:S(2)}, u32[]{:S(2)}) %collective-permute-start.5) | collective-permute-done | bytes 288 | tf_op jit(solution)/shard_map/ppermute | solution.py:375
  26.5 0.1 reshape.10.b_ref
  26.6 6.9 %all-to-all-done.x_ref = bf16[8,2,128,128]{3,2,1,0:T(8,128)(2,1)S(1)} async-done(((bf16[8,2,128,128]{3,2,1,0:T(8,128)(2,1)}), bf16[8,2,128,128]{3,2,1,0:T(8,128)(2,1)S(1)}, u32[]{:S(2)}, u32[]{:S(2)}) %all-to-all-start) | async-done | bytes 524320 | tf_op jit(solution)/shard_map/all_to_all | solution.py:388
  33.4 0.4 local_softmax.1
  33.9 0.1 collective-permute-start.6
  33.9 1.2 %collective-permute-done.6.b_ref = f32[2,16,128]{2,1,0:T(8,128)S(1)} collective-permute-done((f32[2,16,128]{2,1,0:T(8,128)S(1)}, f32[2,16,128]{2,1,0:T(8,128)S(1)}, u32[]{:S(2)}, u32[]{:S(2)}) %collective-permute-start.6) | collective-permute-done | bytes 16416 | tf_op jit(solution)/shard_map/ppermute | solution.py:392
  35.1 0.1 normalize.1
  35.2 13.1 %all_to_all.15.w_ref = bf16[8,256,128]{2,1,0:T(8,128)(2,1)S(1)} all-to-all(bf16[8,256,128]{2,1,0:T(8,128)(2,1)S(1)} %normalize.1), channel_id=1, replica_groups=mesh['yh'=2,'z'=4,'core'=2,'blk'=8] {'blk'}, dimensions={0} | all-to-all | bytes 1048576 | tf_op jit(solution)/shard_map/all_to_all | solution.py:394
  48.3 2.4 %accumulate.1 = bf16[8,64,256]{2,1,0:T(8,128)(2,1)S(1)} custom-call(s32[1]{0:T(128)} %bitcast.me_ref, bf16[8,256,128]{2,1,0:T(8,128)(2,1)S(1)} %all_to_all.15.w_ref, bf16[2,16,128,128]{3,2,1,0:T(8,128)(2,1)S(1)} %halve_images.1._.x_ref), custom_call_target="tpu_custom_call" | custom-call | tf_op jit(solution)/shard_map/accumulate/pallas_call | solution.py:332
  50.8 13.2 %all_to_all.16.x_ref = bf16[8,64,256]{2,1,0:T(8,128)(2,1)S(1)} all-to-all(bf16[8,64,256]{2,1,0:T(8,128)(2,1)S(1)} %accumulate.1), channel_id=1, replica_groups=mesh['yh'=2,'z'=4,'core'=2,'blk'=8] {'yh','z'}, dimensions={0} | all-to-all | bytes 524288 | tf_op jit(solution)/shard_map/all_to_all | solution.py:396
  64.0 0.7 %add_up.1 = f32[64,256]{1,0:T(8,128)} custom-call(bf16[8,64,256]{2,1,0:T(8,128)(2,1)S(1)} %all_to_all.16.x_ref), custom_call_target="tpu_custom_call" | custom-call | tf_op jit(solution)/shard_map/add_up/pallas_call | solution.py:353
  (1 shorter events, 0.0 us)
Async XLA Ops:
  0.0 5.1 %copy-start = (bf16[64,16,256]{2,1,0:T(8,128)(2,1)S(1)}, bf16[64,16,256]{2,1,0:T(8,128)(2,1)}, u32[]{:S(2)}) copy-start(bf16[64,16,256]{2,1,0:T(8,128)(2,1)} %own_ref.1) | copy-start | bytes 1572868
  0.0 5.1 %collective-permute-start = (bf16[64,16,256]{2,1,0:T(8,128)(2,1)}, bf16[64,16,256]{2,1,0:T(8,128)(2,1)S(1)}, u32[]{:S(2)}, u32[]{:S(2)}) collective-permute-start(bf16[64,16,256]{2,1,0:T(8,128)(2,1)} %own_ref.1), channel_id=1, source_target_pairs={{0,8},{8,0},{1,9},{9,1},{2,10},{10,2},{3,11},{11,3},{4,12},{12,4},... | collective-permute-start | bytes 1572872 | tf_op jit(solution)/shard_map/ppermute | solution.py:374
  1.7 5.5 %collective-permute-start.1 = (bf16[64,256]{1,0:T(8,128)(2,1)S(1)}, bf16[64,256]{1,0:T(8,128)(2,1)S(1)}, u32[]{:S(2)}, u32[]{:S(2)}) collective-permute-start(bf16[64,256]{1,0:T(8,128)(2,1)S(1)} %pick_block.1.a_ref), channel_id=1, source_target_pairs={{0,64},{64,0},{1,65},{65,1},{2,66},{66,2},{3,67},{67,3},{4,68},{68... | collective-permute-start | bytes 98312 | tf_op jit(solution)/shard_map/ppermute | solution.py:380
  7.2 5.6 %collective-permute-start.4 = (bf16[2,64,256]{2,1,0:T(8,128)(2,1)S(1)}, bf16[2,64,256]{2,1,0:T(8,128)(2,1)S(1)}, u32[]{:S(2)}, u32[]{:S(2)}) collective-permute-start(bf16[2,64,256]{2,1,0:T(8,128)(2,1)S(1)} %pair_up.1.args_0_), channel_id=1, source_target_pairs={{0,16},{16,0},{32,48},{48,32},{1,17},{17,1},{33,49},{49,33},{2,18}... | collective-permute-start | bytes 196616 | tf_op jit(solution)/shard_map/ppermute | solution.py:385
  9.2 5.6 %collective-permute-start.2 = (bf16[2,64,256]{2,1,0:T(8,128)(2,1)S(1)}, bf16[2,64,256]{2,1,0:T(8,128)(2,1)S(1)}, u32[]{:S(2)}, u32[]{:S(2)}) collective-permute-start(bf16[2,64,256]{2,1,0:T(8,128)(2,1)S(1)} %pair_up.1.args_0_), channel_id=1, source_target_pairs={{0,48},{16,32},{32,16},{48,0},{1,49},{17,33},{33,17},{49,1},{2,50}... | collective-permute-start | bytes 196616 | tf_op jit(solution)/shard_map/ppermute | solution.py:385
  11.8 5.8 %collective-permute-start.3 = (bf16[2,64,256]{2,1,0:T(8,128)(2,1)S(1)}, bf16[2,64,256]{2,1,0:T(8,128)(2,1)S(1)}, u32[]{:S(2)}, u32[]{:S(2)}) collective-permute-start(bf16[2,64,256]{2,1,0:T(8,128)(2,1)S(1)} %pair_up.1.args_0_), channel_id=1, source_target_pairs={{0,32},{16,48},{32,0},{48,16},{1,33},{17,49},{33,1},{49,17},{2,34}... | collective-permute-start | bytes 196616 | tf_op jit(solution)/shard_map/ppermute | solution.py:385
  19.8 5.5 %copy-start.1 = (f32[64]{0:T(128)S(1)}, f32[64]{0:T(128)}, u32[]{:S(2)}) copy-start(f32[64]{0:T(128)} %param.9) | copy-start | bytes 772
  19.8 13.6 %all-to-all-start = ((bf16[8,2,128,128]{3,2,1,0:T(8,128)(2,1)}), bf16[8,2,128,128]{3,2,1,0:T(8,128)(2,1)S(1)}, u32[]{:S(2)}, u32[]{:S(2)}) async-start(bf16[8,2,128,128]{3,2,1,0:T(8,128)(2,1)} %correlate.3), calls=%async_computation | async-start | bytes 1048576 | tf_op jit(solution)/shard_map/all_to_all | solution.py:388
  25.3 1.2 %collective-permute-start.5 = (f32[64]{0:T(128)S(1)}, f32[64]{0:T(128)S(1)}, u32[]{:S(2)}, u32[]{:S(2)}) collective-permute-start(f32[64]{0:T(128)S(1)} %copy-done.1), channel_id=1, source_target_pairs={{0,8},{8,0},{1,9},{9,1},{2,10},{10,2},{3,11},{11,3},{4,12},{12,4},... | collective-permute-start | bytes 776 | tf_op jit(solution)/shard_map/ppermute | solution.py:375
  33.9 1.2 %collective-permute-start.6 = (f32[2,16,128]{2,1,0:T(8,128)S(1)}, f32[2,16,128]{2,1,0:T(8,128)S(1)}, u32[]{:S(2)}, u32[]{:S(2)}) collective-permute-start(f32[2,16,128]{2,1,0:T(8,128)S(1)} %get-tuple-element.8.a_ref), channel_id=1, source_target_pairs={{0,8},{8,0},{1,9},{9,1},{2,10},{10,2},{3,11},{11,3},{4,12},{12,4},... | collective-permute-start | bytes 49160 | tf_op jit(solution)/shard_map/ppermute | solution.py:392

commit v8 on v7

--- a/solution.py
+++ b/solution.py
@@ -11,6 +11,7 @@
 LANES = 128
 N1 = 4
 N2 = 8
+FAR_FIRST = (0, 2, 1, 3)
 
 
 def spec(space=VM):
@@ -115,19 +116,20 @@
     )(own, here(other))
 
 
-def pair_up(mine, theirs, halves):
-    def body(a_ref, b_ref, _, out_ref):
+def pair_up(mine, theirs, *others):
+    def body(a_ref, b_ref, *refs):
+        out_ref = refs[-1]
         out_ref[0] = a_ref[...]
         out_ref[1] = b_ref[...]
 
     return pl.pallas_call(
         body,
         out_shape=VM((2,) + mine.shape, BF),
-        in_specs=[spec()] * 3,
+        in_specs=[spec()] * (2 + len(others)),
         out_specs=spec(),
         compiler_params=params(),
         name="pair_up",
-    )(here(mine), here(theirs), here(halves))
+    )(here(mine), here(theirs), *[here(o) for o in others])
 
 
 def rotate_images(x_ref, r, nb, step):
@@ -326,7 +328,7 @@
         place = me_ref[0] // 2
         y, z = place // nz, place % nz
         for slot in range(owners):
-            dz, dy = (0, 1, 3, 2)[slot // ny], slot % ny
+            dz, dy = FAR_FIRST[slot // ny], slot % ny
             out_ref[(y ^ dy) * nz + (z ^ dz)] = whole[slot]
 
     return pl.pallas_call(
@@ -379,8 +381,8 @@
         mine = pick_block(me, block_owner, class_gain, ref_store[0])
         theirs = lax.ppermute(mine, "yh", swap)
         halves = halve_images(images, other, nb)
-        refs = [pair_up(mine, theirs, halves)]
-        for d in (1, 3, 2):
+        refs = [pair_up(mine, theirs, halves, other_precision)]
+        for d in FAR_FIRST[1:]:
             ring = [(i, i ^ d) for i in range(nz)]
             refs.append(lax.ppermute(refs[0], "z", ring))
         early = correlate(halves, refs[:2], nb, rot)

time: 64.9 us -> 64.9 us (level)
    all_to_all x1, waiting for transfers between devices: 6.85 us -> 8.02 us  [shards(): scores = lax.all_to_all(scores, 'blk', 0, 0)]
    ppermute x1, waiting for transfers between devices: 1.07 us -> 0.01 us  [shards(): other_precision = lax.ppermute(precision, 'core', swap)]
    ppermute x3, waiting for transfers between devices: 3.19 us -> 3.96 us  [shards(): refs.append(lax.ppermute(refs[0], 'z', ring))]
where the time goes in v8:
time: 64.9 us; the launch traced here: 64.6 us
  blocking collectives  26.2 us (40%)
  starting transfers between devices  14 us (22%)
  waiting for transfers between devices  13.7 us (21%)
  Pallas kernels  10.4 us (16%)
    all_to_all x1, blocking collectives, shards(): totals = lax.all_to_all(totals, ('yh', 'z'), 0, 0)  13.1 us
    all_to_all x1, blocking collectives, shards(): weights = lax.all_to_all(weights, 'blk', 0, 0)  13.1 us
    all_to_all x1, waiting for transfers between devices, shards(): scores = lax.all_to_all(scores, 'blk', 0, 0)  8.02 us
    all_to_all x1, starting transfers between devices, shards(): scores = lax.all_to_all(scores, 'blk', 0, 0)  5.31 us
    ppermute x3, starting transfers between devices, shards(): refs.append(lax.ppermute(refs[0], 'z', ring))  5.01 us
    ppermute x3, waiting for transfers between devices, shards(): refs.append(lax.ppermute(refs[0], 'z', ring))  3.96 us
    pallas_call x2, Pallas kernels, correlate(): pl.pallas_call(body, out_shape=out_shape((nb, tiles, 2 * rows, LANES), BF...  3.8 us
    ppermute x1, starting transfers between devices, shards(): theirs = lax.ppermute(mine, 'yh', swap)  3.39 us
  transfers between devices with their start and end apart: 8, of which 6 were waited for; matrix products, arithmetic and copies ran while one was open for 0% of the time, Pallas kernels for 7%

profile of v8, /device:TPU:0, one launch (start us, length us, event | category | flops | bytes accessed | tf_op | source)
XLA Modules:
  0.0 64.6 jit_solution(7062568846832940431)
XLA Ops:
  0.0 0.0 copy-start
  0.0 0.0 collective-permute-start
  0.0 0.0 copy-start.1
  0.0 1.7 %pick_block.1.a_ref = bf16[64,256]{1,0:T(8,128)(2,1)S(1)} custom-call(s32[1]{0:T(128)} %bitcast.me_ref, s32[16]{0:T(128)} %owner_ref.1, f32[64]{0:T(128)} %gain_ref.1, bf16[16,4,16,256]{3,2,1,0:T(8,128)(2,1)} %bitcast.4), custom_call_target="tpu_custom_call" | custom-call | tf_op jit(solution)/shard_map/pick_block/pallas_call | solution.py:81
  1.7 3.4 %collective-permute-start.1 = (bf16[64,256]{1,0:T(8,128)(2,1)S(1)}, bf16[64,256]{1,0:T(8,128)(2,1)S(1)}, u32[]{:S(2)}, u32[]{:S(2)}) collective-permute-start(bf16[64,256]{1,0:T(8,128)(2,1)S(1)} %pick_block.1.a_ref), channel_id=1, source_target_pairs={{0,64},{64,0},{1,65},{65,1},{2,66},{66,2},{3,67},{67,3},{4,68},{68... | collective-permute-start | bytes 98312 | tf_op jit(solution)/shard_map/ppermute | solution.py:382
  5.1 0.0 copy-done.1
  5.1 0.2 collective-permute-start.2
  5.3 0.0 collective-permute-done.other_ref
  5.3 0.0 copy-done
  5.3 1.3 %halve_images.1.refs_0_.x_ref = bf16[2,16,128,128]{3,2,1,0:T(8,128)(2,1)S(1)} custom-call(bf16[64,16,256]{2,1,0:T(8,128)(2,1)S(1)} %copy-done, bf16[64,16,256]{2,1,0:T(8,128)(2,1)S(1)} %collective-permute-done.other_ref), custom_call_target="tpu_custom_call" | custom-call | tf_op jit(solution)/shard_map/halve_images/pallas_call | solution.py:108
  6.6 0.0 collective-permute-done.2.refs_1_
  6.7 0.5 collective-permute-done.1.b_ref
  7.2 4.0 %collective-permute-start.5 = (bf16[2,64,256]{2,1,0:T(8,128)(2,1)S(1)}, bf16[2,64,256]{2,1,0:T(8,128)(2,1)S(1)}, u32[]{:S(2)}, u32[]{:S(2)}) collective-permute-start(bf16[2,64,256]{2,1,0:T(8,128)(2,1)S(1)} %pair_up.1.args_0_), channel_id=1, source_target_pairs={{0,32},{16,48},{32,0},{48,16},{1,33},{17,49},{33,1},{49,17},{2,34}... | collective-permute-start | bytes 196616 | tf_op jit(solution)/shard_map/ppermute | solution.py:387
  11.2 1.0 %collective-permute-start.3 = (bf16[2,64,256]{2,1,0:T(8,128)(2,1)S(1)}, bf16[2,64,256]{2,1,0:T(8,128)(2,1)S(1)}, u32[]{:S(2)}, u32[]{:S(2)}) collective-permute-start(bf16[2,64,256]{2,1,0:T(8,128)(2,1)S(1)} %pair_up.1.args_0_), channel_id=1, source_target_pairs={{0,16},{16,0},{32,48},{48,32},{1,17},{17,1},{33,49},{49,33},{2,18}... | collective-permute-start | bytes 196616 | tf_op jit(solution)/shard_map/ppermute | solution.py:387
  12.2 0.0 collective-permute-start.4
  12.2 1.3 %collective-permute-done.5.args_1_ = bf16[2,64,256]{2,1,0:T(8,128)(2,1)S(1)} collective-permute-done((bf16[2,64,256]{2,1,0:T(8,128)(2,1)S(1)}, bf16[2,64,256]{2,1,0:T(8,128)(2,1)S(1)}, u32[]{:S(2)}, u32[]{:S(2)}) %collective-permute-start.5) | collective-permute-done | bytes 65568 | tf_op jit(solution)/shard_map/ppermute | solution.py:387
  13.5 1.5 %correlate.2.args_2_ = bf16[8,1,128,128]{3,2,1,0:T(8,128)(2,1)S(1)} custom-call(bf16[2,16,128,128]{3,2,1,0:T(8,128)(2,1)S(1)} %halve_images.1.refs_0_.x_ref, bf16[2,64,256]{2,1,0:T(8,128)(2,1)S(1)} %pair_up.1.args_0_, bf16[2,64,256]{2,1,0:T(8,128)(2,1)S(1)} %collective-permute-done.5.args_1_), custom_call_target="tpu_custom_call" | custom-call | tf_op jit(solution)/shard_map/correlate/pallas_call | solution.py:195
  15.0 0.5 collective-permute-done.3.args_0_
  15.5 2.2 %collective-permute-done.4.args_1_ = bf16[2,64,256]{2,1,0:T(8,128)(2,1)S(1)} collective-permute-done((bf16[2,64,256]{2,1,0:T(8,128)(2,1)S(1)}, bf16[2,64,256]{2,1,0:T(8,128)(2,1)S(1)}, u32[]{:S(2)}, u32[]{:S(2)}) %collective-permute-start.4) | collective-permute-done | bytes 65568 | tf_op jit(solution)/shard_map/ppermute | solution.py:387
  17.7 2.3 %correlate.3 = bf16[8,2,128,128]{3,2,1,0:T(8,128)(2,1)} custom-call(bf16[2,16,128,128]{3,2,1,0:T(8,128)(2,1)S(1)} %halve_images.1.refs_0_.x_ref, bf16[2,64,256]{2,1,0:T(8,128)(2,1)S(1)} %collective-permute-done.3.args_0_, bf16[2,64,256]{2,1,0:T(8,128)(2,1)S(1)} %collective-permute-done.4.args_1_, bf16[8,1,128,128]{3,2,1,0:T(8,128)(2,1)S(1)} %correlate.2.args_2_), custom_call_target="tpu_custom_call" | custom-call | tf_op jit(solution)/shard_map/correlate/pallas_call | solution.py:195
  20.0 5.3 %all-to-all-start = ((bf16[8,2,128,128]{3,2,1,0:T(8,128)(2,1)}), bf16[8,2,128,128]{3,2,1,0:T(8,128)(2,1)S(1)}, u32[]{:S(2)}, u32[]{:S(2)}) async-start(bf16[8,2,128,128]{3,2,1,0:T(8,128)(2,1)} %correlate.3), calls=%async_computation | async-start | bytes 1048576 | tf_op jit(solution)/shard_map/all_to_all | solution.py:390
  25.3 0.1 reshape.9.a_ref
  25.4 0.1 reshape.10.b_ref
  25.5 8.0 %all-to-all-done.x_ref = bf16[8,2,128,128]{3,2,1,0:T(8,128)(2,1)S(1)} async-done(((bf16[8,2,128,128]{3,2,1,0:T(8,128)(2,1)}), bf16[8,2,128,128]{3,2,1,0:T(8,128)(2,1)S(1)}, u32[]{:S(2)}, u32[]{:S(2)}) %all-to-all-start) | async-done | bytes 524320 | tf_op jit(solution)/shard_map/all_to_all | solution.py:390
  33.5 0.4 local_softmax.1
  33.9 0.1 collective-permute-start.6
  33.9 1.2 %collective-permute-done.6.b_ref = f32[2,16,128]{2,1,0:T(8,128)S(1)} collective-permute-done((f32[2,16,128]{2,1,0:T(8,128)S(1)}, f32[2,16,128]{2,1,0:T(8,128)S(1)}, u32[]{:S(2)}, u32[]{:S(2)}) %collective-permute-start.6) | collective-permute-done | bytes 16416 | tf_op jit(solution)/shard_map/ppermute | solution.py:394
  35.1 0.1 normalize.1
  35.3 13.1 %all_to_all.15.w_ref = bf16[8,256,128]{2,1,0:T(8,128)(2,1)S(1)} all-to-all(bf16[8,256,128]{2,1,0:T(8,128)(2,1)S(1)} %normalize.1), channel_id=1, replica_groups=mesh['yh'=2,'z'=4,'core'=2,'blk'=8] {'blk'}, dimensions={0} | all-to-all | bytes 1048576 | tf_op jit(solution)/shard_map/all_to_all | solution.py:396
  48.4 2.4 %accumulate.1 = bf16[8,64,256]{2,1,0:T(8,128)(2,1)S(1)} custom-call(s32[1]{0:T(128)} %bitcast.me_ref, bf16[8,256,128]{2,1,0:T(8,128)(2,1)S(1)} %all_to_all.15.w_ref, bf16[2,16,128,128]{3,2,1,0:T(8,128)(2,1)S(1)} %halve_images.1.refs_0_.x_ref), custom_call_target="tpu_custom_call" | custom-call | tf_op jit(solution)/shard_map/accumulate/pallas_call | solution.py:334
  50.8 13.1 %all_to_all.16.x_ref = bf16[8,64,256]{2,1,0:T(8,128)(2,1)S(1)} all-to-all(bf16[8,64,256]{2,1,0:T(8,128)(2,1)S(1)} %accumulate.1), channel_id=1, replica_groups=mesh['yh'=2,'z'=4,'core'=2,'blk'=8] {'yh','z'}, dimensions={0} | all-to-all | bytes 524288 | tf_op jit(solution)/shard_map/all_to_all | solution.py:398
  63.9 0.7 %add_up.1 = f32[64,256]{1,0:T(8,128)} custom-call(bf16[8,64,256]{2,1,0:T(8,128)(2,1)S(1)} %all_to_all.16.x_ref), custom_call_target="tpu_custom_call" | custom-call | tf_op jit(solution)/shard_map/add_up/pallas_call | solution.py:355
  (1 shorter events, 0.0 us)
Async XLA Ops:
  0.0 5.3 %copy-start = (bf16[64,16,256]{2,1,0:T(8,128)(2,1)S(1)}, bf16[64,16,256]{2,1,0:T(8,128)(2,1)}, u32[]{:S(2)}) copy-start(bf16[64,16,256]{2,1,0:T(8,128)(2,1)} %own_ref.1) | copy-start | bytes 1572868
  0.0 5.3 %collective-permute-start = (bf16[64,16,256]{2,1,0:T(8,128)(2,1)}, bf16[64,16,256]{2,1,0:T(8,128)(2,1)S(1)}, u32[]{:S(2)}, u32[]{:S(2)}) collective-permute-start(bf16[64,16,256]{2,1,0:T(8,128)(2,1)} %own_ref.1), channel_id=1, source_target_pairs={{0,8},{8,0},{1,9},{9,1},{2,10},{10,2},{3,11},{11,3},{4,12},{12,4},... | collective-permute-start | bytes 1572872 | tf_op jit(solution)/shard_map/ppermute | solution.py:376
  0.0 5.1 %copy-start.1 = (f32[64]{0:T(128)S(1)}, f32[64]{0:T(128)}, u32[]{:S(2)}) copy-start(f32[64]{0:T(128)} %param.9) | copy-start | bytes 772
  1.7 5.5 %collective-permute-start.1 = (bf16[64,256]{1,0:T(8,128)(2,1)S(1)}, bf16[64,256]{1,0:T(8,128)(2,1)S(1)}, u32[]{:S(2)}, u32[]{:S(2)}) collective-permute-start(bf16[64,256]{1,0:T(8,128)(2,1)S(1)} %pick_block.1.a_ref), channel_id=1, source_target_pairs={{0,64},{64,0},{1,65},{65,1},{2,66},{66,2},{3,67},{67,3},{4,68},{68... | collective-permute-start | bytes 98312 | tf_op jit(solution)/shard_map/ppermute | solution.py:382
  5.1 1.6 %collective-permute-start.2 = (f32[64]{0:T(128)S(1)}, f32[64]{0:T(128)S(1)}, u32[]{:S(2)}, u32[]{:S(2)}) collective-permute-start(f32[64]{0:T(128)S(1)} %copy-done.1), channel_id=1, source_target_pairs={{0,8},{8,0},{1,9},{9,1},{2,10},{10,2},{3,11},{11,3},{4,12},{12,4},... | collective-permute-start | bytes 776 | tf_op jit(solution)/shard_map/ppermute | solution.py:377
  7.2 6.3 %collective-permute-start.5 = (bf16[2,64,256]{2,1,0:T(8,128)(2,1)S(1)}, bf16[2,64,256]{2,1,0:T(8,128)(2,1)S(1)}, u32[]{:S(2)}, u32[]{:S(2)}) collective-permute-start(bf16[2,64,256]{2,1,0:T(8,128)(2,1)S(1)} %pair_up.1.args_0_), channel_id=1, source_target_pairs={{0,32},{16,48},{32,0},{48,16},{1,33},{17,49},{33,1},{49,17},{2,34}... | collective-permute-start | bytes 196616 | tf_op jit(solution)/shard_map/ppermute | solution.py:387
  11.2 4.3 %collective-permute-start.3 = (bf16[2,64,256]{2,1,0:T(8,128)(2,1)S(1)}, bf16[2,64,256]{2,1,0:T(8,128)(2,1)S(1)}, u32[]{:S(2)}, u32[]{:S(2)}) collective-permute-start(bf16[2,64,256]{2,1,0:T(8,128)(2,1)S(1)} %pair_up.1.args_0_), channel_id=1, source_target_pairs={{0,16},{16,0},{32,48},{48,32},{1,17},{17,1},{33,49},{49,33},{2,18}... | collective-permute-start | bytes 196616 | tf_op jit(solution)/shard_map/ppermute | solution.py:387
  12.2 5.5 %collective-permute-start.4 = (bf16[2,64,256]{2,1,0:T(8,128)(2,1)S(1)}, bf16[2,64,256]{2,1,0:T(8,128)(2,1)S(1)}, u32[]{:S(2)}, u32[]{:S(2)}) collective-permute-start(bf16[2,64,256]{2,1,0:T(8,128)(2,1)S(1)} %pair_up.1.args_0_), channel_id=1, source_target_pairs={{0,48},{16,32},{32,16},{48,0},{1,49},{17,33},{33,17},{49,1},{2,50}... | collective-permute-start | bytes 196616 | tf_op jit(solution)/shard_map/ppermute | solution.py:387
  20.0 13.5 %all-to-all-start = ((bf16[8,2,128,128]{3,2,1,0:T(8,128)(2,1)}), bf16[8,2,128,128]{3,2,1,0:T(8,128)(2,1)S(1)}, u32[]{:S(2)}, u32[]{:S(2)}) async-start(bf16[8,2,128,128]{3,2,1,0:T(8,128)(2,1)} %correlate.3), calls=%async_computation | async-start | bytes 1048576 | tf_op jit(solution)/shard_map/all_to_all | solution.py:390
  33.9 1.2 %collective-permute-start.6 = (f32[2,16,128]{2,1,0:T(8,128)S(1)}, f32[2,16,128]{2,1,0:T(8,128)S(1)}, u32[]{:S(2)}, u32[]{:S(2)}) collective-permute-start(f32[2,16,128]{2,1,0:T(8,128)S(1)} %get-tuple-element.8.a_ref), channel_id=1, source_target_pairs={{0,8},{8,0},{1,9},{9,1},{2,10},{10,2},{3,11},{11,3},{4,12},{12,4},... | collective-permute-start | bytes 49160 | tf_op jit(solution)/shard_map/ppermute | solution.py:394

commit v9 on v8

--- a/solution.py
+++ b/solution.py
@@ -5,13 +5,14 @@
 from jax.experimental.pallas import tpu as pltpu
 from jax.sharding import Mesh, PartitionSpec as P
 
+
 BF = jnp.bfloat16
 F32 = jnp.float32
 VM = pltpu.VMEM
 LANES = 128
 N1 = 4
 N2 = 8
-FAR_FIRST = (0, 2, 1, 3)
+PARTNERS = (0, 1, 3, 2)
 
 
 def spec(space=VM):
@@ -144,7 +145,7 @@
     ]
 
 
-def correlate(images, refs, nb, step, before=()):
+def correlate(images, refs, nb, step, tile, tiles, before=()):
     _, cycles, particles, _ = images.shape
     total = N1 * particles
     rows = total // nb
@@ -152,16 +153,10 @@
     classes = len(refs) * near * far // cycles
     cols = N2 * classes
     angles = 2 * LANES
-    first = sum(b.shape[1] for b in before)
-    tiles = first + cols // LANES
 
     def body(x_ref, *args):
-        r_refs, args = args[: len(refs)], args[len(refs) :]
-        b_refs, (out_ref, scr, rr, x) = args[: len(before)], args[len(before) :]
-        at = 0
-        for b_ref in b_refs:
-            out_ref[:, at : at + b_ref.shape[1]] = b_ref[...]
-            at += b_ref.shape[1]
+        r_refs, (out_ref, scr, rr, x, o, sems) = args[: len(refs)], args[-6:]
+        copies = []
         blocks = [r_ref[d].astype(F32) for r_ref in r_refs for d in range(near)]
         fill(scr, jnp.concatenate(blocks, axis=0))
         square = jnp.zeros((classes, LANES), F32)
@@ -186,25 +181,30 @@
             )
             if i == 0:
                 part = part - norm
-            for t in range(cols // LANES):
-                tile = part[:, t * LANES : (t + 1) * LANES].astype(BF)
-                at = slice(i * rows, (i + 1) * rows)
-                out_ref[:, first + t, at, :] = tile.reshape(nb, rows, LANES)
-
-    out_shape = jax.ShapeDtypeStruct if before else VM
-    return pl.pallas_call(
-        body,
-        out_shape=out_shape((nb, tiles, 2 * rows, LANES), BF),
-        in_specs=[spec()] * (1 + len(refs) + len(before)),
-        out_specs=spec(),
+            at = slice(i * rows, (i + 1) * rows)
+            o[:, at, :] = part.astype(BF).reshape(nb, rows, LANES)
+            copy = pltpu.make_async_copy(o.at[:, at, :], out_ref.at[:, tile, at, :], sems.at[i])
+            copy.start()
+            copies.append(copy)
+        for copy in copies:
+            copy.wait()
+
+    return pl.pallas_call(
+        body,
+        out_shape=pltpu.HBM((nb, tiles, 2 * rows, LANES), BF),
+        in_specs=[spec()] * (1 + len(refs)) + [spec(pltpu.HBM)] * len(before),
+        out_specs=spec(pltpu.HBM),
+        input_output_aliases={1 + len(refs): 0} if before else {},
         scratch_shapes=[
             VM((2, classes * cycles, LANES), F32),
             VM((2, cycles, cols, LANES), BF),
             VM((2, cycles, total, LANES), BF),
+            VM((nb, 2 * rows, LANES), BF),
+            pltpu.SemaphoreType.DMA((2,)),
         ],
         compiler_params=params(),
         name="correlate",
-    )(here(images), *[here(r) for r in (*refs, *before)])
+    )(here(images), *[here(r) for r in refs], *[away(b) for b in before])
 
 
 def local_softmax(me, scores, precision, others):
@@ -328,7 +328,7 @@
         place = me_ref[0] // 2
         y, z = place // nz, place % nz
         for slot in range(owners):
-            dz, dy = FAR_FIRST[slot // ny], slot % ny
+            dz, dy = PARTNERS[slot // ny], slot % ny
             out_ref[(y ^ dy) * nz + (z ^ dz)] = whole[slot]
 
     return pl.pallas_call(
@@ -382,11 +382,11 @@
         theirs = lax.ppermute(mine, "yh", swap)
         halves = halve_images(images, other, nb)
         refs = [pair_up(mine, theirs, halves, other_precision)]
-        for d in FAR_FIRST[1:]:
+        for d in PARTNERS[1:]:
             ring = [(i, i ^ d) for i in range(nz)]
             refs.append(lax.ppermute(refs[0], "z", ring))
-        early = correlate(halves, refs[:2], nb, rot)
-        scores = correlate(halves, refs[2:], nb, rot, (early,))
+        scores = correlate(halves, refs[:2], nb, rot, 0, 2)
+        scores = correlate(halves, refs[2:], nb, rot, 1, 2, (scores,))
         scores = lax.all_to_all(scores, "blk", 0, 0)
         e, stats = local_softmax(
             j, scores, precision.reshape(nb, half), other_precision.reshape(nb, half)

time: 64.9 us -> 64.8 us (level)
  waiting for transfers between devices: 13.7 us -> 12.2 us
  Pallas kernels: 10.4 us -> 11.1 us
    ppermute x3, waiting for transfers between devices: 3.96 us -> 2.44 us  [shards(): refs.append(lax.ppermute(refs[0], 'z', ring))]
    pallas_call x2, Pallas kernels: 3.8 us -> 4.53 us  [correlate(): pl.pallas_call(body, out_shape=pltpu.HBM((nb, tiles, 2 * rows, LANES), BF...]
  transfers between devices with their start and end apart: 8 -> 8, of which waited for: 6 -> 4; matrix products, arithmetic and copies ran while one was open for 0% -> 0% of each run, Pallas kernels for 7% -> 8%
where the time goes in v9:
time: 64.8 us; the launch traced here: 64.5 us
  blocking collectives  26.3 us (41%)
  starting transfers between devices  14.6 us (23%)
  waiting for transfers between devices  12.2 us (19%)
  Pallas kernels  11.1 us (17%)
    all_to_all x1, blocking collectives, shards(): totals = lax.all_to_all(totals, ('yh', 'z'), 0, 0)  13.2 us
    all_to_all x1, blocking collectives, shards(): weights = lax.all_to_all(weights, 'blk', 0, 0)  13.1 us
    all_to_all x1, waiting for transfers between devices, shards(): scores = lax.all_to_all(scores, 'blk', 0, 0)  8.02 us
    ppermute x3, starting transfers between devices, shards(): refs.append(lax.ppermute(refs[0], 'z', ring))  5.62 us
    all_to_all x1, starting transfers between devices, shards(): scores = lax.all_to_all(scores, 'blk', 0, 0)  5.32 us
    pallas_call x2, Pallas kernels, correlate(): pl.pallas_call(body, out_shape=pltpu.HBM((nb, tiles, 2 * rows, LANES), BF...  4.53 us
    ppermute x1, starting transfers between devices, shards(): theirs = lax.ppermute(mine, 'yh', swap)  3.39 us
    ppermute x3, waiting for transfers between devices, shards(): refs.append(lax.ppermute(refs[0], 'z', ring))  2.44 us
  transfers between devices with their start and end apart: 8, of which 4 were waited for; matrix products, arithmetic and copies ran while one was open for 0% of the time, Pallas kernels for 8%

profile of v9, /device:TPU:0, one launch (start us, length us, event | category | flops | bytes accessed | tf_op | source)
XLA Modules:
  0.0 64.5 jit_solution(7717858521907891502)
XLA Ops:
  0.0 0.0 copy-start
  0.0 0.0 collective-permute-start
  0.0 0.0 copy-start.1
  0.0 1.7 %pick_block.1.a_ref = bf16[64,256]{1,0:T(8,128)(2,1)S(1)} custom-call(s32[1]{0:T(128)} %bitcast.me_ref, s32[16]{0:T(128)} %owner_ref.1, f32[64]{0:T(128)} %gain_ref.1, bf16[16,4,16,256]{3,2,1,0:T(8,128)(2,1)} %bitcast.4), custom_call_target="tpu_custom_call" | custom-call | tf_op jit(solution)/shard_map/pick_block/pallas_call | solution.py:82
  1.7 3.4 %collective-permute-start.1 = (bf16[64,256]{1,0:T(8,128)(2,1)S(1)}, bf16[64,256]{1,0:T(8,128)(2,1)S(1)}, u32[]{:S(2)}, u32[]{:S(2)}) collective-permute-start(bf16[64,256]{1,0:T(8,128)(2,1)S(1)} %pick_block.1.a_ref), channel_id=1, source_target_pairs={{0,64},{64,0},{1,65},{65,1},{2,66},{66,2},{3,67},{67,3},{4,68},{68... | collective-permute-start | bytes 98312 | tf_op jit(solution)/shard_map/ppermute | solution.py:382
  5.1 0.0 copy-done.1
  5.1 0.2 collective-permute-start.2
  5.3 0.0 collective-permute-done.other_ref
  5.3 0.0 copy-done
  5.3 1.3 %halve_images.1.refs_0_.x_ref = bf16[2,16,128,128]{3,2,1,0:T(8,128)(2,1)S(1)} custom-call(bf16[64,16,256]{2,1,0:T(8,128)(2,1)S(1)} %copy-done, bf16[64,16,256]{2,1,0:T(8,128)(2,1)S(1)} %collective-permute-done.other_ref), custom_call_target="tpu_custom_call" | custom-call | tf_op jit(solution)/shard_map/halve_images/pallas_call | solution.py:109
  6.6 0.0 collective-permute-done.2.refs_1_
  6.7 0.5 collective-permute-done.1.b_ref
  7.2 2.0 %collective-permute-start.5 = (bf16[2,64,256]{2,1,0:T(8,128)(2,1)S(1)}, bf16[2,64,256]{2,1,0:T(8,128)(2,1)S(1)}, u32[]{:S(2)}, u32[]{:S(2)}) collective-permute-start(bf16[2,64,256]{2,1,0:T(8,128)(2,1)S(1)} %pair_up.1.args_0_), channel_id=1, source_target_pairs={{0,16},{16,0},{32,48},{48,32},{1,17},{17,1},{33,49},{49,33},{2,18}... | collective-permute-start | bytes 196616 | tf_op jit(solution)/shard_map/ppermute | solution.py:387
  9.2 2.5 %collective-permute-start.3 = (bf16[2,64,256]{2,1,0:T(8,128)(2,1)S(1)}, bf16[2,64,256]{2,1,0:T(8,128)(2,1)S(1)}, u32[]{:S(2)}, u32[]{:S(2)}) collective-permute-start(bf16[2,64,256]{2,1,0:T(8,128)(2,1)S(1)} %pair_up.1.args_0_), channel_id=1, source_target_pairs={{0,48},{16,32},{32,16},{48,0},{1,49},{17,33},{33,17},{49,1},{2,50}... | collective-permute-start | bytes 196616 | tf_op jit(solution)/shard_map/ppermute | solution.py:387
  11.8 1.1 %collective-permute-start.4 = (bf16[2,64,256]{2,1,0:T(8,128)(2,1)S(1)}, bf16[2,64,256]{2,1,0:T(8,128)(2,1)S(1)}, u32[]{:S(2)}, u32[]{:S(2)}) collective-permute-start(bf16[2,64,256]{2,1,0:T(8,128)(2,1)S(1)} %pair_up.1.args_0_), channel_id=1, source_target_pairs={{0,32},{16,48},{32,0},{48,16},{1,33},{17,49},{33,1},{49,17},{2,34}... | collective-permute-start | bytes 196616 | tf_op jit(solution)/shard_map/ppermute | solution.py:387
  12.8 0.0 collective-permute-done.5.args_1_
  12.8 2.3 %correlate.2.args_2_ = bf16[8,2,128,128]{3,2,1,0:T(8,128)(2,1)} custom-call(bf16[2,16,128,128]{3,2,1,0:T(8,128)(2,1)S(1)} %halve_images.1.refs_0_.x_ref, bf16[2,64,256]{2,1,0:T(8,128)(2,1)S(1)} %pair_up.1.args_0_, bf16[2,64,256]{2,1,0:T(8,128)(2,1)S(1)} %collective-permute-done.5.args_1_), custom_call_target="tpu_custom_call" | custom-call | tf_op jit(solution)/shard_map/correlate/pallas_call | solution.py:192
  15.1 0.0 collective-permute-done.3.args_0_
  15.1 2.4 %collective-permute-done.4.args_1_ = bf16[2,64,256]{2,1,0:T(8,128)(2,1)S(1)} collective-permute-done((bf16[2,64,256]{2,1,0:T(8,128)(2,1)S(1)}, bf16[2,64,256]{2,1,0:T(8,128)(2,1)S(1)}, u32[]{:S(2)}, u32[]{:S(2)}) %collective-permute-start.4) | collective-permute-done | bytes 65568 | tf_op jit(solution)/shard_map/ppermute | solution.py:387
  17.5 2.3 %correlate.3 = bf16[8,2,128,128]{3,2,1,0:T(8,128)(2,1)} custom-call(bf16[2,16,128,128]{3,2,1,0:T(8,128)(2,1)S(1)} %halve_images.1.refs_0_.x_ref, bf16[2,64,256]{2,1,0:T(8,128)(2,1)S(1)} %collective-permute-done.3.args_0_, bf16[2,64,256]{2,1,0:T(8,128)(2,1)S(1)} %collective-permute-done.4.args_1_, ...), custom_call_target="tpu_custom_call", output_to_operand_aliasing={{}: (3, {})} | custom-call | tf_op jit(solution)/shard_map/correlate/pallas_call | solution.py:192
  19.8 5.3 %all-to-all-start = ((bf16[8,2,128,128]{3,2,1,0:T(8,128)(2,1)}), bf16[8,2,128,128]{3,2,1,0:T(8,128)(2,1)S(1)}, u32[]{:S(2)}, u32[]{:S(2)}) async-start(bf16[8,2,128,128]{3,2,1,0:T(8,128)(2,1)} %correlate.3), calls=%async_computation | async-start | bytes 1048576 | tf_op jit(solution)/shard_map/all_to_all | solution.py:390
  25.1 0.1 reshape.9.a_ref
  25.2 0.1 reshape.10.b_ref
  25.3 8.0 %all-to-all-done.x_ref = bf16[8,2,128,128]{3,2,1,0:T(8,128)(2,1)S(1)} async-done(((bf16[8,2,128,128]{3,2,1,0:T(8,128)(2,1)}), bf16[8,2,128,128]{3,2,1,0:T(8,128)(2,1)S(1)}, u32[]{:S(2)}, u32[]{:S(2)}) %all-to-all-start) | async-done | bytes 524320 | tf_op jit(solution)/shard_map/all_to_all | solution.py:390
  33.3 0.4 local_softmax.1
  33.7 0.1 collective-permute-start.6
  33.8 1.2 %collective-permute-done.6.b_ref = f32[2,16,128]{2,1,0:T(8,128)S(1)} collective-permute-done((f32[2,16,128]{2,1,0:T(8,128)S(1)}, f32[2,16,128]{2,1,0:T(8,128)S(1)}, u32[]{:S(2)}, u32[]{:S(2)}) %collective-permute-start.6) | collective-permute-done | bytes 16416 | tf_op jit(solution)/shard_map/ppermute | solution.py:394
  35.0 0.1 normalize.1
  35.1 13.1 %all_to_all.15.w_ref = bf16[8,256,128]{2,1,0:T(8,128)(2,1)S(1)} all-to-all(bf16[8,256,128]{2,1,0:T(8,128)(2,1)S(1)} %normalize.1), channel_id=1, replica_groups=mesh['yh'=2,'z'=4,'core'=2,'blk'=8] {'blk'}, dimensions={0} | all-to-all | bytes 1048576 | tf_op jit(solution)/shard_map/all_to_all | solution.py:396
  48.2 2.4 %accumulate.1 = bf16[8,64,256]{2,1,0:T(8,128)(2,1)S(1)} custom-call(s32[1]{0:T(128)} %bitcast.me_ref, bf16[8,256,128]{2,1,0:T(8,128)(2,1)S(1)} %all_to_all.15.w_ref, bf16[2,16,128,128]{3,2,1,0:T(8,128)(2,1)S(1)} %halve_images.1.refs_0_.x_ref), custom_call_target="tpu_custom_call" | custom-call | tf_op jit(solution)/shard_map/accumulate/pallas_call | solution.py:334
  50.6 13.2 %all_to_all.16.x_ref = bf16[8,64,256]{2,1,0:T(8,128)(2,1)S(1)} all-to-all(bf16[8,64,256]{2,1,0:T(8,128)(2,1)S(1)} %accumulate.1), channel_id=1, replica_groups=mesh['yh'=2,'z'=4,'core'=2,'blk'=8] {'yh','z'}, dimensions={0} | all-to-all | bytes 524288 | tf_op jit(solution)/shard_map/all_to_all | solution.py:398
  63.8 0.7 %add_up.1 = f32[64,256]{1,0:T(8,128)} custom-call(bf16[8,64,256]{2,1,0:T(8,128)(2,1)S(1)} %all_to_all.16.x_ref), custom_call_target="tpu_custom_call" | custom-call | tf_op jit(solution)/shard_map/add_up/pallas_call | solution.py:355
  (1 shorter events, 0.0 us)
Async XLA Ops:
  0.0 5.3 %copy-start = (bf16[64,16,256]{2,1,0:T(8,128)(2,1)S(1)}, bf16[64,16,256]{2,1,0:T(8,128)(2,1)}, u32[]{:S(2)}) copy-start(bf16[64,16,256]{2,1,0:T(8,128)(2,1)} %own_ref.1) | copy-start | bytes 1572868
  0.0 5.3 %collective-permute-start = (bf16[64,16,256]{2,1,0:T(8,128)(2,1)}, bf16[64,16,256]{2,1,0:T(8,128)(2,1)S(1)}, u32[]{:S(2)}, u32[]{:S(2)}) collective-permute-start(bf16[64,16,256]{2,1,0:T(8,128)(2,1)} %own_ref.1), channel_id=1, source_target_pairs={{0,8},{8,0},{1,9},{9,1},{2,10},{10,2},{3,11},{11,3},{4,12},{12,4},... | collective-permute-start | bytes 1572872 | tf_op jit(solution)/shard_map/ppermute | solution.py:376
  0.0 5.1 %copy-start.1 = (f32[64]{0:T(128)S(1)}, f32[64]{0:T(128)}, u32[]{:S(2)}) copy-start(f32[64]{0:T(128)} %param.9) | copy-start | bytes 772
  1.7 5.5 %collective-permute-start.1 = (bf16[64,256]{1,0:T(8,128)(2,1)S(1)}, bf16[64,256]{1,0:T(8,128)(2,1)S(1)}, u32[]{:S(2)}, u32[]{:S(2)}) collective-permute-start(bf16[64,256]{1,0:T(8,128)(2,1)S(1)} %pick_block.1.a_ref), channel_id=1, source_target_pairs={{0,64},{64,0},{1,65},{65,1},{2,66},{66,2},{3,67},{67,3},{4,68},{68... | collective-permute-start | bytes 98312 | tf_op jit(solution)/shard_map/ppermute | solution.py:382
  5.1 1.6 %collective-permute-start.2 = (f32[64]{0:T(128)S(1)}, f32[64]{0:T(128)S(1)}, u32[]{:S(2)}, u32[]{:S(2)}) collective-permute-start(f32[64]{0:T(128)S(1)} %copy-done.1), channel_id=1, source_target_pairs={{0,8},{8,0},{1,9},{9,1},{2,10},{10,2},{3,11},{11,3},{4,12},{12,4},... | collective-permute-start | bytes 776 | tf_op jit(solution)/shard_map/ppermute | solution.py:377
  7.2 5.6 %collective-permute-start.5 = (bf16[2,64,256]{2,1,0:T(8,128)(2,1)S(1)}, bf16[2,64,256]{2,1,0:T(8,128)(2,1)S(1)}, u32[]{:S(2)}, u32[]{:S(2)}) collective-permute-start(bf16[2,64,256]{2,1,0:T(8,128)(2,1)S(1)} %pair_up.1.args_0_), channel_id=1, source_target_pairs={{0,16},{16,0},{32,48},{48,32},{1,17},{17,1},{33,49},{49,33},{2,18}... | collective-permute-start | bytes 196616 | tf_op jit(solution)/shard_map/ppermute | solution.py:387
  9.2 5.9 %collective-permute-start.3 = (bf16[2,64,256]{2,1,0:T(8,128)(2,1)S(1)}, bf16[2,64,256]{2,1,0:T(8,128)(2,1)S(1)}, u32[]{:S(2)}, u32[]{:S(2)}) collective-permute-start(bf16[2,64,256]{2,1,0:T(8,128)(2,1)S(1)} %pair_up.1.args_0_), channel_id=1, source_target_pairs={{0,48},{16,32},{32,16},{48,0},{1,49},{17,33},{33,17},{49,1},{2,50}... | collective-permute-start | bytes 196616 | tf_op jit(solution)/shard_map/ppermute | solution.py:387
  11.8 5.8 %collective-permute-start.4 = (bf16[2,64,256]{2,1,0:T(8,128)(2,1)S(1)}, bf16[2,64,256]{2,1,0:T(8,128)(2,1)S(1)}, u32[]{:S(2)}, u32[]{:S(2)}) collective-permute-start(bf16[2,64,256]{2,1,0:T(8,128)(2,1)S(1)} %pair_up.1.args_0_), channel_id=1, source_target_pairs={{0,32},{16,48},{32,0},{48,16},{1,33},{17,49},{33,1},{49,17},{2,34}... | collective-permute-start | bytes 196616 | tf_op jit(solution)/shard_map/ppermute | solution.py:387
  19.8 13.5 %all-to-all-start = ((bf16[8,2,128,128]{3,2,1,0:T(8,128)(2,1)}), bf16[8,2,128,128]{3,2,1,0:T(8,128)(2,1)S(1)}, u32[]{:S(2)}, u32[]{:S(2)}) async-start(bf16[8,2,128,128]{3,2,1,0:T(8,128)(2,1)} %correlate.3), calls=%async_computation | async-start | bytes 1048576 | tf_op jit(solution)/shard_map/all_to_all | solution.py:390
  33.7 1.2 %collective-permute-start.6 = (f32[2,16,128]{2,1,0:T(8,128)S(1)}, f32[2,16,128]{2,1,0:T(8,128)S(1)}, u32[]{:S(2)}, u32[]{:S(2)}) collective-permute-start(f32[2,16,128]{2,1,0:T(8,128)S(1)} %get-tuple-element.8.a_ref), channel_id=1, source_target_pairs={{0,8},{8,0},{1,9},{9,1},{2,10},{10,2},{3,11},{11,3},{4,12},{12,4},... | collective-permute-start | bytes 49160 | tf_op jit(solution)/shard_map/ppermute | solution.py:394

commit v10 on v8

--- a/solution.py
+++ b/solution.py
@@ -5,13 +5,14 @@
 from jax.experimental.pallas import tpu as pltpu
 from jax.sharding import Mesh, PartitionSpec as P
 
+
 BF = jnp.bfloat16
 F32 = jnp.float32
 VM = pltpu.VMEM
 LANES = 128
 N1 = 4
 N2 = 8
-FAR_FIRST = (0, 2, 1, 3)
+PARTNERS = (0, 1, 3, 2)
 
 
 def spec(space=VM):
@@ -62,13 +63,13 @@
     return pltpu.roll(plus, t, 1), jnp.where(lane < t, -minus, minus)
 
 
-def pick_block(me, block_owner, class_gain, ref_store):
+def pick_block(me, nb, block_owner, class_gain, ref_store):
     nblk, kb, cycles, angles = ref_store.shape
 
     def body(me_ref, owner_ref, gain_ref, store_ref, out_ref, buf, sem):
         block = jnp.int32(0)
         for b in range(nblk):
-            block = jnp.where(owner_ref[b] == me_ref[0], jnp.int32(b), block)
+            block = jnp.where(owner_ref[b] == me_ref[0] // nb, jnp.int32(b), block)
         copy = pltpu.make_async_copy(store_ref.at[block], buf, sem)
         copy.start()
         copy.wait()
@@ -152,16 +153,11 @@
     classes = len(refs) * near * far // cycles
     cols = N2 * classes
     angles = 2 * LANES
-    first = sum(b.shape[1] for b in before)
-    tiles = first + cols // LANES
 
     def body(x_ref, *args):
-        r_refs, args = args[: len(refs)], args[len(refs) :]
-        b_refs, (out_ref, scr, rr, x) = args[: len(before)], args[len(before) :]
-        at = 0
-        for b_ref in b_refs:
-            out_ref[:, at : at + b_ref.shape[1]] = b_ref[...]
-            at += b_ref.shape[1]
+        r_refs, (out_ref, scr, rr, x) = args[: len(refs)], args[-4:]
+        for t, b_ref in enumerate(args[len(refs) : -4]):
+            out_ref[:, t] = b_ref[:, 0]
         blocks = [r_ref[d].astype(F32) for r_ref in r_refs for d in range(near)]
         fill(scr, jnp.concatenate(blocks, axis=0))
         square = jnp.zeros((classes, LANES), F32)
@@ -186,15 +182,12 @@
             )
             if i == 0:
                 part = part - norm
-            for t in range(cols // LANES):
-                tile = part[:, t * LANES : (t + 1) * LANES].astype(BF)
-                at = slice(i * rows, (i + 1) * rows)
-                out_ref[:, first + t, at, :] = tile.reshape(nb, rows, LANES)
-
-    out_shape = jax.ShapeDtypeStruct if before else VM
-    return pl.pallas_call(
-        body,
-        out_shape=out_shape((nb, tiles, 2 * rows, LANES), BF),
+            at = slice(i * rows, (i + 1) * rows)
+            out_ref[:, len(before), at, :] = part.astype(BF).reshape(nb, rows, LANES)
+
+    return pl.pallas_call(
+        body,
+        out_shape=VM((nb, 1 + len(before), 2 * rows, LANES), BF),
         in_specs=[spec()] * (1 + len(refs) + len(before)),
         out_specs=spec(),
         scratch_shapes=[
@@ -224,10 +217,11 @@
             total = total + x_ref[i].astype(F32)
         total = jnp.concatenate([total[t] for t in range(tiles)], axis=1)
         plus, minus = total[:half], total[half:]
-        row = lax.broadcasted_iota(jnp.int32, (own, own), 0)
-        col = lax.broadcasted_iota(jnp.int32, (own, own), 1)
+        wide = (own, nb * own)
+        row = lax.broadcasted_iota(jnp.int32, wide, 0) + me_ref[0] % nb * own
+        mine = row == lax.broadcasted_iota(jnp.int32, wide, 1)
         scale = [
-            jnp.sum(jnp.where(row == col, ref[pl.ds(me_ref[0], 1), :], 0.0), axis=1, keepdims=True)
+            jnp.sum(jnp.where(mine, ref[...], 0.0), axis=1, keepdims=True)
             for ref in (a_ref, b_ref)
         ]
         scale = jnp.concatenate(scale * N1, axis=0) * 0.5
@@ -325,10 +319,10 @@
                 scr.at[1][rows, :] = 0.5 * (plus - minus)
         whole = jnp.concatenate([scr[0], scr[1]], axis=1)
         whole = whole.reshape(out_ref.shape).astype(BF)
-        place = me_ref[0] // 2
+        place = me_ref[0] // (2 * nb)
         y, z = place // nz, place % nz
         for slot in range(owners):
-            dz, dy = FAR_FIRST[slot // ny], slot % ny
+            dz, dy = PARTNERS[slot // ny], slot % ny
             out_ref[(y ^ dy) * nz + (z ^ dz)] = whole[slot]
 
     return pl.pallas_call(
@@ -372,24 +366,24 @@
         particles, cycles, angles = images.shape
         kb = ref_store.shape[2]
         rot = angles // (2 * N1 * N2)
-        half = particles // nb
         other = lax.ppermute(images, "core", swap)
         other_precision = lax.ppermute(precision, "core", swap)
         y, z = lax.axis_index("yh"), lax.axis_index("z")
-        me = ((y * nz + z) * 2 + lax.axis_index("core"))[None].astype(jnp.int32)
-        j = lax.axis_index("blk")[None].astype(jnp.int32)
-        mine = pick_block(me, block_owner, class_gain, ref_store[0])
+        me = ((y * nz + z) * 2 + lax.axis_index("core")) * nb + lax.axis_index("blk")
+        me = me[None].astype(jnp.int32)
+        mine = pick_block(me, nb, block_owner, class_gain, ref_store[0])
         theirs = lax.ppermute(mine, "yh", swap)
         halves = halve_images(images, other, nb)
         refs = [pair_up(mine, theirs, halves, other_precision)]
-        for d in FAR_FIRST[1:]:
+        for d in PARTNERS[1:]:
             ring = [(i, i ^ d) for i in range(nz)]
             refs.append(lax.ppermute(refs[0], "z", ring))
         early = correlate(halves, refs[:2], nb, rot)
         scores = correlate(halves, refs[2:], nb, rot, (early,))
         scores = lax.all_to_all(scores, "blk", 0, 0)
+        flat = (1, particles)
         e, stats = local_softmax(
-            j, scores, precision.reshape(nb, half), other_precision.reshape(nb, half)
+            me, scores, precision.reshape(flat), other_precision.reshape(flat)
         )
         theirs = lax.ppermute(stats, "core", swap)
         weights = normalize(e, stats, theirs, nb)

time: 64.9 us -> 64 us (0.986)
  blocking collectives: 26.2 us -> 39.1 us
  waiting for transfers between devices: 13.7 us -> 5.68 us
  starting transfers between devices: 14 us -> 9.29 us
  Pallas kernels: 10.4 us -> 9.64 us
    all_to_all x0 -> x1, blocking collectives: none -> 13.4 us  [shards(): scores = lax.all_to_all(scores, 'blk', 0, 0)]
    all_to_all x1 -> x0, waiting for transfers between devices: 8.02 us -> none  [shards(): scores = lax.all_to_all(scores, 'blk', 0, 0)]
    all_to_all x1 -> x0, starting transfers between devices: 5.31 us -> none  [shards(): scores = lax.all_to_all(scores, 'blk', 0, 0)]
    pallas_call x2, Pallas kernels: 3.8 us -> 3.02 us  [correlate(): pl.pallas_call(body, out_shape=VM((nb, 1 + len(before), 2 * rows, LANES),...]
  transfers between devices with their start and end apart: 8 -> 7, of which waited for: 6 -> 4; matrix products, arithmetic and copies ran while one was open for 0% -> 0% of each run, Pallas kernels for 7% -> 7%
where the time goes in v10:
time: 64 us; the launch traced here: 63.8 us
  blocking collectives  39.1 us (61%)
  Pallas kernels  9.64 us (15%)
  starting transfers between devices  9.29 us (15%)
  waiting for transfers between devices  5.68 us (9%)
    all_to_all x1, blocking collectives, shards(): scores = lax.all_to_all(scores, 'blk', 0, 0)  13.4 us
    all_to_all x1, blocking collectives, shards(): weights = lax.all_to_all(weights, 'blk', 0, 0)  12.9 us
    all_to_all x1, blocking collectives, shards(): totals = lax.all_to_all(totals, ('yh', 'z'), 0, 0)  12.7 us
    ppermute x3, starting transfers between devices, shards(): refs.append(lax.ppermute(refs[0], 'z', ring))  5.62 us
    ppermute x3, waiting for transfers between devices, shards(): refs.append(lax.ppermute(refs[0], 'z', ring))  3.96 us
    ppermute x1, starting transfers between devices, shards(): theirs = lax.ppermute(mine, 'yh', swap)  3.39 us
    pallas_call x2, Pallas kernels, correlate(): pl.pallas_call(body, out_shape=VM((nb, 1 + len(before), 2 * rows, LANES),...  3.02 us
    pallas_call x1, Pallas kernels, accumulate(): pl.pallas_call(body, out_shape=VM((owners, classes // owners * cycles, pa...  2.4 us
  transfers between devices with their start and end apart: 7, of which 4 were waited for; matrix products, arithmetic and copies ran while one was open for 0% of the time, Pallas kernels for 7%

profile of v10, /device:TPU:0, one launch (start us, length us, event | category | flops | bytes accessed | tf_op | source)
XLA Modules:
  0.0 63.8 jit_solution(8997431172516252637)
XLA Ops:
  0.0 0.0 copy-start
  0.0 0.0 collective-permute-start
  0.0 0.0 copy-start.1
  0.0 1.7 %pick_block.1.a_ref = bf16[64,256]{1,0:T(8,128)(2,1)S(1)} custom-call(s32[1]{0:T(128)} %bitcast.me_ref, s32[16]{0:T(128)} %owner_ref.1, f32[64]{0:T(128)} %gain_ref.1, bf16[16,4,16,256]{3,2,1,0:T(8,128)(2,1)} %bitcast.7), custom_call_target="tpu_custom_call" | custom-call | tf_op jit(solution)/shard_map/pick_block/pallas_call | solution.py:82
  1.7 3.4 %collective-permute-start.1 = (bf16[64,256]{1,0:T(8,128)(2,1)S(1)}, bf16[64,256]{1,0:T(8,128)(2,1)S(1)}, u32[]{:S(2)}, u32[]{:S(2)}) collective-permute-start(bf16[64,256]{1,0:T(8,128)(2,1)S(1)} %pick_block.1.a_ref), channel_id=1, source_target_pairs={{0,64},{64,0},{1,65},{65,1},{2,66},{66,2},{3,67},{67,3},{4,68},{68... | collective-permute-start | bytes 98312 | tf_op jit(solution)/shard_map/ppermute | solution.py:375
  5.1 0.0 copy-done.1
  5.1 0.2 collective-permute-start.2
  5.3 0.0 collective-permute-done.other_ref
  5.3 0.0 copy-done
  5.3 1.3 %halve_images.1.refs_0_.x_ref = bf16[2,16,128,128]{3,2,1,0:T(8,128)(2,1)S(1)} custom-call(bf16[64,16,256]{2,1,0:T(8,128)(2,1)S(1)} %copy-done, bf16[64,16,256]{2,1,0:T(8,128)(2,1)S(1)} %collective-permute-done.other_ref), custom_call_target="tpu_custom_call" | custom-call | tf_op jit(solution)/shard_map/halve_images/pallas_call | solution.py:109
  6.6 0.0 collective-permute-done.2.refs_1_
  6.7 0.5 collective-permute-done.1.b_ref
  7.2 2.0 %collective-permute-start.5 = (bf16[2,64,256]{2,1,0:T(8,128)(2,1)S(1)}, bf16[2,64,256]{2,1,0:T(8,128)(2,1)S(1)}, u32[]{:S(2)}, u32[]{:S(2)}) collective-permute-start(bf16[2,64,256]{2,1,0:T(8,128)(2,1)S(1)} %pair_up.1.args_0_), channel_id=1, source_target_pairs={{0,16},{16,0},{32,48},{48,32},{1,17},{17,1},{33,49},{49,33},{2,18}... | collective-permute-start | bytes 196616 | tf_op jit(solution)/shard_map/ppermute | solution.py:380
  9.2 3.6 %collective-permute-start.4 = (bf16[2,64,256]{2,1,0:T(8,128)(2,1)S(1)}, bf16[2,64,256]{2,1,0:T(8,128)(2,1)S(1)}, u32[]{:S(2)}, u32[]{:S(2)}) collective-permute-start(bf16[2,64,256]{2,1,0:T(8,128)(2,1)S(1)} %pair_up.1.args_0_), channel_id=1, source_target_pairs={{0,32},{16,48},{32,0},{48,16},{1,33},{17,49},{33,1},{49,17},{2,34}... | collective-permute-start | bytes 196616 | tf_op jit(solution)/shard_map/ppermute | solution.py:380
  12.8 0.0 collective-permute-start.3
  12.8 0.0 collective-permute-done.5.args_1_
  12.8 1.5 %correlate.2.args_2_ = bf16[8,1,128,128]{3,2,1,0:T(8,128)(2,1)S(1)} custom-call(bf16[2,16,128,128]{3,2,1,0:T(8,128)(2,1)S(1)} %halve_images.1.refs_0_.x_ref, bf16[2,64,256]{2,1,0:T(8,128)(2,1)S(1)} %pair_up.1.args_0_, bf16[2,64,256]{2,1,0:T(8,128)(2,1)S(1)} %collective-permute-done.5.args_1_), custom_call_target="tpu_custom_call" | custom-call | tf_op jit(solution)/shard_map/correlate/pallas_call | solution.py:188
  14.3 1.6 %collective-permute-done.4.args_1_ = bf16[2,64,256]{2,1,0:T(8,128)(2,1)S(1)} collective-permute-done((bf16[2,64,256]{2,1,0:T(8,128)(2,1)S(1)}, bf16[2,64,256]{2,1,0:T(8,128)(2,1)S(1)}, u32[]{:S(2)}, u32[]{:S(2)}) %collective-permute-start.4) | collective-permute-done | bytes 65568 | tf_op jit(solution)/shard_map/ppermute | solution.py:380
  15.9 2.4 %collective-permute-done.3.args_0_ = bf16[2,64,256]{2,1,0:T(8,128)(2,1)S(1)} collective-permute-done((bf16[2,64,256]{2,1,0:T(8,128)(2,1)S(1)}, bf16[2,64,256]{2,1,0:T(8,128)(2,1)S(1)}, u32[]{:S(2)}, u32[]{:S(2)}) %collective-permute-start.3) | collective-permute-done | bytes 65568 | tf_op jit(solution)/shard_map/ppermute | solution.py:380
  18.3 1.5 %correlate.3 = bf16[8,2,128,128]{3,2,1,0:T(8,128)(2,1)S(1)} custom-call(bf16[2,16,128,128]{3,2,1,0:T(8,128)(2,1)S(1)} %halve_images.1.refs_0_.x_ref, bf16[2,64,256]{2,1,0:T(8,128)(2,1)S(1)} %collective-permute-done.3.args_0_, bf16[2,64,256]{2,1,0:T(8,128)(2,1)S(1)} %collective-permute-done.4.args_1_, bf16[8,1,128,128]{3,2,1,0:T(8,128)(2,1)S(1)} %correlate.2.args_2_), custom_call_target="tpu_custom_call" | custom-call | tf_op jit(solution)/shard_map/correlate/pallas_call | solution.py:188
  19.8 13.4 %all_to_all.15.x_ref = bf16[8,2,128,128]{3,2,1,0:T(8,128)(2,1)S(1)} all-to-all(bf16[8,2,128,128]{3,2,1,0:T(8,128)(2,1)S(1)} %correlate.3), channel_id=1, replica_groups=mesh['yh'=2,'z'=4,'core'=2,'blk'=8] {'blk'}, dimensions={0} | all-to-all | bytes 1048576 | tf_op jit(solution)/shard_map/all_to_all | solution.py:383
  33.3 0.4 local_softmax.1
  33.7 0.1 collective-permute-start.6
  33.7 1.2 %collective-permute-done.6.b_ref = f32[2,16,128]{2,1,0:T(8,128)S(1)} collective-permute-done((f32[2,16,128]{2,1,0:T(8,128)S(1)}, f32[2,16,128]{2,1,0:T(8,128)S(1)}, u32[]{:S(2)}, u32[]{:S(2)}) %collective-permute-start.6) | collective-permute-done | bytes 16416 | tf_op jit(solution)/shard_map/ppermute | solution.py:388
  34.9 0.1 normalize.1
  35.0 12.9 %all_to_all.16.w_ref = bf16[8,256,128]{2,1,0:T(8,128)(2,1)S(1)} all-to-all(bf16[8,256,128]{2,1,0:T(8,128)(2,1)S(1)} %normalize.1), channel_id=1, replica_groups=mesh['yh'=2,'z'=4,'core'=2,'blk'=8] {'blk'}, dimensions={0} | all-to-all | bytes 1048576 | tf_op jit(solution)/shard_map/all_to_all | solution.py:390
  48.0 2.4 %accumulate.1 = bf16[8,64,256]{2,1,0:T(8,128)(2,1)S(1)} custom-call(s32[1]{0:T(128)} %bitcast.me_ref, bf16[8,256,128]{2,1,0:T(8,128)(2,1)S(1)} %all_to_all.16.w_ref, bf16[2,16,128,128]{3,2,1,0:T(8,128)(2,1)S(1)} %halve_images.1.refs_0_.x_ref), custom_call_target="tpu_custom_call" | custom-call | tf_op jit(solution)/shard_map/accumulate/pallas_call | solution.py:328
  50.4 12.7 %all_to_all.17.x_ref = bf16[8,64,256]{2,1,0:T(8,128)(2,1)S(1)} all-to-all(bf16[8,64,256]{2,1,0:T(8,128)(2,1)S(1)} %accumulate.1), channel_id=1, replica_groups=mesh['yh'=2,'z'=4,'core'=2,'blk'=8] {'yh','z'}, dimensions={0} | all-to-all | bytes 524288 | tf_op jit(solution)/shard_map/all_to_all | solution.py:392
  63.1 0.7 %add_up.1 = f32[64,256]{1,0:T(8,128)} custom-call(bf16[8,64,256]{2,1,0:T(8,128)(2,1)S(1)} %all_to_all.17.x_ref), custom_call_target="tpu_custom_call" | custom-call | tf_op jit(solution)/shard_map/add_up/pallas_call | solution.py:349
  (1 shorter events, 0.0 us)
Async XLA Ops:
  0.0 5.3 %copy-start = (bf16[64,16,256]{2,1,0:T(8,128)(2,1)S(1)}, bf16[64,16,256]{2,1,0:T(8,128)(2,1)}, u32[]{:S(2)}) copy-start(bf16[64,16,256]{2,1,0:T(8,128)(2,1)} %own_ref.1) | copy-start | bytes 1572868
  0.0 5.3 %collective-permute-start = (bf16[64,16,256]{2,1,0:T(8,128)(2,1)}, bf16[64,16,256]{2,1,0:T(8,128)(2,1)S(1)}, u32[]{:S(2)}, u32[]{:S(2)}) collective-permute-start(bf16[64,16,256]{2,1,0:T(8,128)(2,1)} %own_ref.1), channel_id=1, source_target_pairs={{0,8},{8,0},{1,9},{9,1},{2,10},{10,2},{3,11},{11,3},{4,12},{12,4},... | collective-permute-start | bytes 1572872 | tf_op jit(solution)/shard_map/ppermute | solution.py:369
  0.0 5.1 %copy-start.1 = (f32[64]{0:T(128)S(1)}, f32[64]{0:T(128)}, u32[]{:S(2)}) copy-start(f32[64]{0:T(128)} %param.9) | copy-start | bytes 772
  1.7 5.5 %collective-permute-start.1 = (bf16[64,256]{1,0:T(8,128)(2,1)S(1)}, bf16[64,256]{1,0:T(8,128)(2,1)S(1)}, u32[]{:S(2)}, u32[]{:S(2)}) collective-permute-start(bf16[64,256]{1,0:T(8,128)(2,1)S(1)} %pick_block.1.a_ref), channel_id=1, source_target_pairs={{0,64},{64,0},{1,65},{65,1},{2,66},{66,2},{3,67},{67,3},{4,68},{68... | collective-permute-start | bytes 98312 | tf_op jit(solution)/shard_map/ppermute | solution.py:375
  5.1 1.6 %collective-permute-start.2 = (f32[64]{0:T(128)S(1)}, f32[64]{0:T(128)S(1)}, u32[]{:S(2)}, u32[]{:S(2)}) collective-permute-start(f32[64]{0:T(128)S(1)} %copy-done.1), channel_id=1, source_target_pairs={{0,8},{8,0},{1,9},{9,1},{2,10},{10,2},{3,11},{11,3},{4,12},{12,4},... | collective-permute-start | bytes 776 | tf_op jit(solution)/shard_map/ppermute | solution.py:370
  7.2 5.6 %collective-permute-start.5 = (bf16[2,64,256]{2,1,0:T(8,128)(2,1)S(1)}, bf16[2,64,256]{2,1,0:T(8,128)(2,1)S(1)}, u32[]{:S(2)}, u32[]{:S(2)}) collective-permute-start(bf16[2,64,256]{2,1,0:T(8,128)(2,1)S(1)} %pair_up.1.args_0_), channel_id=1, source_target_pairs={{0,16},{16,0},{32,48},{48,32},{1,17},{17,1},{33,49},{49,33},{2,18}... | collective-permute-start | bytes 196616 | tf_op jit(solution)/shard_map/ppermute | solution.py:380
  9.2 6.7 %collective-permute-start.4 = (bf16[2,64,256]{2,1,0:T(8,128)(2,1)S(1)}, bf16[2,64,256]{2,1,0:T(8,128)(2,1)S(1)}, u32[]{:S(2)}, u32[]{:S(2)}) collective-permute-start(bf16[2,64,256]{2,1,0:T(8,128)(2,1)S(1)} %pair_up.1.args_0_), channel_id=1, source_target_pairs={{0,32},{16,48},{32,0},{48,16},{1,33},{17,49},{33,1},{49,17},{2,34}... | collective-permute-start | bytes 196616 | tf_op jit(solution)/shard_map/ppermute | solution.py:380
  12.8 5.5 %collective-permute-start.3 = (bf16[2,64,256]{2,1,0:T(8,128)(2,1)S(1)}, bf16[2,64,256]{2,1,0:T(8,128)(2,1)S(1)}, u32[]{:S(2)}, u32[]{:S(2)}) collective-permute-start(bf16[2,64,256]{2,1,0:T(8,128)(2,1)S(1)} %pair_up.1.args_0_), channel_id=1, source_target_pairs={{0,48},{16,32},{32,16},{48,0},{1,49},{17,33},{33,17},{49,1},{2,50}... | collective-permute-start | bytes 196616 | tf_op jit(solution)/shard_map/ppermute | solution.py:380
  33.7 1.2 %collective-permute-start.6 = (f32[2,16,128]{2,1,0:T(8,128)S(1)}, f32[2,16,128]{2,1,0:T(8,128)S(1)}, u32[]{:S(2)}, u32[]{:S(2)}) collective-permute-start(f32[2,16,128]{2,1,0:T(8,128)S(1)} %get-tuple-element.8.a_ref), channel_id=1, source_target_pairs={{0,8},{8,0},{1,9},{9,1},{2,10},{10,2},{3,11},{11,3},{4,12},{12,4},... | collective-permute-start | bytes 49160 | tf_op jit(solution)/shard_map/ppermute | solution.py:388

commit v11 on v10

--- a/solution.py
+++ b/solution.py
@@ -90,11 +90,11 @@
     )(me, block_owner, class_gain, away(ref_store))
 
 
-def halve_images(own, other, nb):
+def halve_images(own, other, nb, after):
     particles, cycles, angles = own.shape
     per = particles // nb
 
-    def body(own_ref, other_ref, out_ref, a_scr, b_scr):
+    def body(own_ref, other_ref, _, out_ref, a_scr, b_scr):
         fill(a_scr, own_ref[...].astype(F32).reshape(particles * cycles, angles))
         fill(b_scr, other_ref[...].astype(F32).reshape(particles * cycles, angles))
         for r in range(cycles):
@@ -109,28 +109,12 @@
     return pl.pallas_call(
         body,
         out_shape=VM((2, cycles, 2 * particles, LANES), BF),
-        in_specs=[spec(), spec()],
+        in_specs=[spec(), spec(), spec()],
         out_specs=spec(),
         scratch_shapes=[VM((2, particles * cycles, LANES), F32)] * 2,
         compiler_params=params(),
         name="halve_images",
-    )(own, here(other))
-
-
-def pair_up(mine, theirs, *others):
-    def body(a_ref, b_ref, *refs):
-        out_ref = refs[-1]
-        out_ref[0] = a_ref[...]
-        out_ref[1] = b_ref[...]
-
-    return pl.pallas_call(
-        body,
-        out_shape=VM((2,) + mine.shape, BF),
-        in_specs=[spec()] * (2 + len(others)),
-        out_specs=spec(),
-        compiler_params=params(),
-        name="pair_up",
-    )(here(mine), here(theirs), *[here(o) for o in others])
+    )(own, here(other), here(after))
 
 
 def rotate_images(x_ref, r, nb, step):
@@ -149,8 +133,7 @@
     _, cycles, particles, _ = images.shape
     total = N1 * particles
     rows = total // nb
-    near, far = refs[0].shape[:2]
-    classes = len(refs) * near * far // cycles
+    classes = len(refs) * refs[0].shape[0] // cycles
     cols = N2 * classes
     angles = 2 * LANES
 
@@ -158,7 +141,7 @@
         r_refs, (out_ref, scr, rr, x) = args[: len(refs)], args[-4:]
         for t, b_ref in enumerate(args[len(refs) : -4]):
             out_ref[:, t] = b_ref[:, 0]
-        blocks = [r_ref[d].astype(F32) for r_ref in r_refs for d in range(near)]
+        blocks = [r_ref[...].astype(F32) for r_ref in r_refs]
         fill(scr, jnp.concatenate(blocks, axis=0))
         square = jnp.zeros((classes, LANES), F32)
         for r in range(cycles):
@@ -322,7 +305,7 @@
         place = me_ref[0] // (2 * nb)
         y, z = place // nz, place % nz
         for slot in range(owners):
-            dz, dy = PARTNERS[slot // ny], slot % ny
+            dy, dz = slot // nz, PARTNERS[slot % nz]
             out_ref[(y ^ dy) * nz + (z ^ dz)] = whole[slot]
 
     return pl.pallas_call(
@@ -372,14 +355,16 @@
         me = ((y * nz + z) * 2 + lax.axis_index("core")) * nb + lax.axis_index("blk")
         me = me[None].astype(jnp.int32)
         mine = pick_block(me, nb, block_owner, class_gain, ref_store[0])
+        refs = []
         theirs = lax.ppermute(mine, "yh", swap)
-        halves = halve_images(images, other, nb)
-        refs = [pair_up(mine, theirs, halves, other_precision)]
-        for d in PARTNERS[1:]:
-            ring = [(i, i ^ d) for i in range(nz)]
-            refs.append(lax.ppermute(refs[0], "z", ring))
-        early = correlate(halves, refs[:2], nb, rot)
-        scores = correlate(halves, refs[2:], nb, rot, (early,))
+        for block in (mine, theirs):
+            refs.append([block])
+            for d in PARTNERS[1:]:
+                ring = [(i, i ^ d) for i in range(nz)]
+                refs[-1].append(lax.ppermute(block, "z", ring))
+        halves = halve_images(images, other, nb, other_precision)
+        early = correlate(halves, refs[0], nb, rot)
+        scores = correlate(halves, refs[1], nb, rot, (early,))
         scores = lax.all_to_all(scores, "blk", 0, 0)
         flat = (1, particles)
         e, stats = local_softmax(

time: 64 us -> 65.2 us (1.019)
  starting transfers between devices: 9.29 us -> 12.7 us
  waiting for transfers between devices: 5.68 us -> 2.72 us
    ppermute x3 -> x6, starting transfers between devices: 5.62 us -> 9.29 us  [shards(): refs[-1].append(lax.ppermute(block, 'z', ring))]
    ppermute x3 -> x6, waiting for transfers between devices: 3.96 us -> 1.1 us  [shards(): refs[-1].append(lax.ppermute(block, 'z', ring))]
    all_to_all x1, blocking collectives: 12.7 us -> 14 us  [shards(): totals = lax.all_to_all(totals, ('yh', 'z'), 0, 0)]
  transfers between devices with their start and end apart: 7 -> 10, of which waited for: 4 -> 3; matrix products, arithmetic and copies ran while one was open for 0% -> 0% of each run, Pallas kernels for 7% -> 7%
where the time goes in v11:
time: 65.2 us; the launch traced here: 64.9 us
  blocking collectives  39.7 us (61%)
  starting transfers between devices  12.7 us (19%)
  Pallas kernels  9.65 us (15%)
  waiting for transfers between devices  2.72 us (4%)
    all_to_all x1, blocking collectives, shards(): totals = lax.all_to_all(totals, ('yh', 'z'), 0, 0)  14 us
    all_to_all x1, blocking collectives, shards(): scores = lax.all_to_all(scores, 'blk', 0, 0)  12.9 us
    all_to_all x1, blocking collectives, shards(): weights = lax.all_to_all(weights, 'blk', 0, 0)  12.8 us
    ppermute x6, starting transfers between devices, shards(): refs[-1].append(lax.ppermute(block, 'z', ring))  9.29 us
    ppermute x1, starting transfers between devices, shards(): theirs = lax.ppermute(mine, 'yh', swap)  3.39 us
    pallas_call x2, Pallas kernels, correlate(): pl.pallas_call(body, out_shape=VM((nb, 1 + len(before), 2 * rows, LANES),...  3.02 us
    pallas_call x1, Pallas kernels, accumulate(): pl.pallas_call(body, out_shape=VM((owners, classes // owners * cycles, pa...  2.41 us
    pallas_call x1, Pallas kernels, pick_block(): pl.pallas_call(body, out_shape=VM((kb * cycles, angles), BF), in_specs=[s...  1.68 us
  transfers between devices with their start and end apart: 10, of which 3 were waited for; matrix products, arithmetic and copies ran while one was open for 0% of the time, Pallas kernels for 7%

profile of v11, /device:TPU:0, one launch (start us, length us, event | category | flops | bytes accessed | tf_op | source)
XLA Modules:
  0.0 64.9 jit_solution(6857674957535594352)
XLA Ops:
  0.0 0.0 copy-start
  0.0 0.0 collective-permute-start
  0.0 0.0 copy-start.1
  0.0 1.7 %pick_block.1.args_0_ = bf16[64,256]{1,0:T(8,128)(2,1)S(1)} custom-call(s32[1]{0:T(128)} %bitcast.me_ref, s32[16]{0:T(128)} %owner_ref.1, f32[64]{0:T(128)} %gain_ref.1, bf16[16,4,16,256]{3,2,1,0:T(8,128)(2,1)} %bitcast.7), custom_call_target="tpu_custom_call" | custom-call | tf_op jit(solution)/shard_map/pick_block/pallas_call | solution.py:82
  1.7 3.4 %collective-permute-start.2 = (bf16[64,256]{1,0:T(8,128)(2,1)S(1)}, bf16[64,256]{1,0:T(8,128)(2,1)S(1)}, u32[]{:S(2)}, u32[]{:S(2)}) collective-permute-start(bf16[64,256]{1,0:T(8,128)(2,1)S(1)} %pick_block.1.args_0_), channel_id=1, source_target_pairs={{0,64},{64,0},{1,65},{65,1},{2,66},{66,2},{3,67},{67,3},{4,68},{68... | collective-permute-start | bytes 98312 | tf_op jit(solution)/shard_map/ppermute | solution.py:359
  5.1 3.9 %collective-permute-start.8 = (bf16[64,256]{1,0:T(8,128)(2,1)S(1)}, bf16[64,256]{1,0:T(8,128)(2,1)S(1)}, u32[]{:S(2)}, u32[]{:S(2)}) collective-permute-start(bf16[64,256]{1,0:T(8,128)(2,1)S(1)} %pick_block.1.args_0_), channel_id=1, source_target_pairs={{0,32},{16,48},{32,0},{48,16},{1,33},{17,49},{33,1},{49,17},{2,34}... | collective-permute-start | bytes 98312 | tf_op jit(solution)/shard_map/ppermute | solution.py:364
  9.0 0.0 copy-done.1
  9.0 0.0 collective-permute-start.1
  9.0 0.7 %collective-permute-start.7 = (bf16[64,256]{1,0:T(8,128)(2,1)S(1)}, bf16[64,256]{1,0:T(8,128)(2,1)S(1)}, u32[]{:S(2)}, u32[]{:S(2)}) collective-permute-start(bf16[64,256]{1,0:T(8,128)(2,1)S(1)} %pick_block.1.args_0_), channel_id=1, source_target_pairs={{0,48},{16,32},{32,16},{48,0},{1,49},{17,33},{33,17},{49,1},{2,50}... | collective-permute-start | bytes 98312 | tf_op jit(solution)/shard_map/ppermute | solution.py:364
  9.7 0.4 collective-permute-done.1._
  10.1 1.0 %collective-permute-start.6 = (bf16[64,256]{1,0:T(8,128)(2,1)S(1)}, bf16[64,256]{1,0:T(8,128)(2,1)S(1)}, u32[]{:S(2)}, u32[]{:S(2)}) collective-permute-start(bf16[64,256]{1,0:T(8,128)(2,1)S(1)} %pick_block.1.args_0_), channel_id=1, source_target_pairs={{0,16},{16,0},{32,48},{48,32},{1,17},{17,1},{33,49},{49,33},{2,18}... | collective-permute-start | bytes 98312 | tf_op jit(solution)/shard_map/ppermute | solution.py:364
  11.2 0.0 collective-permute-done.2.args_0_
  11.2 2.5 %collective-permute-start.5 = (bf16[64,256]{1,0:T(8,128)(2,1)S(1)}, bf16[64,256]{1,0:T(8,128)(2,1)S(1)}, u32[]{:S(2)}, u32[]{:S(2)}) collective-permute-start(bf16[64,256]{1,0:T(8,128)(2,1)S(1)} %collective-permute-done.2.args_0_), channel_id=1, source_target_pairs={{0,32},{16,48},{32,0},{48,16},{1,33},{17,49},{33,1},{49,17},{2,34}... | collective-permute-start | bytes 98312 | tf_op jit(solution)/shard_map/ppermute | solution.py:364
  13.7 0.0 collective-permute-done.8.args_3_
  13.7 1.2 %collective-permute-start.4 = (bf16[64,256]{1,0:T(8,128)(2,1)S(1)}, bf16[64,256]{1,0:T(8,128)(2,1)S(1)}, u32[]{:S(2)}, u32[]{:S(2)}) collective-permute-start(bf16[64,256]{1,0:T(8,128)(2,1)S(1)} %collective-permute-done.2.args_0_), channel_id=1, source_target_pairs={{0,48},{16,32},{32,16},{48,0},{1,49},{17,33},{33,17},{49,1},{2,50}... | collective-permute-start | bytes 98312 | tf_op jit(solution)/shard_map/ppermute | solution.py:364
  14.8 0.0 collective-permute-done.other_ref
  14.8 0.0 collective-permute-start.3
  14.8 0.0 copy-done
  14.9 1.3 %halve_images.1.x_ref = bf16[2,16,128,128]{3,2,1,0:T(8,128)(2,1)S(1)} custom-call(bf16[64,16,256]{2,1,0:T(8,128)(2,1)S(1)} %copy-done, bf16[64,16,256]{2,1,0:T(8,128)(2,1)S(1)} %collective-permute-done.other_ref, f32[64]{0:T(128)S(1)} %collective-permute-done.1._), custom_call_target="tpu_custom_call" | custom-call | tf_op jit(solution)/shard_map/halve_images/pallas_call | solution.py:109
  16.2 0.0 collective-permute-done.7.args_2_
  16.2 0.0 collective-permute-done.6.args_1_
  16.2 1.5 %correlate.2.args_4_ = bf16[8,1,128,128]{3,2,1,0:T(8,128)(2,1)S(1)} custom-call(bf16[2,16,128,128]{3,2,1,0:T(8,128)(2,1)S(1)} %halve_images.1.x_ref, bf16[64,256]{1,0:T(8,128)(2,1)S(1)} %pick_block.1.args_0_, bf16[64,256]{1,0:T(8,128)(2,1)S(1)} %collective-permute-done.6.args_1_, bf16[64,256]{1,0:T(8,128)(2,1)S(1)} %collective-permute-done.7.args_2_, ...), custom_call_target="tpu_custom_call" | custom-call | tf_op jit(solution)/shard_map/correlate/pallas_call | solution.py:171
  17.7 0.0 collective-permute-done.5.args_3_
  17.7 1.1 %collective-permute-done.4.args_2_ = bf16[64,256]{1,0:T(8,128)(2,1)S(1)} collective-permute-done((bf16[64,256]{1,0:T(8,128)(2,1)S(1)}, bf16[64,256]{1,0:T(8,128)(2,1)S(1)}, u32[]{:S(2)}, u32[]{:S(2)}) %collective-permute-start.4) | collective-permute-done | bytes 32800 | tf_op jit(solution)/shard_map/ppermute | solution.py:364
  18.8 0.0 collective-permute-done.3.args_1_
  18.8 1.5 %correlate.3 = bf16[8,2,128,128]{3,2,1,0:T(8,128)(2,1)S(1)} custom-call(bf16[2,16,128,128]{3,2,1,0:T(8,128)(2,1)S(1)} %halve_images.1.x_ref, bf16[64,256]{1,0:T(8,128)(2,1)S(1)} %collective-permute-done.2.args_0_, bf16[64,256]{1,0:T(8,128)(2,1)S(1)} %collective-permute-done.3.args_1_, bf16[64,256]{1,0:T(8,128)(2,1)S(1)} %collective-permute-done.4.args_2_, ...), custom_call_target="tpu_custom_call" | custom-call | tf_op jit(solution)/shard_map/correlate/pallas_call | solution.py:171
  20.3 12.9 %all_to_all.15.x_ref = bf16[8,2,128,128]{3,2,1,0:T(8,128)(2,1)S(1)} all-to-all(bf16[8,2,128,128]{3,2,1,0:T(8,128)(2,1)S(1)} %correlate.3), channel_id=1, replica_groups=mesh['yh'=2,'z'=4,'core'=2,'blk'=8] {'blk'}, dimensions={0} | all-to-all | bytes 1048576 | tf_op jit(solution)/shard_map/all_to_all | solution.py:368
  33.2 0.4 local_softmax.1
  33.6 0.1 collective-permute-start.9
  33.7 1.2 %collective-permute-done.9.b_ref = f32[2,16,128]{2,1,0:T(8,128)S(1)} collective-permute-done((f32[2,16,128]{2,1,0:T(8,128)S(1)}, f32[2,16,128]{2,1,0:T(8,128)S(1)}, u32[]{:S(2)}, u32[]{:S(2)}) %collective-permute-start.9) | collective-permute-done | bytes 16416 | tf_op jit(solution)/shard_map/ppermute | solution.py:373
  34.9 0.1 normalize.1
  35.0 12.8 %all_to_all.16.w_ref = bf16[8,256,128]{2,1,0:T(8,128)(2,1)S(1)} all-to-all(bf16[8,256,128]{2,1,0:T(8,128)(2,1)S(1)} %normalize.1), channel_id=1, replica_groups=mesh['yh'=2,'z'=4,'core'=2,'blk'=8] {'blk'}, dimensions={0} | all-to-all | bytes 1048576 | tf_op jit(solution)/shard_map/all_to_all | solution.py:375
  47.8 2.4 %accumulate.1 = bf16[8,64,256]{2,1,0:T(8,128)(2,1)S(1)} custom-call(s32[1]{0:T(128)} %bitcast.me_ref, bf16[8,256,128]{2,1,0:T(8,128)(2,1)S(1)} %all_to_all.16.w_ref, bf16[2,16,128,128]{3,2,1,0:T(8,128)(2,1)S(1)} %halve_images.1.x_ref), custom_call_target="tpu_custom_call" | custom-call | tf_op jit(solution)/shard_map/accumulate/pallas_call | solution.py:311
  50.2 14.0 %all_to_all.17.x_ref = bf16[8,64,256]{2,1,0:T(8,128)(2,1)S(1)} all-to-all(bf16[8,64,256]{2,1,0:T(8,128)(2,1)S(1)} %accumulate.1), channel_id=1, replica_groups=mesh['yh'=2,'z'=4,'core'=2,'blk'=8] {'yh','z'}, dimensions={0} | all-to-all | bytes 524288 | tf_op jit(solution)/shard_map/all_to_all | solution.py:377
  64.2 0.7 %add_up.1 = f32[64,256]{1,0:T(8,128)} custom-call(bf16[8,64,256]{2,1,0:T(8,128)(2,1)S(1)} %all_to_all.17.x_ref), custom_call_target="tpu_custom_call" | custom-call | tf_op jit(solution)/shard_map/add_up/pallas_call | solution.py:332
Async XLA Ops:
  0.0 14.8 %copy-start = (bf16[64,16,256]{2,1,0:T(8,128)(2,1)S(1)}, bf16[64,16,256]{2,1,0:T(8,128)(2,1)}, u32[]{:S(2)}) copy-start(bf16[64,16,256]{2,1,0:T(8,128)(2,1)} %own_ref.1) | copy-start | bytes 1572868
  0.0 14.8 %collective-permute-start = (bf16[64,16,256]{2,1,0:T(8,128)(2,1)}, bf16[64,16,256]{2,1,0:T(8,128)(2,1)S(1)}, u32[]{:S(2)}, u32[]{:S(2)}) collective-permute-start(bf16[64,16,256]{2,1,0:T(8,128)(2,1)} %own_ref.1), channel_id=1, source_target_pairs={{0,8},{8,0},{1,9},{9,1},{2,10},{10,2},{3,11},{11,3},{4,12},{12,4},... | collective-permute-start | bytes 1572872 | tf_op jit(solution)/shard_map/ppermute | solution.py:352
  0.0 9.0 %copy-start.1 = (f32[64]{0:T(128)S(1)}, f32[64]{0:T(128)}, u32[]{:S(2)}) copy-start(f32[64]{0:T(128)} %param.9) | copy-start | bytes 772
  1.7 9.5 %collective-permute-start.2 = (bf16[64,256]{1,0:T(8,128)(2,1)S(1)}, bf16[64,256]{1,0:T(8,128)(2,1)S(1)}, u32[]{:S(2)}, u32[]{:S(2)}) collective-permute-start(bf16[64,256]{1,0:T(8,128)(2,1)S(1)} %pick_block.1.args_0_), channel_id=1, source_target_pairs={{0,64},{64,0},{1,65},{65,1},{2,66},{66,2},{3,67},{67,3},{4,68},{68... | collective-permute-start | bytes 98312 | tf_op jit(solution)/shard_map/ppermute | solution.py:359
  5.1 8.6 %collective-permute-start.8 = (bf16[64,256]{1,0:T(8,128)(2,1)S(1)}, bf16[64,256]{1,0:T(8,128)(2,1)S(1)}, u32[]{:S(2)}, u32[]{:S(2)}) collective-permute-start(bf16[64,256]{1,0:T(8,128)(2,1)S(1)} %pick_block.1.args_0_), channel_id=1, source_target_pairs={{0,32},{16,48},{32,0},{48,16},{1,33},{17,49},{33,1},{49,17},{2,34}... | collective-permute-start | bytes 98312 | tf_op jit(solution)/shard_map/ppermute | solution.py:364
  9.0 1.2 %collective-permute-start.1 = (f32[64]{0:T(128)S(1)}, f32[64]{0:T(128)S(1)}, u32[]{:S(2)}, u32[]{:S(2)}) collective-permute-start(f32[64]{0:T(128)S(1)} %copy-done.1), channel_id=1, source_target_pairs={{0,8},{8,0},{1,9},{9,1},{2,10},{10,2},{3,11},{11,3},{4,12},{12,4},... | collective-permute-start | bytes 776 | tf_op jit(solution)/shard_map/ppermute | solution.py:353
  9.0 7.2 %collective-permute-start.7 = (bf16[64,256]{1,0:T(8,128)(2,1)S(1)}, bf16[64,256]{1,0:T(8,128)(2,1)S(1)}, u32[]{:S(2)}, u32[]{:S(2)}) collective-permute-start(bf16[64,256]{1,0:T(8,128)(2,1)S(1)} %pick_block.1.args_0_), channel_id=1, source_target_pairs={{0,48},{16,32},{32,16},{48,0},{1,49},{17,33},{33,17},{49,1},{2,50}... | collective-permute-start | bytes 98312 | tf_op jit(solution)/shard_map/ppermute | solution.py:364
  10.1 6.1 %collective-permute-start.6 = (bf16[64,256]{1,0:T(8,128)(2,1)S(1)}, bf16[64,256]{1,0:T(8,128)(2,1)S(1)}, u32[]{:S(2)}, u32[]{:S(2)}) collective-permute-start(bf16[64,256]{1,0:T(8,128)(2,1)S(1)} %pick_block.1.args_0_), channel_id=1, source_target_pairs={{0,16},{16,0},{32,48},{48,32},{1,17},{17,1},{33,49},{49,33},{2,18}... | collective-permute-start | bytes 98312 | tf_op jit(solution)/shard_map/ppermute | solution.py:364
  11.2 6.6 %collective-permute-start.5 = (bf16[64,256]{1,0:T(8,128)(2,1)S(1)}, bf16[64,256]{1,0:T(8,128)(2,1)S(1)}, u32[]{:S(2)}, u32[]{:S(2)}) collective-permute-start(bf16[64,256]{1,0:T(8,128)(2,1)S(1)} %collective-permute-done.2.args_0_), channel_id=1, source_target_pairs={{0,32},{16,48},{32,0},{48,16},{1,33},{17,49},{33,1},{49,17},{2,34}... | collective-permute-start | bytes 98312 | tf_op jit(solution)/shard_map/ppermute | solution.py:364
  13.7 5.1 %collective-permute-start.4 = (bf16[64,256]{1,0:T(8,128)(2,1)S(1)}, bf16[64,256]{1,0:T(8,128)(2,1)S(1)}, u32[]{:S(2)}, u32[]{:S(2)}) collective-permute-start(bf16[64,256]{1,0:T(8,128)(2,1)S(1)} %collective-permute-done.2.args_0_), channel_id=1, source_target_pairs={{0,48},{16,32},{32,16},{48,0},{1,49},{17,33},{33,17},{49,1},{2,50}... | collective-permute-start | bytes 98312 | tf_op jit(solution)/shard_map/ppermute | solution.py:364
  14.8 4.0 %collective-permute-start.3 = (bf16[64,256]{1,0:T(8,128)(2,1)S(1)}, bf16[64,256]{1,0:T(8,128)(2,1)S(1)}, u32[]{:S(2)}, u32[]{:S(2)}) collective-permute-start(bf16[64,256]{1,0:T(8,128)(2,1)S(1)} %collective-permute-done.2.args_0_), channel_id=1, source_target_pairs={{0,16},{16,0},{32,48},{48,32},{1,17},{17,1},{33,49},{49,33},{2,18}... | collective-permute-start | bytes 98312 | tf_op jit(solution)/shard_map/ppermute | solution.py:364
  33.6 1.2 %collective-permute-start.9 = (f32[2,16,128]{2,1,0:T(8,128)S(1)}, f32[2,16,128]{2,1,0:T(8,128)S(1)}, u32[]{:S(2)}, u32[]{:S(2)}) collective-permute-start(f32[2,16,128]{2,1,0:T(8,128)S(1)} %get-tuple-element.8.a_ref), channel_id=1, source_target_pairs={{0,8},{8,0},{1,9},{9,1},{2,10},{10,2},{3,11},{11,3},{4,12},{12,4},... | collective-permute-start | bytes 49160 | tf_op jit(solution)/shard_map/ppermute | solution.py:373

commit v12 on v10

--- a/solution.py
+++ b/solution.py
@@ -66,15 +66,12 @@
 def pick_block(me, nb, block_owner, class_gain, ref_store):
     nblk, kb, cycles, angles = ref_store.shape
 
-    def body(me_ref, owner_ref, gain_ref, store_ref, out_ref, buf, sem):
+    def body(me_ref, owner_ref, gain_ref, store_ref, out_ref):
         block = jnp.int32(0)
         for b in range(nblk):
             block = jnp.where(owner_ref[b] == me_ref[0] // nb, jnp.int32(b), block)
-        copy = pltpu.make_async_copy(store_ref.at[block], buf, sem)
-        copy.start()
-        copy.wait()
         for i in range(kb):
-            piece = (buf[i].astype(F32) * gain_ref[block * kb + i]).astype(BF).astype(F32)
+            piece = (store_ref[block, i].astype(F32) * gain_ref[block * kb + i]).astype(BF).astype(F32)
             a, b = piece[:, :LANES], piece[:, LANES:]
             piece = jnp.concatenate([narrow_sum(a + b), narrow(a - b)], axis=1).astype(BF)
             out_ref[i * cycles : (i + 1) * cycles, :] = piece
@@ -82,9 +79,8 @@
     return pl.pallas_call(
         body,
         out_shape=VM((kb * cycles, angles), BF),
-        in_specs=[spec(pltpu.SMEM), spec(pltpu.SMEM), spec(pltpu.SMEM), spec(pltpu.HBM)],
-        out_specs=spec(),
-        scratch_shapes=[VM((kb, cycles, angles), BF), pltpu.SemaphoreType.DMA],
+        in_specs=[spec(pltpu.SMEM), spec(pltpu.SMEM), spec(pltpu.SMEM), spec()],
+        out_specs=spec(),
         compiler_params=params(60),
         name="pick_block",
     )(me, block_owner, class_gain, away(ref_store))

time: 64 us -> 63.6 us (level)
  transfers between devices with their start and end apart: 7 -> 7, of which waited for: 4 -> 4; matrix products, arithmetic and copies ran while one was open for 0% -> 0% of each run, Pallas kernels for 7% -> 6%
where the time goes in v12:
time: 63.6 us; the launch traced here: 63.3 us
  blocking collectives  39.1 us (61%)
  starting transfers between devices  9.22 us (14%)
  Pallas kernels  9.19 us (14%)
  waiting for transfers between devices  5.74 us (9%)
    all_to_all x1, blocking collectives, shards(): scores = lax.all_to_all(scores, 'blk', 0, 0)  13.4 us
    all_to_all x1, blocking collectives, shards(): weights = lax.all_to_all(weights, 'blk', 0, 0)  12.9 us
    all_to_all x1, blocking collectives, shards(): totals = lax.all_to_all(totals, ('yh', 'z'), 0, 0)  12.7 us
    ppermute x3, starting transfers between devices, shards(): refs.append(lax.ppermute(refs[0], 'z', ring))  5.61 us
    ppermute x3, waiting for transfers between devices, shards(): refs.append(lax.ppermute(refs[0], 'z', ring))  3.96 us
    ppermute x1, starting transfers between devices, shards(): theirs = lax.ppermute(mine, 'yh', swap)  3.39 us
    pallas_call x2, Pallas kernels, correlate(): pl.pallas_call(body, out_shape=VM((nb, 1 + len(before), 2 * rows, LANES),...  3.02 us
    pallas_call x1, Pallas kernels, accumulate(): pl.pallas_call(body, out_shape=VM((owners, classes // owners * cycles, pa...  2.4 us
  transfers between devices with their start and end apart: 7, of which 4 were waited for; matrix products, arithmetic and copies ran while one was open for 0% of the time, Pallas kernels for 6%

profile of v12, /device:TPU:0, one launch (start us, length us, event | category | flops | bytes accessed | tf_op | source)
XLA Modules:
  0.0 63.3 jit_solution(7242837286504855991)
XLA Ops:
  0.0 0.0 copy-start
  0.0 0.0 collective-permute-start
  0.0 0.0 copy-start.1
  0.0 1.2 %pick_block.1.a_ref = bf16[64,256]{1,0:T(8,128)(2,1)S(1)} custom-call(s32[1]{0:T(128)} %bitcast.me_ref, s32[16]{0:T(128)} %owner_ref.1, f32[64]{0:T(128)} %gain_ref.1, bf16[16,4,16,256]{3,2,1,0:T(8,128)(2,1)} %bitcast.7), custom_call_target="tpu_custom_call" | custom-call | tf_op jit(solution)/shard_map/pick_block/pallas_call | solution.py:79
  1.2 3.4 %collective-permute-start.1 = (bf16[64,256]{1,0:T(8,128)(2,1)S(1)}, bf16[64,256]{1,0:T(8,128)(2,1)S(1)}, u32[]{:S(2)}, u32[]{:S(2)}) collective-permute-start(bf16[64,256]{1,0:T(8,128)(2,1)S(1)} %pick_block.1.a_ref), channel_id=1, source_target_pairs={{0,64},{64,0},{1,65},{65,1},{2,66},{66,2},{3,67},{67,3},{4,68},{68... | collective-permute-start | bytes 98312 | tf_op jit(solution)/shard_map/ppermute | solution.py:371
  4.6 0.0 copy-done.1
  4.6 0.2 collective-permute-start.2
  4.8 0.0 collective-permute-done.other_ref
  4.8 0.0 copy-done
  4.8 1.3 %halve_images.1.refs_0_.x_ref = bf16[2,16,128,128]{3,2,1,0:T(8,128)(2,1)S(1)} custom-call(bf16[64,16,256]{2,1,0:T(8,128)(2,1)S(1)} %copy-done, bf16[64,16,256]{2,1,0:T(8,128)(2,1)S(1)} %collective-permute-done.other_ref), custom_call_target="tpu_custom_call" | custom-call | tf_op jit(solution)/shard_map/halve_images/pallas_call | solution.py:105
  6.1 0.0 collective-permute-done.2.refs_1_
  6.1 0.6 collective-permute-done.1.b_ref
  6.8 2.0 %collective-permute-start.5 = (bf16[2,64,256]{2,1,0:T(8,128)(2,1)S(1)}, bf16[2,64,256]{2,1,0:T(8,128)(2,1)S(1)}, u32[]{:S(2)}, u32[]{:S(2)}) collective-permute-start(bf16[2,64,256]{2,1,0:T(8,128)(2,1)S(1)} %pair_up.1.args_0_), channel_id=1, source_target_pairs={{0,16},{16,0},{32,48},{48,32},{1,17},{17,1},{33,49},{49,33},{2,18}... | collective-permute-start | bytes 196616 | tf_op jit(solution)/shard_map/ppermute | solution.py:376
  8.8 3.6 %collective-permute-start.4 = (bf16[2,64,256]{2,1,0:T(8,128)(2,1)S(1)}, bf16[2,64,256]{2,1,0:T(8,128)(2,1)S(1)}, u32[]{:S(2)}, u32[]{:S(2)}) collective-permute-start(bf16[2,64,256]{2,1,0:T(8,128)(2,1)S(1)} %pair_up.1.args_0_), channel_id=1, source_target_pairs={{0,32},{16,48},{32,0},{48,16},{1,33},{17,49},{33,1},{49,17},{2,34}... | collective-permute-start | bytes 196616 | tf_op jit(solution)/shard_map/ppermute | solution.py:376
  12.4 0.0 collective-permute-start.3
  12.4 0.0 collective-permute-done.5.args_1_
  12.4 1.5 %correlate.2.args_2_ = bf16[8,1,128,128]{3,2,1,0:T(8,128)(2,1)S(1)} custom-call(bf16[2,16,128,128]{3,2,1,0:T(8,128)(2,1)S(1)} %halve_images.1.refs_0_.x_ref, bf16[2,64,256]{2,1,0:T(8,128)(2,1)S(1)} %pair_up.1.args_0_, bf16[2,64,256]{2,1,0:T(8,128)(2,1)S(1)} %collective-permute-done.5.args_1_), custom_call_target="tpu_custom_call" | custom-call | tf_op jit(solution)/shard_map/correlate/pallas_call | solution.py:184
  13.9 1.6 %collective-permute-done.4.args_1_ = bf16[2,64,256]{2,1,0:T(8,128)(2,1)S(1)} collective-permute-done((bf16[2,64,256]{2,1,0:T(8,128)(2,1)S(1)}, bf16[2,64,256]{2,1,0:T(8,128)(2,1)S(1)}, u32[]{:S(2)}, u32[]{:S(2)}) %collective-permute-start.4) | collective-permute-done | bytes 65568 | tf_op jit(solution)/shard_map/ppermute | solution.py:376
  15.5 2.4 %collective-permute-done.3.args_0_ = bf16[2,64,256]{2,1,0:T(8,128)(2,1)S(1)} collective-permute-done((bf16[2,64,256]{2,1,0:T(8,128)(2,1)S(1)}, bf16[2,64,256]{2,1,0:T(8,128)(2,1)S(1)}, u32[]{:S(2)}, u32[]{:S(2)}) %collective-permute-start.3) | collective-permute-done | bytes 65568 | tf_op jit(solution)/shard_map/ppermute | solution.py:376
  17.8 1.5 %correlate.3 = bf16[8,2,128,128]{3,2,1,0:T(8,128)(2,1)S(1)} custom-call(bf16[2,16,128,128]{3,2,1,0:T(8,128)(2,1)S(1)} %halve_images.1.refs_0_.x_ref, bf16[2,64,256]{2,1,0:T(8,128)(2,1)S(1)} %collective-permute-done.3.args_0_, bf16[2,64,256]{2,1,0:T(8,128)(2,1)S(1)} %collective-permute-done.4.args_1_, bf16[8,1,128,128]{3,2,1,0:T(8,128)(2,1)S(1)} %correlate.2.args_2_), custom_call_target="tpu_custom_call" | custom-call | tf_op jit(solution)/shard_map/correlate/pallas_call | solution.py:184
  19.4 13.4 %all_to_all.15.x_ref = bf16[8,2,128,128]{3,2,1,0:T(8,128)(2,1)S(1)} all-to-all(bf16[8,2,128,128]{3,2,1,0:T(8,128)(2,1)S(1)} %correlate.3), channel_id=1, replica_groups=mesh['yh'=2,'z'=4,'core'=2,'blk'=8] {'blk'}, dimensions={0} | all-to-all | bytes 1048576 | tf_op jit(solution)/shard_map/all_to_all | solution.py:379
  32.8 0.4 local_softmax.1
  33.2 0.1 collective-permute-start.6
  33.3 1.2 %collective-permute-done.6.b_ref = f32[2,16,128]{2,1,0:T(8,128)S(1)} collective-permute-done((f32[2,16,128]{2,1,0:T(8,128)S(1)}, f32[2,16,128]{2,1,0:T(8,128)S(1)}, u32[]{:S(2)}, u32[]{:S(2)}) %collective-permute-start.6) | collective-permute-done | bytes 16416 | tf_op jit(solution)/shard_map/ppermute | solution.py:384
  34.5 0.1 normalize.1
  34.6 12.9 %all_to_all.16.w_ref = bf16[8,256,128]{2,1,0:T(8,128)(2,1)S(1)} all-to-all(bf16[8,256,128]{2,1,0:T(8,128)(2,1)S(1)} %normalize.1), channel_id=1, replica_groups=mesh['yh'=2,'z'=4,'core'=2,'blk'=8] {'blk'}, dimensions={0} | all-to-all | bytes 1048576 | tf_op jit(solution)/shard_map/all_to_all | solution.py:386
  47.5 2.4 %accumulate.1 = bf16[8,64,256]{2,1,0:T(8,128)(2,1)S(1)} custom-call(s32[1]{0:T(128)} %bitcast.me_ref, bf16[8,256,128]{2,1,0:T(8,128)(2,1)S(1)} %all_to_all.16.w_ref, bf16[2,16,128,128]{3,2,1,0:T(8,128)(2,1)S(1)} %halve_images.1.refs_0_.x_ref), custom_call_target="tpu_custom_call" | custom-call | tf_op jit(solution)/shard_map/accumulate/pallas_call | solution.py:324
  49.9 12.7 %all_to_all.17.x_ref = bf16[8,64,256]{2,1,0:T(8,128)(2,1)S(1)} all-to-all(bf16[8,64,256]{2,1,0:T(8,128)(2,1)S(1)} %accumulate.1), channel_id=1, replica_groups=mesh['yh'=2,'z'=4,'core'=2,'blk'=8] {'yh','z'}, dimensions={0} | all-to-all | bytes 524288 | tf_op jit(solution)/shard_map/all_to_all | solution.py:388
  62.7 0.7 %add_up.1 = f32[64,256]{1,0:T(8,128)} custom-call(bf16[8,64,256]{2,1,0:T(8,128)(2,1)S(1)} %all_to_all.17.x_ref), custom_call_target="tpu_custom_call" | custom-call | tf_op jit(solution)/shard_map/add_up/pallas_call | solution.py:345
  (1 shorter events, 0.0 us)
Async XLA Ops:
  0.0 4.8 %copy-start = (bf16[64,16,256]{2,1,0:T(8,128)(2,1)S(1)}, bf16[64,16,256]{2,1,0:T(8,128)(2,1)}, u32[]{:S(2)}) copy-start(bf16[64,16,256]{2,1,0:T(8,128)(2,1)} %own_ref.1) | copy-start | bytes 1572868
  0.0 4.8 %collective-permute-start = (bf16[64,16,256]{2,1,0:T(8,128)(2,1)}, bf16[64,16,256]{2,1,0:T(8,128)(2,1)S(1)}, u32[]{:S(2)}, u32[]{:S(2)}) collective-permute-start(bf16[64,16,256]{2,1,0:T(8,128)(2,1)} %own_ref.1), channel_id=1, source_target_pairs={{0,8},{8,0},{1,9},{9,1},{2,10},{10,2},{3,11},{11,3},{4,12},{12,4},... | collective-permute-start | bytes 1572872 | tf_op jit(solution)/shard_map/ppermute | solution.py:365
  0.0 4.6 %copy-start.1 = (f32[64]{0:T(128)S(1)}, f32[64]{0:T(128)}, u32[]{:S(2)}) copy-start(f32[64]{0:T(128)} %param.9) | copy-start | bytes 772
  1.2 5.5 %collective-permute-start.1 = (bf16[64,256]{1,0:T(8,128)(2,1)S(1)}, bf16[64,256]{1,0:T(8,128)(2,1)S(1)}, u32[]{:S(2)}, u32[]{:S(2)}) collective-permute-start(bf16[64,256]{1,0:T(8,128)(2,1)S(1)} %pick_block.1.a_ref), channel_id=1, source_target_pairs={{0,64},{64,0},{1,65},{65,1},{2,66},{66,2},{3,67},{67,3},{4,68},{68... | collective-permute-start | bytes 98312 | tf_op jit(solution)/shard_map/ppermute | solution.py:371
  4.6 1.5 %collective-permute-start.2 = (f32[64]{0:T(128)S(1)}, f32[64]{0:T(128)S(1)}, u32[]{:S(2)}, u32[]{:S(2)}) collective-permute-start(f32[64]{0:T(128)S(1)} %copy-done.1), channel_id=1, source_target_pairs={{0,8},{8,0},{1,9},{9,1},{2,10},{10,2},{3,11},{11,3},{4,12},{12,4},... | collective-permute-start | bytes 776 | tf_op jit(solution)/shard_map/ppermute | solution.py:366
  6.8 5.6 %collective-permute-start.5 = (bf16[2,64,256]{2,1,0:T(8,128)(2,1)S(1)}, bf16[2,64,256]{2,1,0:T(8,128)(2,1)S(1)}, u32[]{:S(2)}, u32[]{:S(2)}) collective-permute-start(bf16[2,64,256]{2,1,0:T(8,128)(2,1)S(1)} %pair_up.1.args_0_), channel_id=1, source_target_pairs={{0,16},{16,0},{32,48},{48,32},{1,17},{17,1},{33,49},{49,33},{2,18}... | collective-permute-start | bytes 196616 | tf_op jit(solution)/shard_map/ppermute | solution.py:376
  8.8 6.7 %collective-permute-start.4 = (bf16[2,64,256]{2,1,0:T(8,128)(2,1)S(1)}, bf16[2,64,256]{2,1,0:T(8,128)(2,1)S(1)}, u32[]{:S(2)}, u32[]{:S(2)}) collective-permute-start(bf16[2,64,256]{2,1,0:T(8,128)(2,1)S(1)} %pair_up.1.args_0_), channel_id=1, source_target_pairs={{0,32},{16,48},{32,0},{48,16},{1,33},{17,49},{33,1},{49,17},{2,34}... | collective-permute-start | bytes 196616 | tf_op jit(solution)/shard_map/ppermute | solution.py:376
  12.4 5.5 %collective-permute-start.3 = (bf16[2,64,256]{2,1,0:T(8,128)(2,1)S(1)}, bf16[2,64,256]{2,1,0:T(8,128)(2,1)S(1)}, u32[]{:S(2)}, u32[]{:S(2)}) collective-permute-start(bf16[2,64,256]{2,1,0:T(8,128)(2,1)S(1)} %pair_up.1.args_0_), channel_id=1, source_target_pairs={{0,48},{16,32},{32,16},{48,0},{1,49},{17,33},{33,17},{49,1},{2,50}... | collective-permute-start | bytes 196616 | tf_op jit(solution)/shard_map/ppermute | solution.py:376
  33.2 1.2 %collective-permute-start.6 = (f32[2,16,128]{2,1,0:T(8,128)S(1)}, f32[2,16,128]{2,1,0:T(8,128)S(1)}, u32[]{:S(2)}, u32[]{:S(2)}) collective-permute-start(f32[2,16,128]{2,1,0:T(8,128)S(1)} %get-tuple-element.8.a_ref), channel_id=1, source_target_pairs={{0,8},{8,0},{1,9},{9,1},{2,10},{10,2},{3,11},{11,3},{4,12},{12,4},... | collective-permute-start | bytes 49160 | tf_op jit(solution)/shard_map/ppermute | solution.py:384

commit v13 on v12

--- a/solution.py
+++ b/solution.py
@@ -141,18 +141,35 @@
     ]
 
 
-def correlate(images, refs, nb, step, before=()):
+def turn_images(images, nb, step):
     _, cycles, particles, _ = images.shape
-    total = N1 * particles
+
+    def body(x_ref, out_ref):
+        for r in range(cycles):
+            out_ref[0, r], out_ref[1, r] = rotate_images(x_ref, r, nb, step)
+
+    return pl.pallas_call(
+        body,
+        out_shape=VM((2, cycles, N1 * particles, LANES), BF),
+        in_specs=[spec()],
+        out_specs=spec(),
+        compiler_params=params(),
+        name="turn_images",
+    )(here(images))
+
+
+def correlate(turned, refs, nb, step, before=()):
+    _, cycles, total, _ = turned.shape
     rows = total // nb
     near, far = refs[0].shape[:2]
     classes = len(refs) * near * far // cycles
     cols = N2 * classes
     angles = 2 * LANES
+    tiles = 1 + len(before)
 
     def body(x_ref, *args):
-        r_refs, (out_ref, scr, rr, x) = args[: len(refs)], args[-4:]
-        for t, b_ref in enumerate(args[len(refs) : -4]):
+        r_refs, (out_ref, scr, rr) = args[: len(refs)], args[-3:]
+        for t, b_ref in enumerate(args[len(refs) : -3]):
             out_ref[:, t] = b_ref[:, 0]
         blocks = [r_ref[d].astype(F32) for r_ref in r_refs for d in range(near)]
         fill(scr, jnp.concatenate(blocks, axis=0))
@@ -161,7 +178,6 @@
             plus, minus = take_cycle(scr, r, classes, cycles)
             square = square + 0.5 * (plus * plus + minus * minus)
             plus, minus = plus.astype(BF), minus.astype(BF)
-            x[0, r], x[1, r] = rotate_images(x_ref, r, nb, step)
             for s in range(N2):
                 p, m = turn(plus, minus, angles - step * N1 * s)
                 rr[0, r, s * classes : (s + 1) * classes, :] = p
@@ -171,7 +187,7 @@
         lane = lax.broadcasted_iota(jnp.int32, (classes, cols), 1)
         norm = jnp.sum(jnp.where(lane % classes == k, norm, 0.0), axis=0, keepdims=True)
         for i in range(2):
-            left = jnp.concatenate([x[i, r] for r in range(cycles)], axis=1)
+            left = jnp.concatenate([x_ref[i, r] for r in range(cycles)], axis=1)
             right = jnp.concatenate([rr[i, r] for r in range(cycles)], axis=1)
             part = lax.dot_general(
                 left, right, (((1,), (1,)), ((), ())), preferred_element_type=F32
@@ -179,21 +195,20 @@
             if i == 0:
                 part = part - norm
             at = slice(i * rows, (i + 1) * rows)
-            out_ref[:, len(before), at, :] = part.astype(BF).reshape(nb, rows, LANES)
-
-    return pl.pallas_call(
-        body,
-        out_shape=VM((nb, 1 + len(before), 2 * rows, LANES), BF),
-        in_specs=[spec()] * (1 + len(refs) + len(before)),
+            out_ref[:, tiles - 1, at, :] = part.astype(BF).reshape(nb, rows, LANES)
+
+    return pl.pallas_call(
+        body,
+        out_shape=VM((nb, tiles, 2 * rows, LANES), BF),
+        in_specs=[spec()] * (len(refs) + tiles),
         out_specs=spec(),
         scratch_shapes=[
             VM((2, classes * cycles, LANES), F32),
             VM((2, cycles, cols, LANES), BF),
-            VM((2, cycles, total, LANES), BF),
         ],
         compiler_params=params(),
         name="correlate",
-    )(here(images), *[here(r) for r in (*refs, *before)])
+    )(here(turned), *[here(r) for r in (*refs, *before)])
 
 
 def local_softmax(me, scores, precision, others):
@@ -271,17 +286,15 @@
     )(here(e), here(mine), here(theirs))
 
 
-def accumulate(me, weights, images, ny, nz, step):
+def accumulate(me, weights, turned, ny, nz, step):
     owners = ny * nz
     nb, cols, lanes = weights.shape
-    cycles = images.shape[1]
+    cycles = turned.shape[1]
     classes = cols // N2
     per = LANES // N2
     pair = 2 * LANES
 
-    def body(me_ref, w_ref, x_ref, out_ref, scr, x):
-        for r in range(cycles):
-            x[0, r], x[1, r] = rotate_images(x_ref, r, nb, step)
+    def body(me_ref, w_ref, x_ref, out_ref, scr):
         left = lax.broadcasted_iota(jnp.int32, (cols, lanes), 1) < lanes // 2
         near, far = [], []
         for j in range(0, nb, 2):
@@ -292,7 +305,7 @@
         for c in range(0, cycles, 2):
             spread = []
             for i in range(2):
-                both = jnp.concatenate([x[i, c], x[i, c + 1]], axis=1)
+                both = jnp.concatenate([x_ref[i, c], x_ref[i, c + 1]], axis=1)
                 spread.append(jnp.dot(w[i], both, preferred_element_type=F32))
             for d in range(2):
                 plus = minus = None
@@ -328,11 +341,10 @@
         out_specs=spec(),
         scratch_shapes=[
             VM((2, classes * cycles, LANES), F32),
-            VM((2, cycles, N1 * images.shape[2], LANES), BF),
         ],
         compiler_params=params(),
         name="accumulate",
-    )(me, here(weights), here(images))
+    )(me, here(weights), here(turned))
 
 
 def add_up(parts):
@@ -374,8 +386,9 @@
         for d in PARTNERS[1:]:
             ring = [(i, i ^ d) for i in range(nz)]
             refs.append(lax.ppermute(refs[0], "z", ring))
-        early = correlate(halves, refs[:2], nb, rot)
-        scores = correlate(halves, refs[2:], nb, rot, (early,))
+        turned = turn_images(halves, nb, rot)
+        early = correlate(turned, refs[:2], nb, rot)
+        scores = correlate(turned, refs[2:], nb, rot, (early,))
         scores = lax.all_to_all(scores, "blk", 0, 0)
         flat = (1, particles)
         e, stats = local_softmax(
@@ -384,7 +397,7 @@
         theirs = lax.ppermute(stats, "core", swap)
         weights = normalize(e, stats, theirs, nb)
         weights = lax.all_to_all(weights, "blk", 0, 0)
-        totals = accumulate(me, weights, halves, ny, nz, rot)
+        totals = accumulate(me, weights, turned, ny, nz, rot)
         totals = lax.all_to_all(totals, ("yh", "z"), 0, 0)
         return add_up(totals).reshape(1, 1, kb, cycles, angles)
 

time: 63.6 us -> 62.4 us (0.981)
  waiting for transfers between devices: 5.74 us -> 3.56 us
  local copies, waits for them, and re-layouts: 0.01 us -> 1.05 us
    ppermute x3, waiting for transfers between devices: 3.96 us -> 2.38 us  [shards(): refs.append(lax.ppermute(refs[0], 'z', ring))]
    unnamed x4, local copies, waits for them, and re-layouts: 0.01 us -> 1.05 us
    pallas_call x1, Pallas kernels: 2.4 us -> 1.65 us  [accumulate(): pl.pallas_call(body, out_shape=VM((owners, classes // owners * cycles, pa...]
    pallas_call x2 -> x3, Pallas kernels: 3.02 us -> 3.69 us  [the longest x2 2.81 us: correlate(): pl.pallas_call(body, out_shape=VM((nb, tiles, 2 * rows, LANES), BF), in_s...]
  transfers between devices with their start and end apart: 7 -> 7, of which waited for: 4 -> 2; matrix products, arithmetic and copies ran while one was open for 0% -> 0% of each run, Pallas kernels for 6% -> 8%
where the time goes in v13:
time: 62.4 us; the launch traced here: 62.1 us
  blocking collectives  39.1 us (63%)
  starting transfers between devices  9.25 us (15%)
  Pallas kernels  9.04 us (14%)
  waiting for transfers between devices  3.56 us (6%)
  local copies, waits for them, and re-layouts  1.05 us (2%)
    all_to_all x1, blocking collectives, shards(): totals = lax.all_to_all(totals, ('yh', 'z'), 0, 0)  13.2 us
    all_to_all x1, blocking collectives, shards(): scores = lax.all_to_all(scores, 'blk', 0, 0)  13 us
    all_to_all x1, blocking collectives, shards(): weights = lax.all_to_all(weights, 'blk', 0, 0)  12.9 us
    ppermute x3, starting transfers between devices, shards(): refs.append(lax.ppermute(refs[0], 'z', ring))  5.58 us
    ppermute x1, starting transfers between devices, shards(): theirs = lax.ppermute(mine, 'yh', swap)  3.39 us
    pallas_call x2, Pallas kernels, correlate(): pl.pallas_call(body, out_shape=VM((nb, tiles, 2 * rows, LANES), BF), in_s...  2.81 us
    ppermute x3, waiting for transfers between devices, shards(): refs.append(lax.ppermute(refs[0], 'z', ring))  2.38 us
    pallas_call x1, Pallas kernels, accumulate(): pl.pallas_call(body, out_shape=VM((owners, classes // owners * cycles, pa...  1.65 us
  transfers between devices with their start and end apart: 7, of which 2 were waited for; matrix products, arithmetic and copies ran while one was open for 0% of the time, Pallas kernels for 8%

profile of v13, /device:TPU:0, one launch (start us, length us, event | category | flops | bytes accessed | tf_op | source)
XLA Modules:
  0.0 62.1 jit_solution(10699749528917111989)
XLA Ops:
  0.0 0.0 collective-permute-start
  0.0 1.2 %pick_block.1.a_ref = bf16[64,256]{1,0:T(8,128)(2,1)S(1)} custom-call(s32[1]{0:T(128)} %bitcast.me_ref, s32[16]{0:T(128)} %owner_ref.1, f32[64]{0:T(128)} %gain_ref.1, bf16[16,4,16,256]{3,2,1,0:T(8,128)(2,1)} %bitcast.7), custom_call_target="tpu_custom_call" | custom-call | tf_op jit(solution)/shard_map/pick_block/pallas_call | solution.py:79
  1.2 3.4 %collective-permute-start.1 = (bf16[64,256]{1,0:T(8,128)(2,1)S(1)}, bf16[64,256]{1,0:T(8,128)(2,1)S(1)}, u32[]{:S(2)}, u32[]{:S(2)}) collective-permute-start(bf16[64,256]{1,0:T(8,128)(2,1)S(1)} %pick_block.1.a_ref), channel_id=1, source_target_pairs={{0,64},{64,0},{1,65},{65,1},{2,66},{66,2},{3,67},{67,3},{4,68},{68... | collective-permute-start | bytes 98312 | tf_op jit(solution)/shard_map/ppermute | solution.py:383
  4.6 0.2 collective-permute-start.2
  4.8 0.0 collective-permute-done.other_ref
  4.8 0.0 copy-start
  4.8 1.0 %copy-done = bf16[64,16,256]{2,1,0:T(8,128)(2,1)S(1)} copy-done((bf16[64,16,256]{2,1,0:T(8,128)(2,1)S(1)}, bf16[64,16,256]{2,1,0:T(8,128)(2,1)}, u32[]{:S(2)}) %copy-start) | copy-done | bytes 524312
  5.8 1.3 %halve_images.1.x_ref.refs_0_ = bf16[2,16,128,128]{3,2,1,0:T(8,128)(2,1)S(1)} custom-call(bf16[64,16,256]{2,1,0:T(8,128)(2,1)S(1)} %copy-done, bf16[64,16,256]{2,1,0:T(8,128)(2,1)S(1)} %collective-permute-done.other_ref), custom_call_target="tpu_custom_call" | custom-call | tf_op jit(solution)/shard_map/halve_images/pallas_call | solution.py:105
  7.2 0.0 collective-permute-done.2.refs_1_
  7.2 0.0 collective-permute-done.1.b_ref
  7.2 2.0 %collective-permute-start.5 = (bf16[2,64,256]{2,1,0:T(8,128)(2,1)S(1)}, bf16[2,64,256]{2,1,0:T(8,128)(2,1)S(1)}, u32[]{:S(2)}, u32[]{:S(2)}) collective-permute-start(bf16[2,64,256]{2,1,0:T(8,128)(2,1)S(1)} %pair_up.1.args_0_), channel_id=1, source_target_pairs={{0,16},{16,0},{32,48},{48,32},{1,17},{17,1},{33,49},{49,33},{2,18}... | collective-permute-start | bytes 196616 | tf_op jit(solution)/shard_map/ppermute | solution.py:388
  9.2 2.5 %collective-permute-start.3 = (bf16[2,64,256]{2,1,0:T(8,128)(2,1)S(1)}, bf16[2,64,256]{2,1,0:T(8,128)(2,1)S(1)}, u32[]{:S(2)}, u32[]{:S(2)}) collective-permute-start(bf16[2,64,256]{2,1,0:T(8,128)(2,1)S(1)} %pair_up.1.args_0_), channel_id=1, source_target_pairs={{0,48},{16,32},{32,16},{48,0},{1,49},{17,33},{33,17},{49,1},{2,50}... | collective-permute-start | bytes 196616 | tf_op jit(solution)/shard_map/ppermute | solution.py:388
  11.7 1.1 %collective-permute-start.4 = (bf16[2,64,256]{2,1,0:T(8,128)(2,1)S(1)}, bf16[2,64,256]{2,1,0:T(8,128)(2,1)S(1)}, u32[]{:S(2)}, u32[]{:S(2)}) collective-permute-start(bf16[2,64,256]{2,1,0:T(8,128)(2,1)S(1)} %pair_up.1.args_0_), channel_id=1, source_target_pairs={{0,32},{16,48},{32,0},{48,16},{1,33},{17,49},{33,1},{49,17},{2,34}... | collective-permute-start | bytes 196616 | tf_op jit(solution)/shard_map/ppermute | solution.py:388
  12.8 0.9 %turn_images.1.x_ref = bf16[2,16,512,128]{3,2,1,0:T(8,128)(2,1)S(1)} custom-call(bf16[2,16,128,128]{3,2,1,0:T(8,128)(2,1)S(1)} %halve_images.1.x_ref.refs_0_), custom_call_target="tpu_custom_call" | custom-call | tf_op jit(solution)/shard_map/turn_images/pallas_call | solution.py:151
  13.7 0.0 collective-permute-done.5.args_1_
  13.7 1.4 %correlate.2.args_2_ = bf16[8,1,128,128]{3,2,1,0:T(8,128)(2,1)S(1)} custom-call(bf16[2,16,512,128]{3,2,1,0:T(8,128)(2,1)S(1)} %turn_images.1.x_ref, bf16[2,64,256]{2,1,0:T(8,128)(2,1)S(1)} %pair_up.1.args_0_, bf16[2,64,256]{2,1,0:T(8,128)(2,1)S(1)} %collective-permute-done.5.args_1_), custom_call_target="tpu_custom_call" | custom-call | tf_op jit(solution)/shard_map/correlate/pallas_call | solution.py:200
  15.1 0.0 copy-start.1
  15.1 0.0 collective-permute-done.3.args_0_
  15.1 2.4 %collective-permute-done.4.args_1_ = bf16[2,64,256]{2,1,0:T(8,128)(2,1)S(1)} collective-permute-done((bf16[2,64,256]{2,1,0:T(8,128)(2,1)S(1)}, bf16[2,64,256]{2,1,0:T(8,128)(2,1)S(1)}, u32[]{:S(2)}, u32[]{:S(2)}) %collective-permute-start.4) | collective-permute-done | bytes 65568 | tf_op jit(solution)/shard_map/ppermute | solution.py:388
  17.5 1.4 %correlate.3 = bf16[8,2,128,128]{3,2,1,0:T(8,128)(2,1)S(1)} custom-call(bf16[2,16,512,128]{3,2,1,0:T(8,128)(2,1)S(1)} %turn_images.1.x_ref, bf16[2,64,256]{2,1,0:T(8,128)(2,1)S(1)} %collective-permute-done.3.args_0_, bf16[2,64,256]{2,1,0:T(8,128)(2,1)S(1)} %collective-permute-done.4.args_1_, bf16[8,1,128,128]{3,2,1,0:T(8,128)(2,1)S(1)} %correlate.2.args_2_), custom_call_target="tpu_custom_call" | custom-call | tf_op jit(solution)/shard_map/correlate/pallas_call | solution.py:200
  18.9 13.0 %all_to_all.15.x_ref = bf16[8,2,128,128]{3,2,1,0:T(8,128)(2,1)S(1)} all-to-all(bf16[8,2,128,128]{3,2,1,0:T(8,128)(2,1)S(1)} %correlate.3), channel_id=1, replica_groups=mesh['yh'=2,'z'=4,'core'=2,'blk'=8] {'blk'}, dimensions={0} | all-to-all | bytes 1048576 | tf_op jit(solution)/shard_map/all_to_all | solution.py:392
  31.9 0.0 copy-done.1
  31.9 0.4 local_softmax.1
  32.3 0.1 collective-permute-start.6
  32.3 1.2 %collective-permute-done.6.b_ref = f32[2,16,128]{2,1,0:T(8,128)S(1)} collective-permute-done((f32[2,16,128]{2,1,0:T(8,128)S(1)}, f32[2,16,128]{2,1,0:T(8,128)S(1)}, u32[]{:S(2)}, u32[]{:S(2)}) %collective-permute-start.6) | collective-permute-done | bytes 16416 | tf_op jit(solution)/shard_map/ppermute | solution.py:397
  33.5 0.1 normalize.1
  33.7 12.9 %all_to_all.16.w_ref = bf16[8,256,128]{2,1,0:T(8,128)(2,1)S(1)} all-to-all(bf16[8,256,128]{2,1,0:T(8,128)(2,1)S(1)} %normalize.1), channel_id=1, replica_groups=mesh['yh'=2,'z'=4,'core'=2,'blk'=8] {'blk'}, dimensions={0} | all-to-all | bytes 1048576 | tf_op jit(solution)/shard_map/all_to_all | solution.py:399
  46.6 1.6 %accumulate.1 = bf16[8,64,256]{2,1,0:T(8,128)(2,1)S(1)} custom-call(s32[1]{0:T(128)} %bitcast.me_ref, bf16[8,256,128]{2,1,0:T(8,128)(2,1)S(1)} %all_to_all.16.w_ref, bf16[2,16,512,128]{3,2,1,0:T(8,128)(2,1)S(1)} %turn_images.1.x_ref), custom_call_target="tpu_custom_call" | custom-call | tf_op jit(solution)/shard_map/accumulate/pallas_call | solution.py:337
  48.3 13.2 %all_to_all.17.x_ref = bf16[8,64,256]{2,1,0:T(8,128)(2,1)S(1)} all-to-all(bf16[8,64,256]{2,1,0:T(8,128)(2,1)S(1)} %accumulate.1), channel_id=1, replica_groups=mesh['yh'=2,'z'=4,'core'=2,'blk'=8] {'yh','z'}, dimensions={0} | all-to-all | bytes 524288 | tf_op jit(solution)/shard_map/all_to_all | solution.py:401
  61.5 0.7 %add_up.1 = f32[64,256]{1,0:T(8,128)} custom-call(bf16[8,64,256]{2,1,0:T(8,128)(2,1)S(1)} %all_to_all.17.x_ref), custom_call_target="tpu_custom_call" | custom-call | tf_op jit(solution)/shard_map/add_up/pallas_call | solution.py:357
  (1 shorter events, 0.0 us)
Async XLA Ops:
  0.0 4.8 %collective-permute-start = (bf16[64,16,256]{2,1,0:T(8,128)(2,1)}, bf16[64,16,256]{2,1,0:T(8,128)(2,1)S(1)}, u32[]{:S(2)}, u32[]{:S(2)}) collective-permute-start(bf16[64,16,256]{2,1,0:T(8,128)(2,1)} %own_ref.1), channel_id=1, source_target_pairs={{0,8},{8,0},{1,9},{9,1},{2,10},{10,2},{3,11},{11,3},{4,12},{12,4},... | collective-permute-start | bytes 1572872 | tf_op jit(solution)/shard_map/ppermute | solution.py:377
  1.2 6.0 %collective-permute-start.1 = (bf16[64,256]{1,0:T(8,128)(2,1)S(1)}, bf16[64,256]{1,0:T(8,128)(2,1)S(1)}, u32[]{:S(2)}, u32[]{:S(2)}) collective-permute-start(bf16[64,256]{1,0:T(8,128)(2,1)S(1)} %pick_block.1.a_ref), channel_id=1, source_target_pairs={{0,64},{64,0},{1,65},{65,1},{2,66},{66,2},{3,67},{67,3},{4,68},{68... | collective-permute-start | bytes 98312 | tf_op jit(solution)/shard_map/ppermute | solution.py:383
  4.6 2.6 %collective-permute-start.2 = (f32[64]{0:T(128)}, f32[64]{0:T(128)S(1)}, u32[]{:S(2)}, u32[]{:S(2)}) collective-permute-start(f32[64]{0:T(128)} %param.9), channel_id=1, source_target_pairs={{0,8},{8,0},{1,9},{9,1},{2,10},{10,2},{3,11},{11,3},{4,12},{12,4},... | collective-permute-start | bytes 776 | tf_op jit(solution)/shard_map/ppermute | solution.py:378
  4.8 1.0 %copy-start = (bf16[64,16,256]{2,1,0:T(8,128)(2,1)S(1)}, bf16[64,16,256]{2,1,0:T(8,128)(2,1)}, u32[]{:S(2)}) copy-start(bf16[64,16,256]{2,1,0:T(8,128)(2,1)} %own_ref.1) | copy-start | bytes 1572868
  7.2 6.5 %collective-permute-start.5 = (bf16[2,64,256]{2,1,0:T(8,128)(2,1)S(1)}, bf16[2,64,256]{2,1,0:T(8,128)(2,1)S(1)}, u32[]{:S(2)}, u32[]{:S(2)}) collective-permute-start(bf16[2,64,256]{2,1,0:T(8,128)(2,1)S(1)} %pair_up.1.args_0_), channel_id=1, source_target_pairs={{0,16},{16,0},{32,48},{48,32},{1,17},{17,1},{33,49},{49,33},{2,18}... | collective-permute-start | bytes 196616 | tf_op jit(solution)/shard_map/ppermute | solution.py:388
  9.2 5.9 %collective-permute-start.3 = (bf16[2,64,256]{2,1,0:T(8,128)(2,1)S(1)}, bf16[2,64,256]{2,1,0:T(8,128)(2,1)S(1)}, u32[]{:S(2)}, u32[]{:S(2)}) collective-permute-start(bf16[2,64,256]{2,1,0:T(8,128)(2,1)S(1)} %pair_up.1.args_0_), channel_id=1, source_target_pairs={{0,48},{16,32},{32,16},{48,0},{1,49},{17,33},{33,17},{49,1},{2,50}... | collective-permute-start | bytes 196616 | tf_op jit(solution)/shard_map/ppermute | solution.py:388
  11.7 5.8 %collective-permute-start.4 = (bf16[2,64,256]{2,1,0:T(8,128)(2,1)S(1)}, bf16[2,64,256]{2,1,0:T(8,128)(2,1)S(1)}, u32[]{:S(2)}, u32[]{:S(2)}) collective-permute-start(bf16[2,64,256]{2,1,0:T(8,128)(2,1)S(1)} %pair_up.1.args_0_), channel_id=1, source_target_pairs={{0,32},{16,48},{32,0},{48,16},{1,33},{17,49},{33,1},{49,17},{2,34}... | collective-permute-start | bytes 196616 | tf_op jit(solution)/shard_map/ppermute | solution.py:388
  15.1 16.8 %copy-start.1 = (f32[64]{0:T(128)S(1)}, f32[64]{0:T(128)}, u32[]{:S(2)}) copy-start(f32[64]{0:T(128)} %param.9) | copy-start | bytes 772
  32.3 1.2 %collective-permute-start.6 = (f32[2,16,128]{2,1,0:T(8,128)S(1)}, f32[2,16,128]{2,1,0:T(8,128)S(1)}, u32[]{:S(2)}, u32[]{:S(2)}) collective-permute-start(f32[2,16,128]{2,1,0:T(8,128)S(1)} %get-tuple-element.8.a_ref), channel_id=1, source_target_pairs={{0,8},{8,0},{1,9},{9,1},{2,10},{10,2},{3,11},{11,3},{4,12},{12,4},... | collective-permute-start | bytes 49160 | tf_op jit(solution)/shard_map/ppermute | solution.py:397
